TPU v7x, 256 devices: a whole 4x4x8 slice. The times are simulated.
256 devices in a mesh: row: 32 (over z_hi, x, core), col: 8 (over z_lo, y).
Axes of the slice: x: 4, y: 4, z: 8 (z_hi: 4, z_lo: 2; z = z_hi * 2 + z_lo), core: 2. Of those that a mesh axis runs over, the one named last changes fastest.
Arguments:
- blocks: bfloat16 [32, 512, 128, 128], P('row', 'col')
- block_rows: int32 [32, 512], P('row', 'col'), may hold values from 0 to 255, as said below
- block_cols: int32 [32, 512], P('row', 'col'), may hold values from 0 to 255, as said below
- counts: int32 [32, 8], P('row', 'col'), may hold values from 1 to 64, as said below
- trials: bfloat16 [32768, 256], P(('col', 'row')), may hold values from -6 to 6
Outputs:
- basis: float32 [32768, 256], P(('col', 'row'))
- factor: float32 [256, 256], replicated
Inputs may be any that keep to these rules, and one draw needn't show every extreme that they name: The live slots of a device are its first counts[r, c] slots, and at least one device has all 64 slots live. `block_rows`: for the device at grid position (r, c), every slot's block row leaves remainder r on division by the size of axis row. The live slots of a device name distinct blocks with block row at most block column; slots past the count hold arbitrary blocks whose coordinates have the same form. `block_cols`: for the device at grid position (r, c), every slot's block column divided by the size of axis row gives c.
All inputs are finite; a program needn't handle non-finite values.
Results may differ from a plain program's by a relative error of at most 0.0003.
Values may be sent and summed in bfloat16 or wider, within the bound.
No kernel may reach another device: no remote copies, remote signals or barrier semaphores. Data moves between devices by JAX's collectives and lax.ppermute only.
A program may use at most 64 MiB of HBM per device.

v0:
```python
import jax
import jax.numpy as jnp
from jax import lax
from jax.experimental import pallas as pl
from jax.experimental.pallas import tpu as pltpu
from jax.sharding import PartitionSpec as P


N_ZH, N_X, N_CORE, N_ZL, N_Y = 4, 4, 2, 2, 4
N_ROW = N_ZH * N_X * N_CORE
N_COL = N_ZL * N_Y
F32 = jnp.float32
BLOCK, STEP, SUB, LANES = 64, 4, 8, 128


def row_at(z, x, c):
    return ((z % N_ZH) * N_X + x % N_X) * N_CORE + c


def col_at(zl, y):
    return zl * N_Y + y % N_Y


def row_pairs(move):
    return [(row_at(z, x, c), row_at(*move(z, x, c))) for z in range(N_ZH) for x in range(N_X) for c in range(N_CORE)]


def to_z(v, k):
    return lax.ppermute(v, "row", row_pairs(lambda z, x, c: (z + k, x, c)))


def to_x(v, k):
    return lax.ppermute(v, "row", row_pairs(lambda z, x, c: (z, x + k, c)))


def to_core(v):
    return lax.ppermute(v, "row", row_pairs(lambda z, x, c: (z, x, 1 - c)))


def to_y(v, k):
    return lax.ppermute(v, "col", [(col_at(zl, y), col_at(zl, y + k)) for zl in range(N_ZL) for y in range(N_Y)])


def to_zl(v):
    return lax.ppermute(v, "col", [(col_at(zl, y), col_at(1 - zl, y)) for zl in range(N_ZL) for y in range(N_Y)])


def ring_sum(parts):
    return (parts[0] + parts[2]) + (parts[1] + parts[3])


def slot_loop(counts, rows, cols, blocks, add):
    live = counts[0, 0]

    def visit(s):
        i, j = rows[0, s], cols[0, s]
        q = jnp.where(s < live, jnp.where(i == j, 0.5, 1.0), 0.0)
        tile = jnp.where(q > 0.0, blocks[s].astype(F32) * q, 0.0).astype(jnp.bfloat16)
        add(tile, i >> 5, j & (N_ROW - 1))

    def group(g, carry):
        for u in range(4):
            visit(g * 4 + u)
        return carry

    lax.fori_loop(0, (live + 3) // 4, group, 0)


def row_spot(place, rp):
    return ((rp - place[1]) & 3) * N_ZL + ((rp >> 2) ^ (place[1] >> 2))


def col_spot(place, cp):
    r = place[0]
    zk, xk, cx = ((cp >> 3) - (r >> 3)) & 3, ((cp >> 1) - (r >> 1)) & 3, (cp ^ r) & 1
    return (cx * N_X + xk) * N_ZH + zk


def mirror_kernel(place, counts, rows, cols, blocks, *refs):
    pieces, outs, vectors, acc = refs[:N_Y], refs[N_Y : N_Y + N_CORE], refs[-2], refs[-1]
    acc[...] = jnp.zeros_like(acc)
    for k, piece in enumerate(pieces):
        vectors[k * N_ZL : (k + 1) * N_ZL] = piece[...]

    def add(tile, rp, cp):
        acc[col_spot(place, cp)] += lax.dot_general(
            tile, vectors[row_spot(place, rp)], (((0,), (0,)), ((), ())), preferred_element_type=F32
        )

    slot_loop(counts, rows, cols, blocks, add)
    for k, out in enumerate(outs):
        out[...] = acc[k * N_X * N_ZH : (k + 1) * N_X * N_ZH]


def direct_kernel(place, counts, rows, cols, blocks, *refs):
    n = N_CORE * N_X
    pieces, outs, vectors, acc = refs[:n], refs[n : n + N_Y], refs[-2], refs[-1]
    acc[...] = jnp.zeros_like(acc)
    for k, piece in enumerate(pieces):
        vectors[k * N_ZH : (k + 1) * N_ZH] = piece[...]

    def add(tile, rp, cp):
        acc[row_spot(place, rp)] += jnp.dot(tile, vectors[col_spot(place, cp)], preferred_element_type=F32)

    slot_loop(counts, rows, cols, blocks, add)
    for k, out in enumerate(outs):
        out[...] = acc[k * N_ZL : (k + 1) * N_ZL]


def products_of(kernel, scalars, blocks, pieces, n_out, out_blocks):
    edge, width = pieces[0].shape[1:]
    smem = pl.BlockSpec(memory_space=pltpu.SMEM)
    vmem = pl.BlockSpec(memory_space=pltpu.VMEM)
    n_in = len(pieces) * pieces[0].shape[0]
    return pl.pallas_call(
        kernel,
        out_shape=(jax.ShapeDtypeStruct((out_blocks, edge, width), F32),) * n_out,
        in_specs=[smem] * 4 + [vmem] * (1 + len(pieces)),
        out_specs=(vmem,) * n_out,
        scratch_shapes=[
            pltpu.VMEM((n_in, edge, width), jnp.bfloat16),
            pltpu.VMEM((n_out * out_blocks, edge, width), F32),
        ],
        cost_estimate=pl.CostEstimate(
            flops=2 * blocks.shape[0] * edge * edge * width,
            bytes_accessed=2 * blocks.size + 2 * n_in * edge * width + 4 * n_out * out_blocks * edge * width,
            transcendentals=0,
        ),
    )(*scalars, blocks, *pieces)


def spread(v):
    return jnp.broadcast_to(v, (SUB, LANES))


def eliminate(tiles, offset, done):
    below = lax.broadcasted_iota(jnp.int32, (SUB, LANES), 0) >= STEP
    for k in range(0, BLOCK, STEP):
        g, s = divmod(k, SUB)
        lane = offset + k
        head = tiles[g]
        rows = [spread(head[s + a : s + a + 1, :]) for a in range(STEP)]
        pivot = [[spread(head[s + a : s + a + 1, lane + b : lane + b + 1]) for b in range(a + 1)] for a in range(STEP)]
        rest = list(range(g if s == 0 else g + 1, len(tiles)))
        cols = {i: [spread(tiles[i][:, lane + a : lane + a + 1]) for a in range(STEP)] for i in rest}
        inverse = []
        for a in range(STEP):
            inverse.append(1.0 / pivot[a][a])
            for n in range(a + 1, STEP):
                ratio = pivot[n][a] * inverse[a]
                for b in range(a + 1, n + 1):
                    pivot[n][b] = pivot[n][b] - ratio * pivot[b][a]
                rows[n] = rows[n] - ratio * rows[a]
                for i in rest:
                    cols[i][n] = cols[i][n] - ratio * cols[i][a]
        for a in range(STEP):
            done[k + a : k + a + 1, :] = (rows[a] * lax.rsqrt(pivot[a][a]))[0:1, :]
        scaled = [rows[a] * inverse[a] for a in range(STEP)]
        for i in rest:
            take = (cols[i][0] * scaled[0] + cols[i][1] * scaled[1]) + (cols[i][2] * scaled[2] + cols[i][3] * scaled[3])
            if i == g:
                take = jnp.where(below, take, 0.0)
            tiles[i] = tiles[i] - take


def factor_kernel(place, piece0, piece1, piece2, piece3, products, basis, factor, work, done):
    edge, size = products.shape
    rows = size // (N_CORE * N_Y)
    my_core, my_y = place[0] & (N_CORE - 1), place[1] & (N_Y - 1)
    for k, piece in enumerate((piece0, piece1, piece2, piece3)):
        for side in range(N_CORE):
            at = (((my_core + side) & 1) * N_Y + ((my_y + k) & (N_Y - 1))) * rows
            work[pl.ds(pl.multiple_of(at, rows), rows), :size] = piece[side] * (1.0 / (N_ROW * N_COL * edge))
    work[:, size:] = products[...].T
    for p in range(size // BLOCK):
        top = p * BLOCK
        tile, offset = top // LANES * LANES, top % LANES
        lanes = lax.broadcasted_iota(jnp.int32, (SUB, LANES), 1)
        subs = lax.broadcasted_iota(jnp.int32, (SUB, LANES), 0)
        inside = (lanes >= offset) & (lanes < offset + BLOCK)
        tiles = []
        for i in range(BLOCK // SUB):
            unit = jnp.where(lanes == subs + (i * SUB + BLOCK - offset), 1.0, 0.0)
            part = work[top + i * SUB : top + (i + 1) * SUB, tile : tile + LANES]
            tiles.append(jnp.where(inside, part, unit))
        eliminate(tiles, offset, done)
        inside_all = lax.broadcasted_iota(jnp.int32, (BLOCK, LANES), 1) // BLOCK == offset // BLOCK
        inverse = jnp.where(inside_all, 0.0, done[...])
        panel = work[top : top + BLOCK, :]
        upper = jnp.dot(inverse, jnp.concatenate([panel, panel], 0), precision=lax.Precision.HIGHEST, preferred_element_type=F32)
        rows = lax.broadcasted_iota(jnp.int32, (BLOCK, size), 0) + top
        keep = lax.broadcasted_iota(jnp.int32, (BLOCK, size), 1) >= rows
        head = jnp.where(keep, upper[:, :size], 0.0)
        factor[top : top + BLOCK, :] = head
        work[top : top + BLOCK, size:] = upper[:, size:]
        if top + BLOCK < size:
            low = (top + BLOCK) // LANES * LANES
            full = jnp.concatenate([head, upper[:, size:]], 1)
            take = lax.dot_general(
                head[:, low:], full[:, low:], (((0,), (0,)), ((), ())), precision=lax.Precision.HIGHEST, preferred_element_type=F32
            )
            work[top + BLOCK :, low:] = work[top + BLOCK :, low:] - take[top + BLOCK - low :, :]
    basis[...] = work[:, size:].T


def factor_and_basis(place, pieces, products):
    edge, size = products.shape
    vmem = pl.BlockSpec(memory_space=pltpu.VMEM)
    return pl.pallas_call(
        factor_kernel,
        out_shape=(jax.ShapeDtypeStruct((edge, size), F32), jax.ShapeDtypeStruct((size, size), F32)),
        in_specs=[pl.BlockSpec(memory_space=pltpu.SMEM)] + [vmem] * 5,
        out_specs=(vmem, vmem),
        scratch_shapes=[pltpu.VMEM((size, size + edge), F32), pltpu.VMEM((BLOCK, LANES), F32)],
        name="factor",
    )(place, *pieces, products)


def gram_pieces(products, place):
    width = products.shape[1]
    half, piece = width // N_CORE, width // (N_CORE * N_Y)
    my_core, my_y = place[0] & (N_CORE - 1), place[1] & (N_Y - 1)
    local = jnp.dot(products.T, products, precision=lax.Precision.HIGHEST, preferred_element_type=F32)
    mine = lax.dynamic_slice_in_dim(local, my_core * half, half, 0)
    other = lax.dynamic_slice_in_dim(local, (1 - my_core) * half, half, 0)
    pair = mine + to_core(other)
    parts = [lax.dynamic_slice_in_dim(pair, ((my_y + k) & (N_Y - 1)) * piece, piece, 0) for k in range(N_Y)]
    got = ring_sum([parts[0]] + [to_y(parts[k], k) for k in range(1, N_Y)])
    got = ring_sum([got] + [to_x(got, k) for k in range(1, N_X)])
    got = got + to_zl(got)
    got = ring_sum([got] + [to_z(got, k) for k in range(1, N_ZH)])
    both = jnp.stack([got, to_core(got)])
    return [both] + [to_y(both, -k) for k in range(1, N_Y)]


def body(blocks, block_rows, block_cols, counts, trials):
    place = jnp.stack([lax.axis_index("row"), lax.axis_index("col")]).astype(jnp.int32)
    scalars = (place, counts, block_rows, block_cols)
    first = jnp.stack([trials, to_zl(trials)])
    zs = jnp.stack([trials] + [to_z(trials, -k) for k in range(1, N_ZH)])
    row_pieces = [first] + [to_y(first, -k) for k in range(1, N_Y)]
    col_pieces = [zs] + [to_x(zs, -k) for k in range(1, N_X)]
    col_keep, col_send = products_of(mirror_kernel, scalars, blocks[0], row_pieces, N_CORE, N_X * N_ZH)
    col_pieces = col_pieces + [to_core(v) for v in col_pieces]
    row_outs = products_of(direct_kernel, scalars, blocks[0], col_pieces, N_Y, N_ZL)
    pair = col_keep + to_core(col_send)
    parts = [pair[k * N_ZH : (k + 1) * N_ZH] for k in range(N_X)]
    got = ring_sum([parts[0]] + [to_x(parts[k], k) for k in range(1, N_X)])
    rows = ring_sum([row_outs[0]] + [to_y(row_outs[k], k) for k in range(1, N_Y)])
    row_sum = rows[0] + to_zl(rows[1])
    col_sum = ring_sum([got[0]] + [to_z(got[k], k) for k in range(1, N_ZH)])
    products = row_sum + col_sum
    return factor_and_basis(place, gram_pieces(products, place), products)


def solution(mesh):
    return jax.shard_map(
        body,
        mesh=mesh,
        in_specs=(
            P("row", "col", None, None),
            P("row", "col"),
            P("row", "col"),
            P("row", "col"),
            P(("col", "row"), None),
        ),
        out_specs=(P(("col", "row"), None), P()),
        check_vma=False,
    )
```

profile of v0, /device:TPU:1, one launch (start us, length us, event | category | flops | bytes accessed | tf_op | source)
XLA Modules:
  0.0 173.8 jit_solution(206085413260850420)
XLA Ops:
  0.6 2.5 %collective-permute-start.14 = (bf16[128,256]{1,0:T(8,128)(2,1)}, bf16[128,256]{1,0:T(8,128)(2,1)S(1)}, u32[]{:S(2)}, u32[]{:S(2)}) collective-permute-start(bf16[128,256]{1,0:T(8,128)(2,1)} %param.9), channel_id=1, source_target_pairs={{0,4},{1,5},{2,6},{3,7},{4,0},{5,1},{6,2},{7,3},{8,12},{9,13},{10,... | collective-permute-start | bytes 196616 | tf_op jit(solution)/shard_map/ppermute | solution.py:45
  3.2 1.9 %collective-permute-done.14 = bf16[128,256]{1,0:T(8,128)(2,1)S(1)} collective-permute-done((bf16[128,256]{1,0:T(8,128)(2,1)}, bf16[128,256]{1,0:T(8,128)(2,1)S(1)}, u32[]{:S(2)}, u32[]{:S(2)}) %collective-permute-start.14) | collective-permute-done | bytes 65568 | tf_op jit(solution)/shard_map/ppermute | solution.py:45
  5.9 2.8 %collective-permute-start.15 = (bf16[2,128,256]{2,1,0:T(8,128)(2,1)S(1)}, bf16[2,128,256]{2,1,0:T(8,128)(2,1)S(1)}, u32[]{:S(2)}, u32[]{:S(2)}) collective-permute-start(bf16[2,128,256]{2,1,0:T(8,128)(2,1)S(1)} %pad_maximum_fusion.1.refs_0_), channel_id=1, source_target_pairs={{0,3},{1,0},{2,1},{3,2},{4,7},{5,4},{6,5},{7,6},{8,11},{9,8},{10,9... | collective-permute-start | bytes 393224 | tf_op jit(solution)/shard_map/ppermute | solution.py:41
  11.1 1.4 collective-permute-done.15.refs_1_
  12.4 1.7 collective-permute-done.16.refs_2_
  14.2 3.3 %collective-permute-done.17.refs_3_ = bf16[2,128,256]{2,1,0:T(8,128)(2,1)S(1)} collective-permute-done((bf16[2,128,256]{2,1,0:T(8,128)(2,1)S(1)}, bf16[2,128,256]{2,1,0:T(8,128)(2,1)S(1)}, u32[]{:S(2)}, u32[]{:S(2)}) %collective-permute-start.17) | collective-permute-done | bytes 131104 | tf_op jit(solution)/shard_map/ppermute | solution.py:41
  18.1 5.8 %shard_map.69 = (f32[16,128,256]{2,1,0:T(8,128)}, f32[16,128,256]{2,1,0:T(8,128)}) custom-call(s32[2]{0:T(128)} %pad_add_fusion.place, s32[1,1]{1,0:T(1,128)S(6)} %copy.7.counts, s32[1,64]{1,0:T(1,128)} %rows.3, s32[1,64]{1,0:T(1,128)} %cols.3, bf16[64,128,128]{2,1,0:T(8,128)(2,1)} %bitcast.34, bf16[2,128,256]{2,1,0:T(8,128)(2,1)} %copy-done.3, ...), custom_call_target="tpu_custom_call" | custom-call | flops 536870912 | bytes 6815744 | tf_op jit(solution)/shard_map/pallas_call | solution.py:115
  23.9 2.1 %collective-permute-start.18 = (f32[16,128,256]{2,1,0:T(8,128)}, f32[16,128,256]{2,1,0:T(8,128)}, u32[]{:S(2)}, u32[]{:S(2)}) collective-permute-start(f32[16,128,256]{2,1,0:T(8,128)} %get-tuple-element.13), channel_id=1, source_target_pairs={{0,8},{8,0},{16,24},{24,16},{32,40},{40,32},{48,56},{56,48},{64,72... | collective-permute-start | bytes 6291464 | tf_op jit(solution)/shard_map/ppermute | solution.py:37
  26.0 1.6 collective-permute-start.2
  27.6 4.7 %collective-permute-start.1 = (bf16[128,256]{1,0:T(8,128)(2,1)S(1)}, bf16[128,256]{1,0:T(8,128)(2,1)S(1)}, u32[]{:S(2)}, u32[]{:S(2)}) collective-permute-start(bf16[128,256]{1,0:T(8,128)(2,1)S(1)} %copy-done.6), channel_id=1, source_target_pairs={{0,128},{8,136},{16,144},{24,152},{32,160},{40,168},{48,176},{56,1... | collective-permute-start | bytes 196616 | tf_op jit(solution)/shard_map/ppermute | solution.py:29
  32.3 2.9 %collective-permute-start = (bf16[128,256]{1,0:T(8,128)(2,1)S(1)}, bf16[128,256]{1,0:T(8,128)(2,1)S(1)}, u32[]{:S(2)}, u32[]{:S(2)}) collective-permute-start(bf16[128,256]{1,0:T(8,128)(2,1)S(1)} %copy-done.6), channel_id=1, source_target_pairs={{0,192},{8,200},{16,208},{24,216},{32,224},{40,232},{48,240},{56,2... | collective-permute-start | bytes 196616 | tf_op jit(solution)/shard_map/ppermute | solution.py:29
  35.8 0.9 collective-permute-done
  36.8 5.9 %collective-permute-start.3 = (bf16[4,128,256]{2,1,0:T(8,128)(2,1)S(1)}, bf16[4,128,256]{2,1,0:T(8,128)(2,1)S(1)}, u32[]{:S(2)}, u32[]{:S(2)}) collective-permute-start(bf16[4,128,256]{2,1,0:T(8,128)(2,1)S(1)} %pad_maximum_fusion.refs_0_), channel_id=1, source_target_pairs={{0,48},{8,56},{16,0},{24,8},{32,16},{40,24},{48,32},{56,40},{64,11... | collective-permute-start | bytes 786440 | tf_op jit(solution)/shard_map/ppermute | solution.py:33
  43.3 1.1 collective-permute-start.6
  44.4 8.9 %collective-permute-done.3.refs_1_ = bf16[4,128,256]{2,1,0:T(8,128)(2,1)S(1)} collective-permute-done((bf16[4,128,256]{2,1,0:T(8,128)(2,1)S(1)}, bf16[4,128,256]{2,1,0:T(8,128)(2,1)S(1)}, u32[]{:S(2)}, u32[]{:S(2)}) %collective-permute-start.3) | collective-permute-done | bytes 262176 | tf_op jit(solution)/shard_map/ppermute | solution.py:33
  53.3 1.5 collective-permute-start.7
  54.9 3.1 %collective-permute-done.5.refs_3_ = bf16[4,128,256]{2,1,0:T(8,128)(2,1)S(1)} collective-permute-done((bf16[4,128,256]{2,1,0:T(8,128)(2,1)S(1)}, bf16[4,128,256]{2,1,0:T(8,128)(2,1)S(1)}, u32[]{:S(2)}, u32[]{:S(2)}) %collective-permute-start.5) | collective-permute-done | bytes 262176 | tf_op jit(solution)/shard_map/ppermute | solution.py:33
  60.0 4.8 %shard_map.68 = (f32[2,128,256]{2,1,0:T(8,128)}, f32[2,128,256]{2,1,0:T(8,128)}, f32[2,128,256]{2,1,0:T(8,128)}, f32[2,128,256]{2,1,0:T(8,128)}) custom-call(s32[2]{0:T(128)} %pad_add_fusion.place, s32[1,1]{1,0:T(1,128)S(6)} %copy.7.counts, s32[1,64]{1,0:T(1,128)} %rows.3, s32[1,64]{1,0:T(1,128)} %cols.3, bf16[64,128,128]{2,1,0:T(8,128)(2,1)} %bitcast.35, ...), custom_call_target="tpu_custom_call" | custom-call | flops 536870912 | bytes 5242880 | tf_op jit(solution)/shard_map/pallas_call | solution.py:115
  64.8 2.7 %collective-permute-start.12 = (f32[2,128,256]{2,1,0:T(8,128)}, f32[2,128,256]{2,1,0:T(8,128)S(1)}, u32[]{:S(2)}, u32[]{:S(2)}) collective-permute-start(f32[2,128,256]{2,1,0:T(8,128)} %get-tuple-element.11), channel_id=1, source_target_pairs={{0,3},{1,0},{2,1},{3,2},{4,7},{5,4},{6,5},{7,6},{8,11},{9,8},{10,9... | collective-permute-start | bytes 786440 | tf_op jit(solution)/shard_map/ppermute | solution.py:41
  67.5 1.9 %add.100 = f32[16,128,256]{2,1,0:T(8,128)S(1)} add(f32[16,128,256]{2,1,0:T(8,128)S(1)} %copy-done, f32[16,128,256]{2,1,0:T(8,128)} %collective-permute-done.18) | non-fusion elementwise | flops 524288 | bytes 6291456 | tf_op jit(solution)/shard_map/add | solution.py:246
  69.7 1.6 collective-permute-start.20
  71.3 2.2 %collective-permute-done.11 = f32[2,128,256]{2,1,0:T(8,128)S(1)} collective-permute-done((f32[2,128,256]{2,1,0:T(8,128)}, f32[2,128,256]{2,1,0:T(8,128)S(1)}, u32[]{:S(2)}, u32[]{:S(2)}) %collective-permute-start.11) | collective-permute-done | bytes 262176 | tf_op jit(solution)/shard_map/ppermute | solution.py:41
  73.4 2.2 %collective-permute-start.21 = (f32[4,128,256]{2,1,0:T(8,128)S(1)}, f32[4,128,256]{2,1,0:T(8,128)S(1)}, u32[]{:S(2)}, u32[]{:S(2)}) collective-permute-start(f32[4,128,256]{2,1,0:T(8,128)S(1)} %get-tuple-element.14), channel_id=1, source_target_pairs={{0,48},{8,56},{16,0},{24,8},{32,16},{40,24},{48,32},{56,40},{64,11... | collective-permute-start | bytes 1572872 | tf_op jit(solution)/shard_map/ppermute | solution.py:33
  75.7 4.0 %collective-permute-done.10 = f32[2,128,256]{2,1,0:T(8,128)S(1)} collective-permute-done((f32[2,128,256]{2,1,0:T(8,128)}, f32[2,128,256]{2,1,0:T(8,128)S(1)}, u32[]{:S(2)}, u32[]{:S(2)}) %collective-permute-start.10) | collective-permute-done | bytes 262176 | tf_op jit(solution)/shard_map/ppermute | solution.py:41
  79.8 3.7 %collective-permute-done.19 = f32[4,128,256]{2,1,0:T(8,128)S(1)} collective-permute-done((f32[4,128,256]{2,1,0:T(8,128)S(1)}, f32[4,128,256]{2,1,0:T(8,128)S(1)}, u32[]{:S(2)}, u32[]{:S(2)}) %collective-permute-start.19) | collective-permute-done | bytes 524320 | tf_op jit(solution)/shard_map/ppermute | solution.py:33
  83.5 12.3 %collective-permute-done.20 = f32[4,128,256]{2,1,0:T(8,128)S(1)} collective-permute-done((f32[4,128,256]{2,1,0:T(8,128)S(1)}, f32[4,128,256]{2,1,0:T(8,128)S(1)}, u32[]{:S(2)}, u32[]{:S(2)}) %collective-permute-start.20) | collective-permute-done | bytes 524320 | tf_op jit(solution)/shard_map/ppermute | solution.py:33
  96.0 3.7 %collective-permute-start.22 = (f32[128,256]{1,0:T(8,128)S(1)}, f32[128,256]{1,0:T(8,128)S(1)}, u32[]{:S(2)}, u32[]{:S(2)}) collective-permute-start(f32[128,256]{1,0:T(8,128)S(1)} %get-tuple-element.19), channel_id=1, source_target_pairs={{0,128},{8,136},{16,144},{24,152},{32,160},{40,168},{48,176},{56,1... | collective-permute-start | bytes 393224 | tf_op jit(solution)/shard_map/ppermute | solution.py:29
  99.7 2.0 %collective-permute-start.23 = (f32[128,256]{1,0:T(8,128)S(1)}, f32[128,256]{1,0:T(8,128)S(1)}, u32[]{:S(2)}, u32[]{:S(2)}) collective-permute-start(f32[128,256]{1,0:T(8,128)S(1)} %get-tuple-element.18), channel_id=1, source_target_pairs={{0,64},{8,72},{16,80},{24,88},{32,96},{40,104},{48,112},{56,120},{... | collective-permute-start | bytes 393224 | tf_op jit(solution)/shard_map/ppermute | solution.py:29
  101.8 1.5 collective-permute-start.24
  103.3 1.1 collective-permute-done.22
  104.4 5.7 %collective-permute-done.23 = f32[128,256]{1,0:T(8,128)S(1)} collective-permute-done((f32[128,256]{1,0:T(8,128)S(1)}, f32[128,256]{1,0:T(8,128)S(1)}, u32[]{:S(2)}, u32[]{:S(2)}) %collective-permute-start.23) | collective-permute-done | bytes 131104 | tf_op jit(solution)/shard_map/ppermute | solution.py:29
  110.1 3.9 %collective-permute-done.24 = f32[128,256]{1,0:T(8,128)S(1)} collective-permute-done((f32[128,256]{1,0:T(8,128)S(1)}, f32[128,256]{1,0:T(8,128)S(1)}, u32[]{:S(2)}, u32[]{:S(2)}) %collective-permute-start.24) | collective-permute-done | bytes 131104 | tf_op jit(solution)/shard_map/ppermute | solution.py:29
  115.1 1.0 collective-permute-done.25
  116.5 2.5 %collective-permute-start.28 = (f32[32,256]{1,0:T(8,128)S(1)}, f32[32,256]{1,0:T(8,128)S(1)}, u32[]{:S(2)}, u32[]{:S(2)}) collective-permute-start(f32[32,256]{1,0:T(8,128)S(1)} %get-tuple-element.21), channel_id=1, source_target_pairs={{0,3},{1,0},{2,1},{3,2},{4,7},{5,4},{6,5},{7,6},{8,11},{9,8},{10,9... | collective-permute-start | bytes 98312 | tf_op jit(solution)/shard_map/ppermute | solution.py:41
  120.2 3.0 %collective-permute-done.26 = f32[32,256]{1,0:T(8,128)S(1)} collective-permute-done((f32[32,256]{1,0:T(8,128)S(1)}, f32[32,256]{1,0:T(8,128)S(1)}, u32[]{:S(2)}, u32[]{:S(2)}) %collective-permute-start.26) | collective-permute-done | bytes 32800 | tf_op jit(solution)/shard_map/ppermute | solution.py:41
  123.3 2.6 %collective-permute-start.31 = (f32[32,256]{1,0:T(8,128)S(1)}, f32[32,256]{1,0:T(8,128)S(1)}, u32[]{:S(2)}, u32[]{:S(2)}) collective-permute-start(f32[32,256]{1,0:T(8,128)S(1)} %add_add_fusion.3), channel_id=1, source_target_pairs={{0,48},{8,56},{16,0},{24,8},{32,16},{40,24},{48,32},{56,40},{64,11... | collective-permute-start | bytes 98312 | tf_op jit(solution)/shard_map/ppermute | solution.py:33
  127.3 3.0 %collective-permute-done.29 = f32[32,256]{1,0:T(8,128)S(1)} collective-permute-done((f32[32,256]{1,0:T(8,128)S(1)}, f32[32,256]{1,0:T(8,128)S(1)}, u32[]{:S(2)}, u32[]{:S(2)}) %collective-permute-start.29) | collective-permute-done | bytes 32800 | tf_op jit(solution)/shard_map/ppermute | solution.py:33
  130.6 2.8 %collective-permute-done.32 = f32[32,256]{1,0:T(8,128)S(1)} collective-permute-done((f32[32,256]{1,0:T(8,128)S(1)}, f32[32,256]{1,0:T(8,128)S(1)}, u32[]{:S(2)}, u32[]{:S(2)}) %collective-permute-start.32) | collective-permute-done | bytes 32800 | tf_op jit(solution)/shard_map/ppermute | solution.py:45
  133.7 3.3 %collective-permute-start.35 = (f32[32,256]{1,0:T(8,128)S(1)}, f32[32,256]{1,0:T(8,128)S(1)}, u32[]{:S(2)}, u32[]{:S(2)}) collective-permute-start(f32[32,256]{1,0:T(8,128)S(1)} %add.124), channel_id=1, source_target_pairs={{0,192},{8,200},{16,208},{24,216},{32,224},{40,232},{48,240},{56,2... | collective-permute-start | bytes 98312 | tf_op jit(solution)/shard_map/ppermute | solution.py:29
  137.0 2.4 %collective-permute-start.33 = (f32[32,256]{1,0:T(8,128)S(1)}, f32[32,256]{1,0:T(8,128)S(1)}, u32[]{:S(2)}, u32[]{:S(2)}) collective-permute-start(f32[32,256]{1,0:T(8,128)S(1)} %add.124), channel_id=1, source_target_pairs={{0,128},{8,136},{16,144},{24,152},{32,160},{40,168},{48,176},{56,1... | collective-permute-start | bytes 98312 | tf_op jit(solution)/shard_map/ppermute | solution.py:29
  139.4 4.3 %collective-permute-done.33 = f32[32,256]{1,0:T(8,128)S(1)} collective-permute-done((f32[32,256]{1,0:T(8,128)S(1)}, f32[32,256]{1,0:T(8,128)S(1)}, u32[]{:S(2)}, u32[]{:S(2)}) %collective-permute-start.33) | collective-permute-done | bytes 32800 | tf_op jit(solution)/shard_map/ppermute | solution.py:29
  143.7 6.8 %collective-permute-start.36 = (f32[32,256]{1,0:T(8,128)S(1)}, f32[32,256]{1,0:T(8,128)S(1)}, u32[]{:S(2)}, u32[]{:S(2)}) collective-permute-start(f32[32,256]{1,0:T(8,128)S(1)} %add_add_fusion.1), channel_id=1, source_target_pairs={{0,8},{8,0},{16,24},{24,16},{32,40},{40,32},{48,56},{56,48},{64,72... | collective-permute-start | bytes 98312 | tf_op jit(solution)/shard_map/ppermute | solution.py:37
  150.4 0.9 collective-permute-done.36
  151.9 0.9 collective-permute-start.39
  152.8 1.6 collective-permute-done.37.piece1
  154.5 1.6 collective-permute-done.38.piece2
  156.1 2.1 %collective-permute-done.39.piece3 = f32[2,32,256]{2,1,0:T(8,128)S(1)} collective-permute-done((f32[2,32,256]{2,1,0:T(8,128)S(1)}, f32[2,32,256]{2,1,0:T(8,128)S(1)}, u32[]{:S(2)}, u32[]{:S(2)}) %collective-permute-start.39) | collective-permute-done | bytes 65568 | tf_op jit(solution)/shard_map/ppermute | solution.py:41
  158.8 15.0 %factor.1 = (f32[128,256]{1,0:T(8,128)}, f32[256,256]{1,0:T(8,128)}) custom-call(s32[2]{0:T(128)} %pad_add_fusion.place, f32[2,32,256]{2,1,0:T(8,128)} %copy-done.5, f32[2,32,256]{2,1,0:T(8,128)} %copy-done.16, f32[2,32,256]{2,1,0:T(8,128)} %copy-done.17, f32[2,32,256]{2,1,0:T(8,128)} %copy-done.18, f32[128,256]{1,0:T(8,128)} %copy-done.1), custom_call_target="tpu_custom_call" | custom-call | tf_op jit(solution)/shard_map/factor/pallas_call | solution.py:209
  (92 shorter events, 13.3 us)
Async XLA Ops:
  0.6 25.4 %copy-start.6 = (bf16[128,256]{1,0:T(8,128)(2,1)S(1)}, bf16[128,256]{1,0:T(8,128)(2,1)}, u32[]{:S(2)}) copy-start(bf16[128,256]{1,0:T(8,128)(2,1)} %param.9) | copy-start | bytes 196612
  0.6 4.4 %collective-permute-start.14 = (bf16[128,256]{1,0:T(8,128)(2,1)}, bf16[128,256]{1,0:T(8,128)(2,1)S(1)}, u32[]{:S(2)}, u32[]{:S(2)}) collective-permute-start(bf16[128,256]{1,0:T(8,128)(2,1)} %param.9), channel_id=1, source_target_pairs={{0,4},{1,5},{2,6},{3,7},{4,0},{5,1},{6,2},{7,3},{8,12},{9,13},{10,... | collective-permute-start | bytes 196616 | tf_op jit(solution)/shard_map/ppermute | solution.py:45
  5.9 11.5 %copy-start.3 = (bf16[2,128,256]{2,1,0:T(8,128)(2,1)}, bf16[2,128,256]{2,1,0:T(8,128)(2,1)S(1)}, u32[]{:S(2)}) copy-start(bf16[2,128,256]{2,1,0:T(8,128)(2,1)S(1)} %pad_maximum_fusion.1.refs_0_) | copy-start | bytes 393220
  5.9 6.5 %collective-permute-start.15 = (bf16[2,128,256]{2,1,0:T(8,128)(2,1)S(1)}, bf16[2,128,256]{2,1,0:T(8,128)(2,1)S(1)}, u32[]{:S(2)}, u32[]{:S(2)}) collective-permute-start(bf16[2,128,256]{2,1,0:T(8,128)(2,1)S(1)} %pad_maximum_fusion.1.refs_0_), channel_id=1, source_target_pairs={{0,3},{1,0},{2,1},{3,2},{4,7},{5,4},{6,5},{7,6},{8,11},{9,8},{10,9... | collective-permute-start | bytes 393224 | tf_op jit(solution)/shard_map/ppermute | solution.py:41
  8.7 5.4 %collective-permute-start.16 = (bf16[2,128,256]{2,1,0:T(8,128)(2,1)S(1)}, bf16[2,128,256]{2,1,0:T(8,128)(2,1)S(1)}, u32[]{:S(2)}, u32[]{:S(2)}) collective-permute-start(bf16[2,128,256]{2,1,0:T(8,128)(2,1)S(1)} %pad_maximum_fusion.1.refs_0_), channel_id=1, source_target_pairs={{0,2},{1,3},{2,0},{3,1},{4,6},{5,7},{6,4},{7,5},{8,10},{9,11},{10,... | collective-permute-start | bytes 393224 | tf_op jit(solution)/shard_map/ppermute | solution.py:41
  9.1 8.3 %collective-permute-start.17 = (bf16[2,128,256]{2,1,0:T(8,128)(2,1)S(1)}, bf16[2,128,256]{2,1,0:T(8,128)(2,1)S(1)}, u32[]{:S(2)}, u32[]{:S(2)}) collective-permute-start(bf16[2,128,256]{2,1,0:T(8,128)(2,1)S(1)} %pad_maximum_fusion.1.refs_0_), channel_id=1, source_target_pairs={{0,1},{1,2},{2,3},{3,0},{4,5},{5,6},{6,7},{7,4},{8,9},{9,10},{10,1... | collective-permute-start | bytes 393224 | tf_op jit(solution)/shard_map/ppermute | solution.py:41
  23.9 43.6 %collective-permute-start.18 = (f32[16,128,256]{2,1,0:T(8,128)}, f32[16,128,256]{2,1,0:T(8,128)}, u32[]{:S(2)}, u32[]{:S(2)}) collective-permute-start(f32[16,128,256]{2,1,0:T(8,128)} %get-tuple-element.13), channel_id=1, source_target_pairs={{0,8},{8,0},{16,24},{24,16},{32,40},{40,32},{48,56},{56,48},{64,72... | collective-permute-start | bytes 6291464 | tf_op jit(solution)/shard_map/ppermute | solution.py:37
  26.0 9.2 %collective-permute-start.2 = (bf16[128,256]{1,0:T(8,128)(2,1)S(1)}, bf16[128,256]{1,0:T(8,128)(2,1)S(1)}, u32[]{:S(2)}, u32[]{:S(2)}) collective-permute-start(bf16[128,256]{1,0:T(8,128)(2,1)S(1)} %copy-done.6), channel_id=1, source_target_pairs={{0,64},{8,72},{16,80},{24,88},{32,96},{40,104},{48,112},{56,120},{... | collective-permute-start | bytes 196616 | tf_op jit(solution)/shard_map/ppermute | solution.py:29
  27.6 8.2 %collective-permute-start.1 = (bf16[128,256]{1,0:T(8,128)(2,1)S(1)}, bf16[128,256]{1,0:T(8,128)(2,1)S(1)}, u32[]{:S(2)}, u32[]{:S(2)}) collective-permute-start(bf16[128,256]{1,0:T(8,128)(2,1)S(1)} %copy-done.6), channel_id=1, source_target_pairs={{0,128},{8,136},{16,144},{24,152},{32,160},{40,168},{48,176},{56,1... | collective-permute-start | bytes 196616 | tf_op jit(solution)/shard_map/ppermute | solution.py:29
  32.3 4.4 %collective-permute-start = (bf16[128,256]{1,0:T(8,128)(2,1)S(1)}, bf16[128,256]{1,0:T(8,128)(2,1)S(1)}, u32[]{:S(2)}, u32[]{:S(2)}) collective-permute-start(bf16[128,256]{1,0:T(8,128)(2,1)S(1)} %copy-done.6), channel_id=1, source_target_pairs={{0,192},{8,200},{16,208},{24,216},{32,224},{40,232},{48,240},{56,2... | collective-permute-start | bytes 196616 | tf_op jit(solution)/shard_map/ppermute | solution.py:29
  36.7 23.3 %copy-start.2 = (bf16[4,128,256]{2,1,0:T(8,128)(2,1)}, bf16[4,128,256]{2,1,0:T(8,128)(2,1)S(1)}, u32[]{:S(2)}) copy-start(bf16[4,128,256]{2,1,0:T(8,128)(2,1)S(1)} %pad_maximum_fusion.refs_0_) | copy-start | bytes 786436
  36.8 30.7 %copy-start = (f32[16,128,256]{2,1,0:T(8,128)S(1)}, f32[16,128,256]{2,1,0:T(8,128)}, u32[]{:S(2)}) copy-start(f32[16,128,256]{2,1,0:T(8,128)} %get-tuple-element.12) | copy-start | bytes 6291460
  36.8 16.5 %collective-permute-start.3 = (bf16[4,128,256]{2,1,0:T(8,128)(2,1)S(1)}, bf16[4,128,256]{2,1,0:T(8,128)(2,1)S(1)}, u32[]{:S(2)}, u32[]{:S(2)}) collective-permute-start(bf16[4,128,256]{2,1,0:T(8,128)(2,1)S(1)} %pad_maximum_fusion.refs_0_), channel_id=1, source_target_pairs={{0,48},{8,56},{16,0},{24,8},{32,16},{40,24},{48,32},{56,40},{64,11... | collective-permute-start | bytes 786440 | tf_op jit(solution)/shard_map/ppermute | solution.py:33
  42.7 12.1 %collective-permute-start.4 = (bf16[4,128,256]{2,1,0:T(8,128)(2,1)S(1)}, bf16[4,128,256]{2,1,0:T(8,128)(2,1)S(1)}, u32[]{:S(2)}, u32[]{:S(2)}) collective-permute-start(bf16[4,128,256]{2,1,0:T(8,128)(2,1)S(1)} %pad_maximum_fusion.refs_0_), channel_id=1, source_target_pairs={{0,32},{8,40},{16,48},{24,56},{32,0},{40,8},{48,16},{56,24},{64,96... | collective-permute-start | bytes 786440 | tf_op jit(solution)/shard_map/ppermute | solution.py:33
  43.0 15.1 %collective-permute-start.5 = (bf16[4,128,256]{2,1,0:T(8,128)(2,1)S(1)}, bf16[4,128,256]{2,1,0:T(8,128)(2,1)S(1)}, u32[]{:S(2)}, u32[]{:S(2)}) collective-permute-start(bf16[4,128,256]{2,1,0:T(8,128)(2,1)S(1)} %pad_maximum_fusion.refs_0_), channel_id=1, source_target_pairs={{0,16},{8,24},{16,32},{24,40},{32,48},{40,56},{48,0},{56,8},{64,80... | collective-permute-start | bytes 786440 | tf_op jit(solution)/shard_map/ppermute | solution.py:33
  43.3 15.2 %collective-permute-start.6 = (bf16[4,128,256]{2,1,0:T(8,128)(2,1)S(1)}, bf16[4,128,256]{2,1,0:T(8,128)(2,1)S(1)}, u32[]{:S(2)}, u32[]{:S(2)}) collective-permute-start(bf16[4,128,256]{2,1,0:T(8,128)(2,1)S(1)} %pad_maximum_fusion.refs_0_), channel_id=1, source_target_pairs={{0,8},{8,0},{16,24},{24,16},{32,40},{40,32},{48,56},{56,48},{64,72... | collective-permute-start | bytes 786440 | tf_op jit(solution)/shard_map/ppermute | solution.py:37
  53.3 6.7 %copy-start.7 = (bf16[4,128,256]{2,1,0:T(8,128)(2,1)}, bf16[4,128,256]{2,1,0:T(8,128)(2,1)S(1)}, u32[]{:S(2)}) copy-start(bf16[4,128,256]{2,1,0:T(8,128)(2,1)S(1)} %collective-permute-done.3.refs_1_) | copy-start | bytes 786436
  53.3 5.2 %collective-permute-start.7 = (bf16[4,128,256]{2,1,0:T(8,128)(2,1)S(1)}, bf16[4,128,256]{2,1,0:T(8,128)(2,1)S(1)}, u32[]{:S(2)}, u32[]{:S(2)}) collective-permute-start(bf16[4,128,256]{2,1,0:T(8,128)(2,1)S(1)} %collective-permute-done.3.refs_1_), channel_id=1, source_target_pairs={{0,8},{8,0},{16,24},{24,16},{32,40},{40,32},{48,56},{56,48},{64,72... | collective-permute-start | bytes 786440 | tf_op jit(solution)/shard_map/ppermute | solution.py:37
  54.8 3.7 %collective-permute-start.8 = (bf16[4,128,256]{2,1,0:T(8,128)(2,1)S(1)}, bf16[4,128,256]{2,1,0:T(8,128)(2,1)S(1)}, u32[]{:S(2)}, u32[]{:S(2)}) collective-permute-start(bf16[4,128,256]{2,1,0:T(8,128)(2,1)S(1)} %collective-permute-done.4.refs_2_), channel_id=1, source_target_pairs={{0,8},{8,0},{16,24},{24,16},{32,40},{40,32},{48,56},{56,48},{64,72... | collective-permute-start | bytes 786440 | tf_op jit(solution)/shard_map/ppermute | solution.py:37
  58.0 2.0 %collective-permute-start.9 = (bf16[4,128,256]{2,1,0:T(8,128)(2,1)S(1)}, bf16[4,128,256]{2,1,0:T(8,128)(2,1)}, u32[]{:S(2)}, u32[]{:S(2)}) collective-permute-start(bf16[4,128,256]{2,1,0:T(8,128)(2,1)S(1)} %collective-permute-done.5.refs_3_), channel_id=1, source_target_pairs={{0,8},{8,0},{16,24},{24,16},{32,40},{40,32},{48,56},{56,48},{64,72... | collective-permute-start | bytes 786440 | tf_op jit(solution)/shard_map/ppermute | solution.py:37
  64.8 8.6 %collective-permute-start.11 = (f32[2,128,256]{2,1,0:T(8,128)}, f32[2,128,256]{2,1,0:T(8,128)S(1)}, u32[]{:S(2)}, u32[]{:S(2)}) collective-permute-start(f32[2,128,256]{2,1,0:T(8,128)} %get-tuple-element.10), channel_id=1, source_target_pairs={{0,1},{1,2},{2,3},{3,0},{4,5},{5,6},{6,7},{7,4},{8,9},{9,10},{10,1... | collective-permute-start | bytes 786440 | tf_op jit(solution)/shard_map/ppermute | solution.py:41
  64.8 10.9 %collective-permute-start.12 = (f32[2,128,256]{2,1,0:T(8,128)}, f32[2,128,256]{2,1,0:T(8,128)S(1)}, u32[]{:S(2)}, u32[]{:S(2)}) collective-permute-start(f32[2,128,256]{2,1,0:T(8,128)} %get-tuple-element.11), channel_id=1, source_target_pairs={{0,3},{1,0},{2,1},{3,2},{4,7},{5,4},{6,5},{7,6},{8,11},{9,8},{10,9... | collective-permute-start | bytes 786440 | tf_op jit(solution)/shard_map/ppermute | solution.py:41
  67.5 12.1 %collective-permute-start.10 = (f32[2,128,256]{2,1,0:T(8,128)}, f32[2,128,256]{2,1,0:T(8,128)S(1)}, u32[]{:S(2)}, u32[]{:S(2)}) collective-permute-start(f32[2,128,256]{2,1,0:T(8,128)} %get-tuple-element.9), channel_id=1, source_target_pairs={{0,2},{1,3},{2,0},{3,1},{4,6},{5,7},{6,4},{7,5},{8,10},{9,11},{10,... | collective-permute-start | bytes 786440 | tf_op jit(solution)/shard_map/ppermute | solution.py:41
  69.4 10.3 %copy-start.4 = (f32[2,128,256]{2,1,0:T(8,128)S(1)}, f32[2,128,256]{2,1,0:T(8,128)}, u32[]{:S(2)}) copy-start(f32[2,128,256]{2,1,0:T(8,128)} %get-tuple-element.8) | copy-start | bytes 786436
  69.6 13.9 %collective-permute-start.19 = (f32[4,128,256]{2,1,0:T(8,128)S(1)}, f32[4,128,256]{2,1,0:T(8,128)S(1)}, u32[]{:S(2)}, u32[]{:S(2)}) collective-permute-start(f32[4,128,256]{2,1,0:T(8,128)S(1)} %get-tuple-element.16), channel_id=1, source_target_pairs={{0,32},{8,40},{16,48},{24,56},{32,0},{40,8},{48,16},{56,24},{64,96... | collective-permute-start | bytes 1572872 | tf_op jit(solution)/shard_map/ppermute | solution.py:33
  69.7 26.2 %collective-permute-start.20 = (f32[4,128,256]{2,1,0:T(8,128)S(1)}, f32[4,128,256]{2,1,0:T(8,128)S(1)}, u32[]{:S(2)}, u32[]{:S(2)}) collective-permute-start(f32[4,128,256]{2,1,0:T(8,128)S(1)} %get-tuple-element.15), channel_id=1, source_target_pairs={{0,16},{8,24},{16,32},{24,40},{32,48},{40,56},{48,0},{56,8},{64,80... | collective-permute-start | bytes 1572872 | tf_op jit(solution)/shard_map/ppermute | solution.py:33
  73.4 22.4 %collective-permute-start.21 = (f32[4,128,256]{2,1,0:T(8,128)S(1)}, f32[4,128,256]{2,1,0:T(8,128)S(1)}, u32[]{:S(2)}, u32[]{:S(2)}) collective-permute-start(f32[4,128,256]{2,1,0:T(8,128)S(1)} %get-tuple-element.14), channel_id=1, source_target_pairs={{0,48},{8,56},{16,0},{24,8},{32,16},{40,24},{48,32},{56,40},{64,11... | collective-permute-start | bytes 1572872 | tf_op jit(solution)/shard_map/ppermute | solution.py:33
  79.7 23.6 %collective-permute-start.13 = (f32[128,256]{1,0:T(8,128)S(1)}, f32[128,256]{1,0:T(8,128)S(1)}, u32[]{:S(2)}, u32[]{:S(2)}) collective-permute-start(f32[128,256]{1,0:T(8,128)S(1)} %slice_bitcast_fusion.4), channel_id=1, source_target_pairs={{0,4},{1,5},{2,6},{3,7},{4,0},{5,1},{6,2},{7,3},{8,12},{9,13},{10,... | collective-permute-start | bytes 393224 | tf_op jit(solution)/shard_map/ppermute | solution.py:45
  96.0 8.4 %collective-permute-start.22 = (f32[128,256]{1,0:T(8,128)S(1)}, f32[128,256]{1,0:T(8,128)S(1)}, u32[]{:S(2)}, u32[]{:S(2)}) collective-permute-start(f32[128,256]{1,0:T(8,128)S(1)} %get-tuple-element.19), channel_id=1, source_target_pairs={{0,128},{8,136},{16,144},{24,152},{32,160},{40,168},{48,176},{56,1... | collective-permute-start | bytes 393224 | tf_op jit(solution)/shard_map/ppermute | solution.py:29
  99.7 10.4 %collective-permute-start.23 = (f32[128,256]{1,0:T(8,128)S(1)}, f32[128,256]{1,0:T(8,128)S(1)}, u32[]{:S(2)}, u32[]{:S(2)}) collective-permute-start(f32[128,256]{1,0:T(8,128)S(1)} %get-tuple-element.18), channel_id=1, source_target_pairs={{0,64},{8,72},{16,80},{24,88},{32,96},{40,104},{48,112},{56,120},{... | collective-permute-start | bytes 393224 | tf_op jit(solution)/shard_map/ppermute | solution.py:29
  101.8 12.3 %collective-permute-start.24 = (f32[128,256]{1,0:T(8,128)S(1)}, f32[128,256]{1,0:T(8,128)S(1)}, u32[]{:S(2)}, u32[]{:S(2)}) collective-permute-start(f32[128,256]{1,0:T(8,128)S(1)} %get-tuple-element.17), channel_id=1, source_target_pairs={{0,192},{8,200},{16,208},{24,216},{32,224},{40,232},{48,240},{56,2... | collective-permute-start | bytes 393224 | tf_op jit(solution)/shard_map/ppermute | solution.py:29
  114.1 44.0 %copy-start.1 = (f32[128,256]{1,0:T(8,128)}, f32[128,256]{1,0:T(8,128)S(1)}, u32[]{:S(2)}) copy-start(f32[128,256]{1,0:T(8,128)S(1)} %fusion.3.products) | copy-start | bytes 393220
  114.6 1.6 collective-permute-start.25
  116.2 4.1 %collective-permute-start.27 = (f32[32,256]{1,0:T(8,128)S(1)}, f32[32,256]{1,0:T(8,128)S(1)}, u32[]{:S(2)}, u32[]{:S(2)}) collective-permute-start(f32[32,256]{1,0:T(8,128)S(1)} %get-tuple-element.22), channel_id=1, source_target_pairs={{0,1},{1,2},{2,3},{3,0},{4,5},{5,6},{6,7},{7,4},{8,9},{9,10},{10,1... | collective-permute-start | bytes 98312 | tf_op jit(solution)/shard_map/ppermute | solution.py:41
  116.5 3.8 %collective-permute-start.28 = (f32[32,256]{1,0:T(8,128)S(1)}, f32[32,256]{1,0:T(8,128)S(1)}, u32[]{:S(2)}, u32[]{:S(2)}) collective-permute-start(f32[32,256]{1,0:T(8,128)S(1)} %get-tuple-element.21), channel_id=1, source_target_pairs={{0,3},{1,0},{2,1},{3,2},{4,7},{5,4},{6,5},{7,6},{8,11},{9,8},{10,9... | collective-permute-start | bytes 98312 | tf_op jit(solution)/shard_map/ppermute | solution.py:41
  118.9 4.3 %collective-permute-start.26 = (f32[32,256]{1,0:T(8,128)S(1)}, f32[32,256]{1,0:T(8,128)S(1)}, u32[]{:S(2)}, u32[]{:S(2)}) collective-permute-start(f32[32,256]{1,0:T(8,128)S(1)} %get-tuple-element.20), channel_id=1, source_target_pairs={{0,2},{1,3},{2,0},{3,1},{4,6},{5,7},{6,4},{7,5},{8,10},{9,11},{10,... | collective-permute-start | bytes 98312 | tf_op jit(solution)/shard_map/ppermute | solution.py:41
  123.2 4.1 %collective-permute-start.30 = (f32[32,256]{1,0:T(8,128)S(1)}, f32[32,256]{1,0:T(8,128)S(1)}, u32[]{:S(2)}, u32[]{:S(2)}) collective-permute-start(f32[32,256]{1,0:T(8,128)S(1)} %add_add_fusion.3), channel_id=1, source_target_pairs={{0,16},{8,24},{16,32},{24,40},{32,48},{40,56},{48,0},{56,8},{64,80... | collective-permute-start | bytes 98312 | tf_op jit(solution)/shard_map/ppermute | solution.py:33
  123.3 3.9 %collective-permute-start.31 = (f32[32,256]{1,0:T(8,128)S(1)}, f32[32,256]{1,0:T(8,128)S(1)}, u32[]{:S(2)}, u32[]{:S(2)}) collective-permute-start(f32[32,256]{1,0:T(8,128)S(1)} %add_add_fusion.3), channel_id=1, source_target_pairs={{0,48},{8,56},{16,0},{24,8},{32,16},{40,24},{48,32},{56,40},{64,11... | collective-permute-start | bytes 98312 | tf_op jit(solution)/shard_map/ppermute | solution.py:33
  126.0 4.3 %collective-permute-start.29 = (f32[32,256]{1,0:T(8,128)S(1)}, f32[32,256]{1,0:T(8,128)S(1)}, u32[]{:S(2)}, u32[]{:S(2)}) collective-permute-start(f32[32,256]{1,0:T(8,128)S(1)} %add_add_fusion.3), channel_id=1, source_target_pairs={{0,32},{8,40},{16,48},{24,56},{32,0},{40,8},{48,16},{56,24},{64,96... | collective-permute-start | bytes 98312 | tf_op jit(solution)/shard_map/ppermute | solution.py:33
  130.2 3.1 %collective-permute-start.32 = (f32[32,256]{1,0:T(8,128)S(1)}, f32[32,256]{1,0:T(8,128)S(1)}, u32[]{:S(2)}, u32[]{:S(2)}) collective-permute-start(f32[32,256]{1,0:T(8,128)S(1)} %add_add_fusion.2), channel_id=1, source_target_pairs={{0,4},{1,5},{2,6},{3,7},{4,0},{5,1},{6,2},{7,3},{8,12},{9,13},{10,... | collective-permute-start | bytes 98312 | tf_op jit(solution)/shard_map/ppermute | solution.py:45
  133.4 6.0 %collective-permute-start.34 = (f32[32,256]{1,0:T(8,128)S(1)}, f32[32,256]{1,0:T(8,128)S(1)}, u32[]{:S(2)}, u32[]{:S(2)}) collective-permute-start(f32[32,256]{1,0:T(8,128)S(1)} %add.124), channel_id=1, source_target_pairs={{0,64},{8,72},{16,80},{24,88},{32,96},{40,104},{48,112},{56,120},{... | collective-permute-start | bytes 98312 | tf_op jit(solution)/shard_map/ppermute | solution.py:29
  133.7 5.7 %collective-permute-start.35 = (f32[32,256]{1,0:T(8,128)S(1)}, f32[32,256]{1,0:T(8,128)S(1)}, u32[]{:S(2)}, u32[]{:S(2)}) collective-permute-start(f32[32,256]{1,0:T(8,128)S(1)} %add.124), channel_id=1, source_target_pairs={{0,192},{8,200},{16,208},{24,216},{32,224},{40,232},{48,240},{56,2... | collective-permute-start | bytes 98312 | tf_op jit(solution)/shard_map/ppermute | solution.py:29
  137.0 6.7 %collective-permute-start.33 = (f32[32,256]{1,0:T(8,128)S(1)}, f32[32,256]{1,0:T(8,128)S(1)}, u32[]{:S(2)}, u32[]{:S(2)}) collective-permute-start(f32[32,256]{1,0:T(8,128)S(1)} %add.124), channel_id=1, source_target_pairs={{0,128},{8,136},{16,144},{24,152},{32,160},{40,168},{48,176},{56,1... | collective-permute-start | bytes 98312 | tf_op jit(solution)/shard_map/ppermute | solution.py:29
  143.7 7.6 %collective-permute-start.36 = (f32[32,256]{1,0:T(8,128)S(1)}, f32[32,256]{1,0:T(8,128)S(1)}, u32[]{:S(2)}, u32[]{:S(2)}) collective-permute-start(f32[32,256]{1,0:T(8,128)S(1)} %add_add_fusion.1), channel_id=1, source_target_pairs={{0,8},{8,0},{16,24},{24,16},{32,40},{40,32},{48,56},{56,48},{64,72... | collective-permute-start | bytes 98312 | tf_op jit(solution)/shard_map/ppermute | solution.py:37
  151.3 6.8 %copy-start.5 = (f32[2,32,256]{2,1,0:T(8,128)}, f32[2,32,256]{2,1,0:T(8,128)S(1)}, u32[]{:S(2)}) copy-start(f32[2,32,256]{2,1,0:T(8,128)S(1)} %pad_maximum_fusion.2.piece0) | copy-start | bytes 196612
  151.3 3.1 %collective-permute-start.37 = (f32[2,32,256]{2,1,0:T(8,128)S(1)}, f32[2,32,256]{2,1,0:T(8,128)S(1)}, u32[]{:S(2)}, u32[]{:S(2)}) collective-permute-start(f32[2,32,256]{2,1,0:T(8,128)S(1)} %pad_maximum_fusion.2.piece0), channel_id=1, source_target_pairs={{0,3},{1,0},{2,1},{3,2},{4,7},{5,4},{6,5},{7,6},{8,11},{9,8},{10,9... | collective-permute-start | bytes 196616 | tf_op jit(solution)/shard_map/ppermute | solution.py:41
  151.4 4.7 %collective-permute-start.38 = (f32[2,32,256]{2,1,0:T(8,128)S(1)}, f32[2,32,256]{2,1,0:T(8,128)S(1)}, u32[]{:S(2)}, u32[]{:S(2)}) collective-permute-start(f32[2,32,256]{2,1,0:T(8,128)S(1)} %pad_maximum_fusion.2.piece0), channel_id=1, source_target_pairs={{0,2},{1,3},{2,0},{3,1},{4,6},{5,7},{6,4},{7,5},{8,10},{9,11},{10,... | collective-permute-start | bytes 196616 | tf_op jit(solution)/shard_map/ppermute | solution.py:41
  151.9 6.2 %collective-permute-start.39 = (f32[2,32,256]{2,1,0:T(8,128)S(1)}, f32[2,32,256]{2,1,0:T(8,128)S(1)}, u32[]{:S(2)}, u32[]{:S(2)}) collective-permute-start(f32[2,32,256]{2,1,0:T(8,128)S(1)} %pad_maximum_fusion.2.piece0), channel_id=1, source_target_pairs={{0,1},{1,2},{2,3},{3,0},{4,5},{5,6},{6,7},{7,4},{8,9},{9,10},{10,1... | collective-permute-start | bytes 196616 | tf_op jit(solution)/shard_map/ppermute | solution.py:41
  (11 other events, 25.4 us)
where the time goes:
time: 174 us
  waiting for transfers between devices  75.9 us (44%)
  starting transfers between devices  63.5 us (36%)
  Pallas kernels  25.6 us (15%)
  other arithmetic  3.76 us (2%)
  local copies, waits for them, and re-layouts  3.01 us (2%)
    ppermute x9, waiting for transfers between devices, to_x(): return lax.ppermute(v, 'row', row_pairs(lambda z, x, c: (z, x + k, c)))  31.7 us
    ppermute x9, starting transfers between devices, to_z(): return lax.ppermute(v, 'row', row_pairs(lambda z, x, c: (z + k, x, c)))  22.5 us
    ppermute x12, waiting for transfers between devices, to_y(): lax.ppermute(v, 'col', [(col_at(zl, y), col_at(zl, y + k)) for zl in rang...  21.2 us
    ppermute x9, waiting for transfers between devices, to_z(): return lax.ppermute(v, 'row', row_pairs(lambda z, x, c: (z + k, x, c)))  16.5 us
    pallas_call x1, Pallas kernels, factor_and_basis(): pl.pallas_call(factor_kernel, out_shape=(jax.ShapeDtypeStruct((edge, size...  15 us
    ppermute x9, starting transfers between devices, to_x(): return lax.ppermute(v, 'row', row_pairs(lambda z, x, c: (z, x + k, c)))  13.9 us
    ppermute x7, starting transfers between devices, to_core(): return lax.ppermute(v, 'row', row_pairs(lambda z, x, c: (z, x, 1 - c)))  12.6 us
    ppermute x12, starting transfers between devices, to_y(): lax.ppermute(v, 'col', [(col_at(zl, y), col_at(zl, y + k)) for zl in rang...  11.6 us
  transfers between devices with their start and end apart: 40, of which 26 were waited for; matrix products, arithmetic and copies ran while one was open for 2% of the time, Pallas kernels for 3%

commit v1 on v0

--- a/solution.py
+++ b/solution.py
@@ -77,14 +77,12 @@
 
 
 def mirror_kernel(place, counts, rows, cols, blocks, *refs):
-    pieces, outs, vectors, acc = refs[:N_Y], refs[N_Y : N_Y + N_CORE], refs[-2], refs[-1]
+    vectors, outs, acc = refs[0], refs[1 : 1 + N_CORE], refs[-1]
     acc[...] = jnp.zeros_like(acc)
-    for k, piece in enumerate(pieces):
-        vectors[k * N_ZL : (k + 1) * N_ZL] = piece[...]
 
     def add(tile, rp, cp):
         acc[col_spot(place, cp)] += lax.dot_general(
-            tile, vectors[row_spot(place, rp)], (((0,), (0,)), ((), ())), preferred_element_type=F32
+            tile, vectors[rp], (((0,), (0,)), ((), ())), preferred_element_type=F32
         )
 
     slot_loop(counts, rows, cols, blocks, add)
@@ -234,11 +232,12 @@
 
 
 def body(blocks, block_rows, block_cols, counts, trials):
+    edge, width = trials.shape
     place = jnp.stack([lax.axis_index("row"), lax.axis_index("col")]).astype(jnp.int32)
     scalars = (place, counts, block_rows, block_cols)
-    first = jnp.stack([trials, to_zl(trials)])
     zs = jnp.stack([trials] + [to_z(trials, -k) for k in range(1, N_ZH)])
-    row_pieces = [first] + [to_y(first, -k) for k in range(1, N_Y)]
+    copies = jnp.broadcast_to(trials[None], (N_COL, edge, width))
+    row_pieces = [lax.all_to_all(copies, "col", 0, 0, tiled=True)]
     col_pieces = [zs] + [to_x(zs, -k) for k in range(1, N_X)]
     col_keep, col_send = products_of(mirror_kernel, scalars, blocks[0], row_pieces, N_CORE, N_X * N_ZH)
     col_pieces = col_pieces + [to_core(v) for v in col_pieces]

time: 174 us -> 174 us (level)
  the two profiles are of different devices: /device:TPU:1 before, /device:TPU:2 now
where the time goes in v1:
time: 174 us; the launch traced here: 172 us
  waiting for transfers between devices  69.6 us (40%)
  starting transfers between devices  66.7 us (38%)
  Pallas kernels  26 us (15%)
  local copies, waits for them, and re-layouts  4.62 us (3%)
  other arithmetic  2.87 us (2%)
    ppermute x9, waiting for transfers between devices, to_x(): return lax.ppermute(v, 'row', row_pairs(lambda z, x, c: (z, x + k, c)))  28 us
    ppermute x9, starting transfers between devices, to_z(): return lax.ppermute(v, 'row', row_pairs(lambda z, x, c: (z + k, x, c)))  26.5 us
    ppermute x9, starting transfers between devices, to_x(): return lax.ppermute(v, 'row', row_pairs(lambda z, x, c: (z, x + k, c)))  21 us
    ppermute x9, waiting for transfers between devices, to_z(): return lax.ppermute(v, 'row', row_pairs(lambda z, x, c: (z + k, x, c)))  17.2 us
    pallas_call x1, Pallas kernels, factor_and_basis(): pl.pallas_call(factor_kernel, out_shape=(jax.ShapeDtypeStruct((edge, size...  15 us
    ppermute x9, starting transfers between devices, to_y(): lax.ppermute(v, 'col', [(col_at(zl, y), col_at(zl, y + k)) for zl in rang...  11.8 us
    pallas_call x2, Pallas kernels, products_of(): pl.pallas_call(kernel, out_shape=(jax.ShapeDtypeStruct((out_blocks, edge,...  11 us
    ppermute x9, waiting for transfers between devices, to_y(): lax.ppermute(v, 'col', [(col_at(zl, y), col_at(zl, y + k)) for zl in rang...  10.2 us
  transfers between devices with their start and end apart: 37, of which 26 were waited for; matrix products, arithmetic and copies ran while one was open for 2% of the time, Pallas kernels for 3%

profile of v1, /device:TPU:2, one launch (start us, length us, event | category | flops | bytes accessed | tf_op | source)
XLA Modules:
  0.0 171.8 jit_solution(9219600517081454105)
XLA Ops:
  0.6 1.7 %broadcast_in_dim.2 = bf16[8,128,256]{2,1,0:T(8,128)(2,1)} broadcast(bf16[128,256]{1,0:T(8,128)(2,1)} %param.9), dimensions={1,2} | broadcast | bytes 589824 | tf_op jit(solution)/shard_map/broadcast_in_dim | solution.py:239
  2.4 5.8 %all-to-all-start = ((bf16[8,128,256]{2,1,0:T(8,128)(2,1)}), bf16[8,128,256]{2,1,0:T(8,128)(2,1)S(1)}, u32[]{:S(2)}, u32[]{:S(2)}) async-start(bf16[8,128,256]{2,1,0:T(8,128)(2,1)} %broadcast_in_dim.2), calls=%async_computation | async-start | bytes 1048576 | tf_op jit(solution)/shard_map/all_to_all | solution.py:240
  9.5 8.3 %all-to-all-done.refs_0_ = bf16[8,128,256]{2,1,0:T(8,128)(2,1)S(1)} async-done(((bf16[8,128,256]{2,1,0:T(8,128)(2,1)}), bf16[8,128,256]{2,1,0:T(8,128)(2,1)S(1)}, u32[]{:S(2)}, u32[]{:S(2)}) %all-to-all-start) | async-done | bytes 524320 | tf_op jit(solution)/shard_map/all_to_all | solution.py:240
  18.5 6.0 %shard_map.69 = (f32[16,128,256]{2,1,0:T(8,128)}, f32[16,128,256]{2,1,0:T(8,128)}) custom-call(s32[2]{0:T(128)} %pad_add_fusion.place, s32[1,1]{1,0:T(1,128)S(6)} %copy.7.counts, s32[1,64]{1,0:T(1,128)} %rows.3, s32[1,64]{1,0:T(1,128)} %cols.3, bf16[64,128,128]{2,1,0:T(8,128)(2,1)} %bitcast.33, bf16[8,128,256]{2,1,0:T(8,128)(2,1)} %copy-done.2), custom_call_target="tpu_custom_call" | custom-call | flops 536870912 | bytes 6815744 | tf_op jit(solution)/shard_map/pallas_call | solution.py:113
  24.5 2.8 %collective-permute-start.2 = (bf16[128,256]{1,0:T(8,128)(2,1)S(1)}, bf16[128,256]{1,0:T(8,128)(2,1)S(1)}, u32[]{:S(2)}, u32[]{:S(2)}) collective-permute-start(bf16[128,256]{1,0:T(8,128)(2,1)S(1)} %copy-done.6), channel_id=1, source_target_pairs={{0,64},{8,72},{16,80},{24,88},{32,96},{40,104},{48,112},{56,120},{... | collective-permute-start | bytes 196616 | tf_op jit(solution)/shard_map/ppermute | solution.py:29
  27.3 3.7 %collective-permute-start.1 = (bf16[128,256]{1,0:T(8,128)(2,1)S(1)}, bf16[128,256]{1,0:T(8,128)(2,1)S(1)}, u32[]{:S(2)}, u32[]{:S(2)}) collective-permute-start(bf16[128,256]{1,0:T(8,128)(2,1)S(1)} %copy-done.6), channel_id=1, source_target_pairs={{0,128},{8,136},{16,144},{24,152},{32,160},{40,168},{48,176},{56,1... | collective-permute-start | bytes 196616 | tf_op jit(solution)/shard_map/ppermute | solution.py:29
  31.0 3.2 %collective-permute-start = (bf16[128,256]{1,0:T(8,128)(2,1)S(1)}, bf16[128,256]{1,0:T(8,128)(2,1)S(1)}, u32[]{:S(2)}, u32[]{:S(2)}) collective-permute-start(bf16[128,256]{1,0:T(8,128)(2,1)S(1)} %copy-done.6), channel_id=1, source_target_pairs={{0,192},{8,200},{16,208},{24,216},{32,224},{40,232},{48,240},{56,2... | collective-permute-start | bytes 196616 | tf_op jit(solution)/shard_map/ppermute | solution.py:29
  34.2 2.7 %collective-permute-done.1 = bf16[128,256]{1,0:T(8,128)(2,1)S(1)} collective-permute-done((bf16[128,256]{1,0:T(8,128)(2,1)S(1)}, bf16[128,256]{1,0:T(8,128)(2,1)S(1)}, u32[]{:S(2)}, u32[]{:S(2)}) %collective-permute-start.1) | collective-permute-done | bytes 65568 | tf_op jit(solution)/shard_map/ppermute | solution.py:29
  37.0 0.9 collective-permute-done
  38.0 1.2 collective-permute-start.3
  39.2 2.5 %collective-permute-start.4 = (bf16[4,128,256]{2,1,0:T(8,128)(2,1)S(1)}, bf16[4,128,256]{2,1,0:T(8,128)(2,1)S(1)}, u32[]{:S(2)}, u32[]{:S(2)}) collective-permute-start(bf16[4,128,256]{2,1,0:T(8,128)(2,1)S(1)} %pad_maximum_fusion.refs_0_), channel_id=1, source_target_pairs={{0,32},{8,40},{16,48},{24,56},{32,0},{40,8},{48,16},{56,24},{64,96... | collective-permute-start | bytes 786440 | tf_op jit(solution)/shard_map/ppermute | solution.py:33
  41.7 2.5 %collective-permute-start.5 = (bf16[4,128,256]{2,1,0:T(8,128)(2,1)S(1)}, bf16[4,128,256]{2,1,0:T(8,128)(2,1)S(1)}, u32[]{:S(2)}, u32[]{:S(2)}) collective-permute-start(bf16[4,128,256]{2,1,0:T(8,128)(2,1)S(1)} %pad_maximum_fusion.refs_0_), channel_id=1, source_target_pairs={{0,16},{8,24},{16,32},{24,40},{32,48},{40,56},{48,0},{56,8},{64,80... | collective-permute-start | bytes 786440 | tf_op jit(solution)/shard_map/ppermute | solution.py:33
  44.2 1.3 collective-permute-done.3.refs_1_
  45.5 8.0 %collective-permute-done.4.refs_2_ = bf16[4,128,256]{2,1,0:T(8,128)(2,1)S(1)} collective-permute-done((bf16[4,128,256]{2,1,0:T(8,128)(2,1)S(1)}, bf16[4,128,256]{2,1,0:T(8,128)(2,1)S(1)}, u32[]{:S(2)}, u32[]{:S(2)}) %collective-permute-start.4) | collective-permute-done | bytes 262176 | tf_op jit(solution)/shard_map/ppermute | solution.py:33
  56.2 5.0 %shard_map.68 = (f32[2,128,256]{2,1,0:T(8,128)}, f32[2,128,256]{2,1,0:T(8,128)}, f32[2,128,256]{2,1,0:T(8,128)}, f32[2,128,256]{2,1,0:T(8,128)}) custom-call(s32[2]{0:T(128)} %pad_add_fusion.place, s32[1,1]{1,0:T(1,128)S(6)} %copy.7.counts, s32[1,64]{1,0:T(1,128)} %rows.3, s32[1,64]{1,0:T(1,128)} %cols.3, bf16[64,128,128]{2,1,0:T(8,128)(2,1)} %bitcast.34, ...), custom_call_target="tpu_custom_call" | custom-call | flops 536870912 | bytes 5242880 | tf_op jit(solution)/shard_map/pallas_call | solution.py:113
  61.3 1.8 %collective-permute-start.11 = (f32[2,128,256]{2,1,0:T(8,128)}, f32[2,128,256]{2,1,0:T(8,128)S(1)}, u32[]{:S(2)}, u32[]{:S(2)}) collective-permute-start(f32[2,128,256]{2,1,0:T(8,128)} %get-tuple-element.10), channel_id=1, source_target_pairs={{0,1},{1,2},{2,3},{3,0},{4,5},{5,6},{6,7},{7,4},{8,9},{9,10},{10,1... | collective-permute-start | bytes 786440 | tf_op jit(solution)/shard_map/ppermute | solution.py:41
  63.1 1.4 collective-permute-start.12
  64.5 1.9 %collective-permute-start.10 = (f32[2,128,256]{2,1,0:T(8,128)}, f32[2,128,256]{2,1,0:T(8,128)S(1)}, u32[]{:S(2)}, u32[]{:S(2)}) collective-permute-start(f32[2,128,256]{2,1,0:T(8,128)} %get-tuple-element.9), channel_id=1, source_target_pairs={{0,2},{1,3},{2,0},{3,1},{4,6},{5,7},{6,4},{7,5},{8,10},{9,11},{10,... | collective-permute-start | bytes 786440 | tf_op jit(solution)/shard_map/ppermute | solution.py:41
  66.4 1.9 %add.100 = f32[16,128,256]{2,1,0:T(8,128)S(1)} add(f32[16,128,256]{2,1,0:T(8,128)S(1)} %copy-done, f32[16,128,256]{2,1,0:T(8,128)} %collective-permute-done.14) | non-fusion elementwise | flops 524288 | bytes 6291456 | tf_op jit(solution)/shard_map/add | solution.py:245
  68.5 1.7 %collective-permute-start.15 = (f32[4,128,256]{2,1,0:T(8,128)S(1)}, f32[4,128,256]{2,1,0:T(8,128)S(1)}, u32[]{:S(2)}, u32[]{:S(2)}) collective-permute-start(f32[4,128,256]{2,1,0:T(8,128)S(1)} %get-tuple-element.16), channel_id=1, source_target_pairs={{0,32},{8,40},{16,48},{24,56},{32,0},{40,8},{48,16},{56,24},{64,96... | collective-permute-start | bytes 1572872 | tf_op jit(solution)/shard_map/ppermute | solution.py:33
  70.2 1.4 collective-permute-start.16
  71.7 7.9 %collective-permute-start.17 = (f32[4,128,256]{2,1,0:T(8,128)S(1)}, f32[4,128,256]{2,1,0:T(8,128)S(1)}, u32[]{:S(2)}, u32[]{:S(2)}) collective-permute-start(f32[4,128,256]{2,1,0:T(8,128)S(1)} %get-tuple-element.14), channel_id=1, source_target_pairs={{0,48},{8,56},{16,0},{24,8},{32,16},{40,24},{48,32},{56,40},{64,11... | collective-permute-start | bytes 1572872 | tf_op jit(solution)/shard_map/ppermute | solution.py:33
  79.7 5.1 %collective-permute-done.15 = f32[4,128,256]{2,1,0:T(8,128)S(1)} collective-permute-done((f32[4,128,256]{2,1,0:T(8,128)S(1)}, f32[4,128,256]{2,1,0:T(8,128)S(1)}, u32[]{:S(2)}, u32[]{:S(2)}) %collective-permute-start.15) | collective-permute-done | bytes 524320 | tf_op jit(solution)/shard_map/ppermute | solution.py:33
  84.8 8.7 %collective-permute-done.16 = f32[4,128,256]{2,1,0:T(8,128)S(1)} collective-permute-done((f32[4,128,256]{2,1,0:T(8,128)S(1)}, f32[4,128,256]{2,1,0:T(8,128)S(1)}, u32[]{:S(2)}, u32[]{:S(2)}) %collective-permute-start.16) | collective-permute-done | bytes 524320 | tf_op jit(solution)/shard_map/ppermute | solution.py:33
  93.9 4.7 %collective-permute-start.18 = (f32[128,256]{1,0:T(8,128)S(1)}, f32[128,256]{1,0:T(8,128)S(1)}, u32[]{:S(2)}, u32[]{:S(2)}) collective-permute-start(f32[128,256]{1,0:T(8,128)S(1)} %get-tuple-element.19), channel_id=1, source_target_pairs={{0,128},{8,136},{16,144},{24,152},{32,160},{40,168},{48,176},{56,1... | collective-permute-start | bytes 393224 | tf_op jit(solution)/shard_map/ppermute | solution.py:29
  98.6 2.4 %collective-permute-start.19 = (f32[128,256]{1,0:T(8,128)S(1)}, f32[128,256]{1,0:T(8,128)S(1)}, u32[]{:S(2)}, u32[]{:S(2)}) collective-permute-start(f32[128,256]{1,0:T(8,128)S(1)} %get-tuple-element.18), channel_id=1, source_target_pairs={{0,64},{8,72},{16,80},{24,88},{32,96},{40,104},{48,112},{56,120},{... | collective-permute-start | bytes 393224 | tf_op jit(solution)/shard_map/ppermute | solution.py:29
  100.9 1.8 %collective-permute-start.20 = (f32[128,256]{1,0:T(8,128)S(1)}, f32[128,256]{1,0:T(8,128)S(1)}, u32[]{:S(2)}, u32[]{:S(2)}) collective-permute-start(f32[128,256]{1,0:T(8,128)S(1)} %get-tuple-element.17), channel_id=1, source_target_pairs={{0,192},{8,200},{16,208},{24,216},{32,224},{40,232},{48,240},{56,2... | collective-permute-start | bytes 393224 | tf_op jit(solution)/shard_map/ppermute | solution.py:29
  103.4 7.0 %collective-permute-done.19 = f32[128,256]{1,0:T(8,128)S(1)} collective-permute-done((f32[128,256]{1,0:T(8,128)S(1)}, f32[128,256]{1,0:T(8,128)S(1)}, u32[]{:S(2)}, u32[]{:S(2)}) %collective-permute-start.19) | collective-permute-done | bytes 131104 | tf_op jit(solution)/shard_map/ppermute | solution.py:29
  110.3 1.9 %collective-permute-done.20 = f32[128,256]{1,0:T(8,128)S(1)} collective-permute-done((f32[128,256]{1,0:T(8,128)S(1)}, f32[128,256]{1,0:T(8,128)S(1)}, u32[]{:S(2)}, u32[]{:S(2)}) %collective-permute-start.20) | collective-permute-done | bytes 131104 | tf_op jit(solution)/shard_map/ppermute | solution.py:29
  112.9 1.3 collective-permute-done.21
  114.2 1.1 collective-permute-start.23
  115.3 2.2 %collective-permute-start.24 = (f32[32,256]{1,0:T(8,128)S(1)}, f32[32,256]{1,0:T(8,128)S(1)}, u32[]{:S(2)}, u32[]{:S(2)}) collective-permute-start(f32[32,256]{1,0:T(8,128)S(1)} %get-tuple-element.21), channel_id=1, source_target_pairs={{0,3},{1,0},{2,1},{3,2},{4,7},{5,4},{6,5},{7,6},{8,11},{9,8},{10,9... | collective-permute-start | bytes 98312 | tf_op jit(solution)/shard_map/ppermute | solution.py:41
  118.4 1.1 collective-permute-done.23
  119.4 3.5 %collective-permute-done.22 = f32[32,256]{1,0:T(8,128)S(1)} collective-permute-done((f32[32,256]{1,0:T(8,128)S(1)}, f32[32,256]{1,0:T(8,128)S(1)}, u32[]{:S(2)}, u32[]{:S(2)}) %collective-permute-start.22) | collective-permute-done | bytes 32800 | tf_op jit(solution)/shard_map/ppermute | solution.py:41
  123.2 1.9 %collective-permute-start.27 = (f32[32,256]{1,0:T(8,128)S(1)}, f32[32,256]{1,0:T(8,128)S(1)}, u32[]{:S(2)}, u32[]{:S(2)}) collective-permute-start(f32[32,256]{1,0:T(8,128)S(1)} %add_add_fusion.3), channel_id=1, source_target_pairs={{0,48},{8,56},{16,0},{24,8},{32,16},{40,24},{48,32},{56,40},{64,11... | collective-permute-start | bytes 98312 | tf_op jit(solution)/shard_map/ppermute | solution.py:33
  125.1 1.6 collective-permute-start.25
  127.1 3.4 %collective-permute-done.25 = f32[32,256]{1,0:T(8,128)S(1)} collective-permute-done((f32[32,256]{1,0:T(8,128)S(1)}, f32[32,256]{1,0:T(8,128)S(1)}, u32[]{:S(2)}, u32[]{:S(2)}) %collective-permute-start.25) | collective-permute-done | bytes 32800 | tf_op jit(solution)/shard_map/ppermute | solution.py:33
  130.5 1.3 collective-permute-start.28
  131.8 2.7 %collective-permute-done.28 = f32[32,256]{1,0:T(8,128)S(1)} collective-permute-done((f32[32,256]{1,0:T(8,128)S(1)}, f32[32,256]{1,0:T(8,128)S(1)}, u32[]{:S(2)}, u32[]{:S(2)}) %collective-permute-start.28) | collective-permute-done | bytes 32800 | tf_op jit(solution)/shard_map/ppermute | solution.py:45
  134.5 1.8 %collective-permute-start.30 = (f32[32,256]{1,0:T(8,128)S(1)}, f32[32,256]{1,0:T(8,128)S(1)}, u32[]{:S(2)}, u32[]{:S(2)}) collective-permute-start(f32[32,256]{1,0:T(8,128)S(1)} %add.124), channel_id=1, source_target_pairs={{0,64},{8,72},{16,80},{24,88},{32,96},{40,104},{48,112},{56,120},{... | collective-permute-start | bytes 98312 | tf_op jit(solution)/shard_map/ppermute | solution.py:29
  136.3 2.3 %collective-permute-start.31 = (f32[32,256]{1,0:T(8,128)S(1)}, f32[32,256]{1,0:T(8,128)S(1)}, u32[]{:S(2)}, u32[]{:S(2)}) collective-permute-start(f32[32,256]{1,0:T(8,128)S(1)} %add.124), channel_id=1, source_target_pairs={{0,192},{8,200},{16,208},{24,216},{32,224},{40,232},{48,240},{56,2... | collective-permute-start | bytes 98312 | tf_op jit(solution)/shard_map/ppermute | solution.py:29
  138.7 3.8 %collective-permute-start.29 = (f32[32,256]{1,0:T(8,128)S(1)}, f32[32,256]{1,0:T(8,128)S(1)}, u32[]{:S(2)}, u32[]{:S(2)}) collective-permute-start(f32[32,256]{1,0:T(8,128)S(1)} %add.124), channel_id=1, source_target_pairs={{0,128},{8,136},{16,144},{24,152},{32,160},{40,168},{48,176},{56,1... | collective-permute-start | bytes 98312 | tf_op jit(solution)/shard_map/ppermute | solution.py:29
  142.5 4.0 %collective-permute-done.29 = f32[32,256]{1,0:T(8,128)S(1)} collective-permute-done((f32[32,256]{1,0:T(8,128)S(1)}, f32[32,256]{1,0:T(8,128)S(1)}, u32[]{:S(2)}, u32[]{:S(2)}) %collective-permute-start.29) | collective-permute-done | bytes 32800 | tf_op jit(solution)/shard_map/ppermute | solution.py:29
  146.6 1.2 collective-permute-done.32
  147.8 1.4 collective-permute-start.33
  150.3 2.6 %collective-permute-done.33.piece1 = f32[2,32,256]{2,1,0:T(8,128)S(1)} collective-permute-done((f32[2,32,256]{2,1,0:T(8,128)S(1)}, f32[2,32,256]{2,1,0:T(8,128)S(1)}, u32[]{:S(2)}, u32[]{:S(2)}) %collective-permute-start.33) | collective-permute-done | bytes 65568 | tf_op jit(solution)/shard_map/ppermute | solution.py:41
  152.9 2.7 %collective-permute-done.34.piece2 = f32[2,32,256]{2,1,0:T(8,128)S(1)} collective-permute-done((f32[2,32,256]{2,1,0:T(8,128)S(1)}, f32[2,32,256]{2,1,0:T(8,128)S(1)}, u32[]{:S(2)}, u32[]{:S(2)}) %collective-permute-start.34) | collective-permute-done | bytes 65568 | tf_op jit(solution)/shard_map/ppermute | solution.py:41
  156.8 15.0 %factor.1 = (f32[128,256]{1,0:T(8,128)}, f32[256,256]{1,0:T(8,128)}) custom-call(s32[2]{0:T(128)} %pad_add_fusion.place, f32[2,32,256]{2,1,0:T(8,128)} %copy-done.5, f32[2,32,256]{2,1,0:T(8,128)} %copy-done.13, f32[2,32,256]{2,1,0:T(8,128)} %copy-done.14, f32[2,32,256]{2,1,0:T(8,128)} %copy-done.15, f32[128,256]{1,0:T(8,128)} %copy-done.1), custom_call_target="tpu_custom_call" | custom-call | tf_op jit(solution)/shard_map/factor/pallas_call | solution.py:207
  (80 shorter events, 10.0 us)
Async XLA Ops:
  0.6 23.9 %copy-start.6 = (bf16[128,256]{1,0:T(8,128)(2,1)S(1)}, bf16[128,256]{1,0:T(8,128)(2,1)}, u32[]{:S(2)}) copy-start(bf16[128,256]{1,0:T(8,128)(2,1)} %param.9) | copy-start | bytes 196612
  2.4 15.4 %all-to-all-start = ((bf16[8,128,256]{2,1,0:T(8,128)(2,1)}), bf16[8,128,256]{2,1,0:T(8,128)(2,1)S(1)}, u32[]{:S(2)}, u32[]{:S(2)}) async-start(bf16[8,128,256]{2,1,0:T(8,128)(2,1)} %broadcast_in_dim.2), calls=%async_computation | async-start | bytes 1048576 | tf_op jit(solution)/shard_map/all_to_all | solution.py:240
  24.5 41.9 %collective-permute-start.14 = (f32[16,128,256]{2,1,0:T(8,128)}, f32[16,128,256]{2,1,0:T(8,128)}, u32[]{:S(2)}, u32[]{:S(2)}) collective-permute-start(f32[16,128,256]{2,1,0:T(8,128)} %get-tuple-element.13), channel_id=1, source_target_pairs={{0,8},{8,0},{16,24},{24,16},{32,40},{40,32},{48,56},{56,48},{64,72... | collective-permute-start | bytes 6291464 | tf_op jit(solution)/shard_map/ppermute | solution.py:37
  24.5 9.7 %collective-permute-start.2 = (bf16[128,256]{1,0:T(8,128)(2,1)S(1)}, bf16[128,256]{1,0:T(8,128)(2,1)S(1)}, u32[]{:S(2)}, u32[]{:S(2)}) collective-permute-start(bf16[128,256]{1,0:T(8,128)(2,1)S(1)} %copy-done.6), channel_id=1, source_target_pairs={{0,64},{8,72},{16,80},{24,88},{32,96},{40,104},{48,112},{56,120},{... | collective-permute-start | bytes 196616 | tf_op jit(solution)/shard_map/ppermute | solution.py:29
  27.3 9.6 %collective-permute-start.1 = (bf16[128,256]{1,0:T(8,128)(2,1)S(1)}, bf16[128,256]{1,0:T(8,128)(2,1)S(1)}, u32[]{:S(2)}, u32[]{:S(2)}) collective-permute-start(bf16[128,256]{1,0:T(8,128)(2,1)S(1)} %copy-done.6), channel_id=1, source_target_pairs={{0,128},{8,136},{16,144},{24,152},{32,160},{40,168},{48,176},{56,1... | collective-permute-start | bytes 196616 | tf_op jit(solution)/shard_map/ppermute | solution.py:29
  31.0 6.9 %collective-permute-start = (bf16[128,256]{1,0:T(8,128)(2,1)S(1)}, bf16[128,256]{1,0:T(8,128)(2,1)S(1)}, u32[]{:S(2)}, u32[]{:S(2)}) collective-permute-start(bf16[128,256]{1,0:T(8,128)(2,1)S(1)} %copy-done.6), channel_id=1, source_target_pairs={{0,192},{8,200},{16,208},{24,216},{32,224},{40,232},{48,240},{56,2... | collective-permute-start | bytes 196616 | tf_op jit(solution)/shard_map/ppermute | solution.py:29
  37.9 18.2 %copy-start.3 = (bf16[4,128,256]{2,1,0:T(8,128)(2,1)}, bf16[4,128,256]{2,1,0:T(8,128)(2,1)S(1)}, u32[]{:S(2)}) copy-start(bf16[4,128,256]{2,1,0:T(8,128)(2,1)S(1)} %pad_maximum_fusion.refs_0_) | copy-start | bytes 786436
  38.0 28.4 %copy-start = (f32[16,128,256]{2,1,0:T(8,128)S(1)}, f32[16,128,256]{2,1,0:T(8,128)}, u32[]{:S(2)}) copy-start(f32[16,128,256]{2,1,0:T(8,128)} %get-tuple-element.12) | copy-start | bytes 6291460
  38.0 7.6 %collective-permute-start.3 = (bf16[4,128,256]{2,1,0:T(8,128)(2,1)S(1)}, bf16[4,128,256]{2,1,0:T(8,128)(2,1)S(1)}, u32[]{:S(2)}, u32[]{:S(2)}) collective-permute-start(bf16[4,128,256]{2,1,0:T(8,128)(2,1)S(1)} %pad_maximum_fusion.refs_0_), channel_id=1, source_target_pairs={{0,48},{8,56},{16,0},{24,8},{32,16},{40,24},{48,32},{56,40},{64,11... | collective-permute-start | bytes 786440 | tf_op jit(solution)/shard_map/ppermute | solution.py:33
  39.2 14.4 %collective-permute-start.4 = (bf16[4,128,256]{2,1,0:T(8,128)(2,1)S(1)}, bf16[4,128,256]{2,1,0:T(8,128)(2,1)S(1)}, u32[]{:S(2)}, u32[]{:S(2)}) collective-permute-start(bf16[4,128,256]{2,1,0:T(8,128)(2,1)S(1)} %pad_maximum_fusion.refs_0_), channel_id=1, source_target_pairs={{0,32},{8,40},{16,48},{24,56},{32,0},{40,8},{48,16},{56,24},{64,96... | collective-permute-start | bytes 786440 | tf_op jit(solution)/shard_map/ppermute | solution.py:33
  41.7 12.8 %collective-permute-start.5 = (bf16[4,128,256]{2,1,0:T(8,128)(2,1)S(1)}, bf16[4,128,256]{2,1,0:T(8,128)(2,1)S(1)}, u32[]{:S(2)}, u32[]{:S(2)}) collective-permute-start(bf16[4,128,256]{2,1,0:T(8,128)(2,1)S(1)} %pad_maximum_fusion.refs_0_), channel_id=1, source_target_pairs={{0,16},{8,24},{16,32},{24,40},{32,48},{40,56},{48,0},{56,8},{64,80... | collective-permute-start | bytes 786440 | tf_op jit(solution)/shard_map/ppermute | solution.py:33
  44.2 10.3 %collective-permute-start.6 = (bf16[4,128,256]{2,1,0:T(8,128)(2,1)S(1)}, bf16[4,128,256]{2,1,0:T(8,128)(2,1)S(1)}, u32[]{:S(2)}, u32[]{:S(2)}) collective-permute-start(bf16[4,128,256]{2,1,0:T(8,128)(2,1)S(1)} %pad_maximum_fusion.refs_0_), channel_id=1, source_target_pairs={{0,8},{8,0},{16,24},{24,16},{32,40},{40,32},{48,56},{56,48},{64,72... | collective-permute-start | bytes 786440 | tf_op jit(solution)/shard_map/ppermute | solution.py:37
  45.5 10.6 %copy-start.7 = (bf16[4,128,256]{2,1,0:T(8,128)(2,1)}, bf16[4,128,256]{2,1,0:T(8,128)(2,1)S(1)}, u32[]{:S(2)}) copy-start(bf16[4,128,256]{2,1,0:T(8,128)(2,1)S(1)} %collective-permute-done.3.refs_1_) | copy-start | bytes 786436
  45.5 9.0 %collective-permute-start.7 = (bf16[4,128,256]{2,1,0:T(8,128)(2,1)S(1)}, bf16[4,128,256]{2,1,0:T(8,128)(2,1)S(1)}, u32[]{:S(2)}, u32[]{:S(2)}) collective-permute-start(bf16[4,128,256]{2,1,0:T(8,128)(2,1)S(1)} %collective-permute-done.3.refs_1_), channel_id=1, source_target_pairs={{0,8},{8,0},{16,24},{24,16},{32,40},{40,32},{48,56},{56,48},{64,72... | collective-permute-start | bytes 786440 | tf_op jit(solution)/shard_map/ppermute | solution.py:37
  53.6 2.6 %copy-start.8 = (bf16[4,128,256]{2,1,0:T(8,128)(2,1)}, bf16[4,128,256]{2,1,0:T(8,128)(2,1)S(1)}, u32[]{:S(2)}) copy-start(bf16[4,128,256]{2,1,0:T(8,128)(2,1)S(1)} %collective-permute-done.4.refs_2_) | copy-start | bytes 786436
  53.6 1.5 collective-permute-start.8
  54.5 1.7 copy-start.9
  54.5 1.7 collective-permute-start.9
  54.5 1.7 copy-start.10
  61.3 10.4 %collective-permute-start.11 = (f32[2,128,256]{2,1,0:T(8,128)}, f32[2,128,256]{2,1,0:T(8,128)S(1)}, u32[]{:S(2)}, u32[]{:S(2)}) collective-permute-start(f32[2,128,256]{2,1,0:T(8,128)} %get-tuple-element.10), channel_id=1, source_target_pairs={{0,1},{1,2},{2,3},{3,0},{4,5},{5,6},{6,7},{7,4},{8,9},{9,10},{10,1... | collective-permute-start | bytes 786440 | tf_op jit(solution)/shard_map/ppermute | solution.py:41
  63.1 16.4 %collective-permute-start.12 = (f32[2,128,256]{2,1,0:T(8,128)}, f32[2,128,256]{2,1,0:T(8,128)S(1)}, u32[]{:S(2)}, u32[]{:S(2)}) collective-permute-start(f32[2,128,256]{2,1,0:T(8,128)} %get-tuple-element.11), channel_id=1, source_target_pairs={{0,3},{1,0},{2,1},{3,2},{4,7},{5,4},{6,5},{7,6},{8,11},{9,8},{10,9... | collective-permute-start | bytes 786440 | tf_op jit(solution)/shard_map/ppermute | solution.py:41
  64.5 15.0 %collective-permute-start.10 = (f32[2,128,256]{2,1,0:T(8,128)}, f32[2,128,256]{2,1,0:T(8,128)S(1)}, u32[]{:S(2)}, u32[]{:S(2)}) collective-permute-start(f32[2,128,256]{2,1,0:T(8,128)} %get-tuple-element.9), channel_id=1, source_target_pairs={{0,2},{1,3},{2,0},{3,1},{4,6},{5,7},{6,4},{7,5},{8,10},{9,11},{10,... | collective-permute-start | bytes 786440 | tf_op jit(solution)/shard_map/ppermute | solution.py:41
  68.3 11.2 %copy-start.4 = (f32[2,128,256]{2,1,0:T(8,128)S(1)}, f32[2,128,256]{2,1,0:T(8,128)}, u32[]{:S(2)}) copy-start(f32[2,128,256]{2,1,0:T(8,128)} %get-tuple-element.8) | copy-start | bytes 786436
  68.5 16.4 %collective-permute-start.15 = (f32[4,128,256]{2,1,0:T(8,128)S(1)}, f32[4,128,256]{2,1,0:T(8,128)S(1)}, u32[]{:S(2)}, u32[]{:S(2)}) collective-permute-start(f32[4,128,256]{2,1,0:T(8,128)S(1)} %get-tuple-element.16), channel_id=1, source_target_pairs={{0,32},{8,40},{16,48},{24,56},{32,0},{40,8},{48,16},{56,24},{64,96... | collective-permute-start | bytes 1572872 | tf_op jit(solution)/shard_map/ppermute | solution.py:33
  70.2 23.3 %collective-permute-start.16 = (f32[4,128,256]{2,1,0:T(8,128)S(1)}, f32[4,128,256]{2,1,0:T(8,128)S(1)}, u32[]{:S(2)}, u32[]{:S(2)}) collective-permute-start(f32[4,128,256]{2,1,0:T(8,128)S(1)} %get-tuple-element.15), channel_id=1, source_target_pairs={{0,16},{8,24},{16,32},{24,40},{32,48},{40,56},{48,0},{56,8},{64,80... | collective-permute-start | bytes 1572872 | tf_op jit(solution)/shard_map/ppermute | solution.py:33
  71.7 22.0 %collective-permute-start.17 = (f32[4,128,256]{2,1,0:T(8,128)S(1)}, f32[4,128,256]{2,1,0:T(8,128)S(1)}, u32[]{:S(2)}, u32[]{:S(2)}) collective-permute-start(f32[4,128,256]{2,1,0:T(8,128)S(1)} %get-tuple-element.14), channel_id=1, source_target_pairs={{0,48},{8,56},{16,0},{24,8},{32,16},{40,24},{48,32},{56,40},{64,11... | collective-permute-start | bytes 1572872 | tf_op jit(solution)/shard_map/ppermute | solution.py:33
  79.6 23.1 %collective-permute-start.13 = (f32[128,256]{1,0:T(8,128)S(1)}, f32[128,256]{1,0:T(8,128)S(1)}, u32[]{:S(2)}, u32[]{:S(2)}) collective-permute-start(f32[128,256]{1,0:T(8,128)S(1)} %slice_bitcast_fusion.4), channel_id=1, source_target_pairs={{0,4},{1,5},{2,6},{3,7},{4,0},{5,1},{6,2},{7,3},{8,12},{9,13},{10,... | collective-permute-start | bytes 393224 | tf_op jit(solution)/shard_map/ppermute | solution.py:45
  93.9 9.5 %collective-permute-start.18 = (f32[128,256]{1,0:T(8,128)S(1)}, f32[128,256]{1,0:T(8,128)S(1)}, u32[]{:S(2)}, u32[]{:S(2)}) collective-permute-start(f32[128,256]{1,0:T(8,128)S(1)} %get-tuple-element.19), channel_id=1, source_target_pairs={{0,128},{8,136},{16,144},{24,152},{32,160},{40,168},{48,176},{56,1... | collective-permute-start | bytes 393224 | tf_op jit(solution)/shard_map/ppermute | solution.py:29
  98.6 11.8 %collective-permute-start.19 = (f32[128,256]{1,0:T(8,128)S(1)}, f32[128,256]{1,0:T(8,128)S(1)}, u32[]{:S(2)}, u32[]{:S(2)}) collective-permute-start(f32[128,256]{1,0:T(8,128)S(1)} %get-tuple-element.18), channel_id=1, source_target_pairs={{0,64},{8,72},{16,80},{24,88},{32,96},{40,104},{48,112},{56,120},{... | collective-permute-start | bytes 393224 | tf_op jit(solution)/shard_map/ppermute | solution.py:29
  100.9 11.3 %collective-permute-start.20 = (f32[128,256]{1,0:T(8,128)S(1)}, f32[128,256]{1,0:T(8,128)S(1)}, u32[]{:S(2)}, u32[]{:S(2)}) collective-permute-start(f32[128,256]{1,0:T(8,128)S(1)} %get-tuple-element.17), channel_id=1, source_target_pairs={{0,192},{8,200},{16,208},{24,216},{32,224},{40,232},{48,240},{56,2... | collective-permute-start | bytes 393224 | tf_op jit(solution)/shard_map/ppermute | solution.py:29
  112.3 43.7 %copy-start.1 = (f32[128,256]{1,0:T(8,128)}, f32[128,256]{1,0:T(8,128)S(1)}, u32[]{:S(2)}) copy-start(f32[128,256]{1,0:T(8,128)S(1)} %fusion.3.products) | copy-start | bytes 393220
  112.7 1.4 collective-permute-start.21
  114.2 5.2 %collective-permute-start.23 = (f32[32,256]{1,0:T(8,128)S(1)}, f32[32,256]{1,0:T(8,128)S(1)}, u32[]{:S(2)}, u32[]{:S(2)}) collective-permute-start(f32[32,256]{1,0:T(8,128)S(1)} %get-tuple-element.22), channel_id=1, source_target_pairs={{0,1},{1,2},{2,3},{3,0},{4,5},{5,6},{6,7},{7,4},{8,9},{9,10},{10,1... | collective-permute-start | bytes 98312 | tf_op jit(solution)/shard_map/ppermute | solution.py:41
  115.3 4.1 %collective-permute-start.24 = (f32[32,256]{1,0:T(8,128)S(1)}, f32[32,256]{1,0:T(8,128)S(1)}, u32[]{:S(2)}, u32[]{:S(2)}) collective-permute-start(f32[32,256]{1,0:T(8,128)S(1)} %get-tuple-element.21), channel_id=1, source_target_pairs={{0,3},{1,0},{2,1},{3,2},{4,7},{5,4},{6,5},{7,6},{8,11},{9,8},{10,9... | collective-permute-start | bytes 98312 | tf_op jit(solution)/shard_map/ppermute | solution.py:41
  117.5 5.4 %collective-permute-start.22 = (f32[32,256]{1,0:T(8,128)S(1)}, f32[32,256]{1,0:T(8,128)S(1)}, u32[]{:S(2)}, u32[]{:S(2)}) collective-permute-start(f32[32,256]{1,0:T(8,128)S(1)} %get-tuple-element.20), channel_id=1, source_target_pairs={{0,2},{1,3},{2,0},{3,1},{4,6},{5,7},{6,4},{7,5},{8,10},{9,11},{10,... | collective-permute-start | bytes 98312 | tf_op jit(solution)/shard_map/ppermute | solution.py:41
  123.0 4.0 %collective-permute-start.26 = (f32[32,256]{1,0:T(8,128)S(1)}, f32[32,256]{1,0:T(8,128)S(1)}, u32[]{:S(2)}, u32[]{:S(2)}) collective-permute-start(f32[32,256]{1,0:T(8,128)S(1)} %add_add_fusion.3), channel_id=1, source_target_pairs={{0,16},{8,24},{16,32},{24,40},{32,48},{40,56},{48,0},{56,8},{64,80... | collective-permute-start | bytes 98312 | tf_op jit(solution)/shard_map/ppermute | solution.py:33
  123.2 3.9 %collective-permute-start.27 = (f32[32,256]{1,0:T(8,128)S(1)}, f32[32,256]{1,0:T(8,128)S(1)}, u32[]{:S(2)}, u32[]{:S(2)}) collective-permute-start(f32[32,256]{1,0:T(8,128)S(1)} %add_add_fusion.3), channel_id=1, source_target_pairs={{0,48},{8,56},{16,0},{24,8},{32,16},{40,24},{48,32},{56,40},{64,11... | collective-permute-start | bytes 98312 | tf_op jit(solution)/shard_map/ppermute | solution.py:33
  125.1 5.4 %collective-permute-start.25 = (f32[32,256]{1,0:T(8,128)S(1)}, f32[32,256]{1,0:T(8,128)S(1)}, u32[]{:S(2)}, u32[]{:S(2)}) collective-permute-start(f32[32,256]{1,0:T(8,128)S(1)} %add_add_fusion.3), channel_id=1, source_target_pairs={{0,32},{8,40},{16,48},{24,56},{32,0},{40,8},{48,16},{56,24},{64,96... | collective-permute-start | bytes 98312 | tf_op jit(solution)/shard_map/ppermute | solution.py:33
  130.5 4.0 %collective-permute-start.28 = (f32[32,256]{1,0:T(8,128)S(1)}, f32[32,256]{1,0:T(8,128)S(1)}, u32[]{:S(2)}, u32[]{:S(2)}) collective-permute-start(f32[32,256]{1,0:T(8,128)S(1)} %add_add_fusion.2), channel_id=1, source_target_pairs={{0,4},{1,5},{2,6},{3,7},{4,0},{5,1},{6,2},{7,3},{8,12},{9,13},{10,... | collective-permute-start | bytes 98312 | tf_op jit(solution)/shard_map/ppermute | solution.py:45
  134.5 7.9 %collective-permute-start.30 = (f32[32,256]{1,0:T(8,128)S(1)}, f32[32,256]{1,0:T(8,128)S(1)}, u32[]{:S(2)}, u32[]{:S(2)}) collective-permute-start(f32[32,256]{1,0:T(8,128)S(1)} %add.124), channel_id=1, source_target_pairs={{0,64},{8,72},{16,80},{24,88},{32,96},{40,104},{48,112},{56,120},{... | collective-permute-start | bytes 98312 | tf_op jit(solution)/shard_map/ppermute | solution.py:29
  136.3 6.2 %collective-permute-start.31 = (f32[32,256]{1,0:T(8,128)S(1)}, f32[32,256]{1,0:T(8,128)S(1)}, u32[]{:S(2)}, u32[]{:S(2)}) collective-permute-start(f32[32,256]{1,0:T(8,128)S(1)} %add.124), channel_id=1, source_target_pairs={{0,192},{8,200},{16,208},{24,216},{32,224},{40,232},{48,240},{56,2... | collective-permute-start | bytes 98312 | tf_op jit(solution)/shard_map/ppermute | solution.py:29
  138.7 7.8 %collective-permute-start.29 = (f32[32,256]{1,0:T(8,128)S(1)}, f32[32,256]{1,0:T(8,128)S(1)}, u32[]{:S(2)}, u32[]{:S(2)}) collective-permute-start(f32[32,256]{1,0:T(8,128)S(1)} %add.124), channel_id=1, source_target_pairs={{0,128},{8,136},{16,144},{24,152},{32,160},{40,168},{48,176},{56,1... | collective-permute-start | bytes 98312 | tf_op jit(solution)/shard_map/ppermute | solution.py:29
  146.5 1.3 collective-permute-start.32
  147.8 8.2 %copy-start.5 = (f32[2,32,256]{2,1,0:T(8,128)}, f32[2,32,256]{2,1,0:T(8,128)S(1)}, u32[]{:S(2)}) copy-start(f32[2,32,256]{2,1,0:T(8,128)S(1)} %pad_maximum_fusion.1.piece0) | copy-start | bytes 196612
  147.8 5.1 %collective-permute-start.33 = (f32[2,32,256]{2,1,0:T(8,128)S(1)}, f32[2,32,256]{2,1,0:T(8,128)S(1)}, u32[]{:S(2)}, u32[]{:S(2)}) collective-permute-start(f32[2,32,256]{2,1,0:T(8,128)S(1)} %pad_maximum_fusion.1.piece0), channel_id=1, source_target_pairs={{0,3},{1,0},{2,1},{3,2},{4,7},{5,4},{6,5},{7,6},{8,11},{9,8},{10,9... | collective-permute-start | bytes 196616 | tf_op jit(solution)/shard_map/ppermute | solution.py:41
  149.2 6.4 %collective-permute-start.34 = (f32[2,32,256]{2,1,0:T(8,128)S(1)}, f32[2,32,256]{2,1,0:T(8,128)S(1)}, u32[]{:S(2)}, u32[]{:S(2)}) collective-permute-start(f32[2,32,256]{2,1,0:T(8,128)S(1)} %pad_maximum_fusion.1.piece0), channel_id=1, source_target_pairs={{0,2},{1,3},{2,0},{3,1},{4,6},{5,7},{6,4},{7,5},{8,10},{9,11},{10,... | collective-permute-start | bytes 196616 | tf_op jit(solution)/shard_map/ppermute | solution.py:41
  150.0 6.0 %collective-permute-start.35 = (f32[2,32,256]{2,1,0:T(8,128)S(1)}, f32[2,32,256]{2,1,0:T(8,128)S(1)}, u32[]{:S(2)}, u32[]{:S(2)}) collective-permute-start(f32[2,32,256]{2,1,0:T(8,128)S(1)} %pad_maximum_fusion.1.piece0), channel_id=1, source_target_pairs={{0,1},{1,2},{2,3},{3,0},{4,5},{5,6},{6,7},{7,4},{8,9},{9,10},{10,1... | collective-permute-start | bytes 196616 | tf_op jit(solution)/shard_map/ppermute | solution.py:41
  152.9 3.0 %copy-start.13 = (f32[2,32,256]{2,1,0:T(8,128)}, f32[2,32,256]{2,1,0:T(8,128)S(1)}, u32[]{:S(2)}) copy-start(f32[2,32,256]{2,1,0:T(8,128)S(1)} %collective-permute-done.33.piece1) | copy-start | bytes 196612
  (5 other events, 3.5 us)

commit v2 on v0

--- a/solution.py
+++ b/solution.py
@@ -25,8 +25,13 @@
     return [(row_at(z, x, c), row_at(*move(z, x, c))) for z in range(N_ZH) for x in range(N_X) for c in range(N_CORE)]
 
 
-def to_z(v, k):
-    return lax.ppermute(v, "row", row_pairs(lambda z, x, c: (z + k, x, c)))
+def swap_z(v):
+    groups = [[row_at(z, x, c) for z in range(N_ZH)] for x in range(N_X) for c in range(N_CORE)]
+    return lax.all_to_all(v, "row", 0, 0, tiled=True, axis_index_groups=groups)
+
+
+def copies(v, n):
+    return jnp.broadcast_to(v[None], (n,) + v.shape)
 
 
 def to_x(v, k):
@@ -72,8 +77,8 @@
 
 def col_spot(place, cp):
     r = place[0]
-    zk, xk, cx = ((cp >> 3) - (r >> 3)) & 3, ((cp >> 1) - (r >> 1)) & 3, (cp ^ r) & 1
-    return (cx * N_X + xk) * N_ZH + zk
+    z, xk, cx = cp >> 3, ((cp >> 1) - (r >> 1)) & 3, (cp ^ r) & 1
+    return (cx * N_X + xk) * N_ZH + z
 
 
 def mirror_kernel(place, counts, rows, cols, blocks, *refs):
@@ -94,17 +99,15 @@
 
 def direct_kernel(place, counts, rows, cols, blocks, *refs):
     n = N_CORE * N_X
-    pieces, outs, vectors, acc = refs[:n], refs[n : n + N_Y], refs[-2], refs[-1]
+    pieces, acc, vectors = refs[:n], refs[n], refs[n + 1]
     acc[...] = jnp.zeros_like(acc)
     for k, piece in enumerate(pieces):
         vectors[k * N_ZH : (k + 1) * N_ZH] = piece[...]
 
     def add(tile, rp, cp):
-        acc[row_spot(place, rp)] += jnp.dot(tile, vectors[col_spot(place, cp)], preferred_element_type=F32)
+        acc[rp] += jnp.dot(tile, vectors[col_spot(place, cp)], preferred_element_type=F32)
 
     slot_loop(counts, rows, cols, blocks, add)
-    for k, out in enumerate(outs):
-        out[...] = acc[k * N_ZL : (k + 1) * N_ZL]
 
 
 def products_of(kernel, scalars, blocks, pieces, n_out, out_blocks):
@@ -228,7 +231,7 @@
     got = ring_sum([parts[0]] + [to_y(parts[k], k) for k in range(1, N_Y)])
     got = ring_sum([got] + [to_x(got, k) for k in range(1, N_X)])
     got = got + to_zl(got)
-    got = ring_sum([got] + [to_z(got, k) for k in range(1, N_ZH)])
+    got = ring_sum(swap_z(copies(got, N_ZH)))
     both = jnp.stack([got, to_core(got)])
     return [both] + [to_y(both, -k) for k in range(1, N_Y)]
 
@@ -237,18 +240,17 @@
     place = jnp.stack([lax.axis_index("row"), lax.axis_index("col")]).astype(jnp.int32)
     scalars = (place, counts, block_rows, block_cols)
     first = jnp.stack([trials, to_zl(trials)])
-    zs = jnp.stack([trials] + [to_z(trials, -k) for k in range(1, N_ZH)])
+    zs = swap_z(copies(trials, N_ZH))
     row_pieces = [first] + [to_y(first, -k) for k in range(1, N_Y)]
     col_pieces = [zs] + [to_x(zs, -k) for k in range(1, N_X)]
     col_keep, col_send = products_of(mirror_kernel, scalars, blocks[0], row_pieces, N_CORE, N_X * N_ZH)
     col_pieces = col_pieces + [to_core(v) for v in col_pieces]
-    row_outs = products_of(direct_kernel, scalars, blocks[0], col_pieces, N_Y, N_ZL)
+    (row_out,) = products_of(direct_kernel, scalars, blocks[0], col_pieces, 1, N_COL)
     pair = col_keep + to_core(col_send)
     parts = [pair[k * N_ZH : (k + 1) * N_ZH] for k in range(N_X)]
     got = ring_sum([parts[0]] + [to_x(parts[k], k) for k in range(1, N_X)])
-    rows = ring_sum([row_outs[0]] + [to_y(row_outs[k], k) for k in range(1, N_Y)])
-    row_sum = rows[0] + to_zl(rows[1])
-    col_sum = ring_sum([got[0]] + [to_z(got[k], k) for k in range(1, N_ZH)])
+    row_sum = lax.all_to_all(row_out, "col", 0, 0, tiled=True).sum(0)
+    col_sum = ring_sum(swap_z(got))
     products = row_sum + col_sum
     return factor_and_basis(place, gram_pieces(products, place), products)
 

time: 174 us -> 183 us (1.052)
  the two profiles are of different devices: /device:TPU:1 before, /device:TPU:2 now
where the time goes in v2:
time: 183 us; the launch traced here: 180 us
  waiting for transfers between devices  70.4 us (38%)
  starting transfers between devices  44.1 us (24%)
  blocking collectives  30.6 us (17%)
  Pallas kernels  26.1 us (14%)
  other arithmetic  5.1 us (3%)
  local copies, waits for them, and re-layouts  2.26 us (1%)
    ppermute x9, waiting for transfers between devices, to_x(): return lax.ppermute(v, 'row', row_pairs(lambda z, x, c: (z, x + k, c)))  37.8 us
    all_to_all x2, blocking collectives, swap_z(): return lax.all_to_all(v, 'row', 0, 0, tiled=True, axis_index_groups=groups)  30.6 us
    ppermute x9, starting transfers between devices, to_y(): lax.ppermute(v, 'col', [(col_at(zl, y), col_at(zl, y + k)) for zl in rang...  16.1 us
    pallas_call x1, Pallas kernels, factor_and_basis(): pl.pallas_call(factor_kernel, out_shape=(jax.ShapeDtypeStruct((edge, size...  15 us
    all_to_all x1, waiting for transfers between devices, swap_z(): return lax.all_to_all(v, 'row', 0, 0, tiled=True, axis_index_groups=groups)  13.3 us
    pallas_call x2, Pallas kernels, products_of(): pl.pallas_call(kernel, out_shape=(jax.ShapeDtypeStruct((out_blocks, edge,...  11 us
    ppermute x9, waiting for transfers between devices, to_y(): lax.ppermute(v, 'col', [(col_at(zl, y), col_at(zl, y + k)) for zl in rang...  10.9 us
    ppermute x9, starting transfers between devices, to_x(): return lax.ppermute(v, 'row', row_pairs(lambda z, x, c: (z, x + k, c)))  10.5 us
  transfers between devices with their start and end apart: 29, of which 21 were waited for; matrix products, arithmetic and copies ran while one was open for 2% of the time, Pallas kernels for 3%

profile of v2, /device:TPU:2, one launch (start us, length us, event | category | flops | bytes accessed | tf_op | source)
XLA Modules:
  0.0 180.5 jit_solution(2726443630924989296)
XLA Ops:
  0.6 2.0 %collective-permute-start.7 = (bf16[128,256]{1,0:T(8,128)(2,1)}, bf16[128,256]{1,0:T(8,128)(2,1)S(1)}, u32[]{:S(2)}, u32[]{:S(2)}) collective-permute-start(bf16[128,256]{1,0:T(8,128)(2,1)} %param.9), channel_id=1, source_target_pairs={{0,4},{1,5},{2,6},{3,7},{4,0},{5,1},{6,2},{7,3},{8,12},{9,13},{10,... | collective-permute-start | bytes 196616 | tf_op jit(solution)/shard_map/ppermute | solution.py:50
  2.6 2.6 %collective-permute-done.7 = bf16[128,256]{1,0:T(8,128)(2,1)S(1)} collective-permute-done((bf16[128,256]{1,0:T(8,128)(2,1)}, bf16[128,256]{1,0:T(8,128)(2,1)S(1)}, u32[]{:S(2)}, u32[]{:S(2)}) %collective-permute-start.7) | collective-permute-done | bytes 65568 | tf_op jit(solution)/shard_map/ppermute | solution.py:50
  5.2 0.9 pad_maximum_fusion.refs_0_
  6.1 1.7 collective-permute-start.10
  7.7 1.7 collective-permute-start.8
  9.4 2.0 %collective-permute-start.9 = (bf16[2,128,256]{2,1,0:T(8,128)(2,1)S(1)}, bf16[2,128,256]{2,1,0:T(8,128)(2,1)S(1)}, u32[]{:S(2)}, u32[]{:S(2)}) collective-permute-start(bf16[2,128,256]{2,1,0:T(8,128)(2,1)S(1)} %pad_maximum_fusion.refs_0_), channel_id=1, source_target_pairs={{0,2},{1,3},{2,0},{3,1},{4,6},{5,7},{6,4},{7,5},{8,10},{9,11},{10,... | collective-permute-start | bytes 393224 | tf_op jit(solution)/shard_map/ppermute | solution.py:46
  12.9 0.8 collective-permute-done.8.refs_1_
  13.7 2.4 %collective-permute-done.9.refs_2_ = bf16[2,128,256]{2,1,0:T(8,128)(2,1)S(1)} collective-permute-done((bf16[2,128,256]{2,1,0:T(8,128)(2,1)S(1)}, bf16[2,128,256]{2,1,0:T(8,128)(2,1)S(1)}, u32[]{:S(2)}, u32[]{:S(2)}) %collective-permute-start.9) | collective-permute-done | bytes 131104 | tf_op jit(solution)/shard_map/ppermute | solution.py:46
  16.2 0.6 copy-done.14
  16.8 6.1 %shard_map.69 = (f32[16,128,256]{2,1,0:T(8,128)}, f32[16,128,256]{2,1,0:T(8,128)}) custom-call(s32[2]{0:T(128)} %pad_add_fusion.place, s32[1,1]{1,0:T(1,128)S(6)} %copy.7.counts, s32[1,64]{1,0:T(1,128)} %rows.3, s32[1,64]{1,0:T(1,128)} %cols.3, bf16[64,128,128]{2,1,0:T(8,128)(2,1)} %bitcast.18, bf16[2,128,256]{2,1,0:T(8,128)(2,1)} %copy-done.2, ...), custom_call_target="tpu_custom_call" | custom-call | flops 536870912 | bytes 6815744 | tf_op jit(solution)/shard_map/pallas_call | solution.py:118
  22.9 18.4 %all_to_all.20.refs_0_ = bf16[4,128,256]{2,1,0:T(8,128)(2,1)S(1)} all-to-all(bf16[4,128,256]{2,1,0:T(8,128)(2,1)S(1)} %broadcast_in_dim.6), channel_id=1, replica_groups={{0,64,128,192},{8,72,136,200},{16,80,144,208},{24,88,152,216},{32,96,16..., dimensions={0} | all-to-all | bytes 524288 | tf_op jit(solution)/shard_map/all_to_all | solution.py:30
  41.3 1.5 collective-permute-start
  42.9 2.2 %collective-permute-start.1 = (bf16[4,128,256]{2,1,0:T(8,128)(2,1)S(1)}, bf16[4,128,256]{2,1,0:T(8,128)(2,1)S(1)}, u32[]{:S(2)}, u32[]{:S(2)}) collective-permute-start(bf16[4,128,256]{2,1,0:T(8,128)(2,1)S(1)} %all_to_all.20.refs_0_), channel_id=1, source_target_pairs={{0,32},{8,40},{16,48},{24,56},{32,0},{40,8},{48,16},{56,24},{64,96... | collective-permute-start | bytes 786440 | tf_op jit(solution)/shard_map/ppermute | solution.py:38
  45.0 0.8 collective-permute-start.2
  45.8 5.4 %collective-permute-done.refs_1_ = bf16[4,128,256]{2,1,0:T(8,128)(2,1)S(1)} collective-permute-done((bf16[4,128,256]{2,1,0:T(8,128)(2,1)S(1)}, bf16[4,128,256]{2,1,0:T(8,128)(2,1)S(1)}, u32[]{:S(2)}, u32[]{:S(2)}) %collective-permute-start) | collective-permute-done | bytes 262176 | tf_op jit(solution)/shard_map/ppermute | solution.py:38
  51.3 3.0 %collective-permute-done.1.refs_2_ = bf16[4,128,256]{2,1,0:T(8,128)(2,1)S(1)} collective-permute-done((bf16[4,128,256]{2,1,0:T(8,128)(2,1)S(1)}, bf16[4,128,256]{2,1,0:T(8,128)(2,1)S(1)}, u32[]{:S(2)}, u32[]{:S(2)}) %collective-permute-start.1) | collective-permute-done | bytes 262176 | tf_op jit(solution)/shard_map/ppermute | solution.py:38
  54.2 1.7 collective-permute-done.2.refs_3_
  56.0 1.5 collective-permute-done.6.refs_7_
  57.5 0.7 copy-done.9
  58.2 5.0 %shard_map.68 = f32[8,128,256]{2,1,0:T(8,128)} custom-call(s32[2]{0:T(128)} %pad_add_fusion.place, s32[1,1]{1,0:T(1,128)S(6)} %copy.7.counts, s32[1,64]{1,0:T(1,128)} %rows.3, s32[1,64]{1,0:T(1,128)} %cols.3, bf16[64,128,128]{2,1,0:T(8,128)(2,1)} %bitcast.19, bf16[4,128,256]{2,1,0:T(8,128)(2,1)} %copy-done.1, bf16[4,128,256]{2,1,0:T(8,128)(2,1)} %copy-done.3, ...), custom_call_target="tpu_custom_call" | custom-call | flops 536870912 | bytes 5242880 | tf_op jit(solution)/shard_map/pallas_call | solution.py:118
  63.2 6.3 %all-to-all-start.1 = ((f32[8,128,256]{2,1,0:T(8,128)}), f32[8,128,256]{2,1,0:T(8,128)S(1)}, u32[]{:S(2)}, u32[]{:S(2)}) async-start(f32[8,128,256]{2,1,0:T(8,128)} %shard_map.68), calls=%async_computation.1 | async-start | bytes 2097152 | tf_op jit(solution)/shard_map/all_to_all | solution.py:252
  69.4 1.9 %add.107 = f32[16,128,256]{2,1,0:T(8,128)S(1)} add(f32[16,128,256]{2,1,0:T(8,128)S(1)} %copy-done, f32[16,128,256]{2,1,0:T(8,128)} %collective-permute-done.11) | non-fusion elementwise | flops 524288 | bytes 6291456 | tf_op jit(solution)/shard_map/add | solution.py:249
  71.5 0.9 collective-permute-start.12
  72.4 1.6 collective-permute-start.13
  74.0 0.7 collective-permute-start.14
  74.7 12.9 %collective-permute-done.12 = f32[4,128,256]{2,1,0:T(8,128)S(1)} collective-permute-done((f32[4,128,256]{2,1,0:T(8,128)S(1)}, f32[4,128,256]{2,1,0:T(8,128)S(1)}, u32[]{:S(2)}, u32[]{:S(2)}) %collective-permute-start.12) | collective-permute-done | bytes 524320 | tf_op jit(solution)/shard_map/ppermute | solution.py:38
  87.7 9.8 %collective-permute-done.13 = f32[4,128,256]{2,1,0:T(8,128)S(1)} collective-permute-done((f32[4,128,256]{2,1,0:T(8,128)S(1)}, f32[4,128,256]{2,1,0:T(8,128)S(1)}, u32[]{:S(2)}, u32[]{:S(2)}) %collective-permute-start.13) | collective-permute-done | bytes 524320 | tf_op jit(solution)/shard_map/ppermute | solution.py:38
  97.4 1.7 collective-permute-done.14
  99.1 1.0 fusion
  100.1 3.7 %all-to-all-start.2 = ((f32[4,128,256]{2,1,0:T(8,128)}), f32[4,128,256]{2,1,0:T(8,128)S(1)}, u32[]{:S(2)}, u32[]{:S(2)}) async-start(f32[4,128,256]{2,1,0:T(8,128)} %fusion), calls=%async_computation.2 | async-start | bytes 1048576 | tf_op jit(solution)/shard_map/all_to_all | solution.py:30
  103.8 13.3 %all-to-all-done.2 = f32[4,128,256]{2,1,0:T(8,128)S(1)} async-done(((f32[4,128,256]{2,1,0:T(8,128)}), f32[4,128,256]{2,1,0:T(8,128)S(1)}, u32[]{:S(2)}, u32[]{:S(2)}) %all-to-all-start.2) | async-done | bytes 524320 | tf_op jit(solution)/shard_map/all_to_all | solution.py:30
  117.1 0.7 bitcast_add_fusion
  118.4 1.3 collective-permute-done.15
  119.8 3.3 %collective-permute-start.16 = (f32[32,256]{1,0:T(8,128)S(1)}, f32[32,256]{1,0:T(8,128)S(1)}, u32[]{:S(2)}, u32[]{:S(2)}) collective-permute-start(f32[32,256]{1,0:T(8,128)S(1)} %get-tuple-element.11), channel_id=1, source_target_pairs={{0,2},{1,3},{2,0},{3,1},{4,6},{5,7},{6,4},{7,5},{8,10},{9,11},{10,... | collective-permute-start | bytes 98312 | tf_op jit(solution)/shard_map/ppermute | solution.py:46
  123.6 2.7 %collective-permute-start.18 = (f32[32,256]{1,0:T(8,128)S(1)}, f32[32,256]{1,0:T(8,128)S(1)}, u32[]{:S(2)}, u32[]{:S(2)}) collective-permute-start(f32[32,256]{1,0:T(8,128)S(1)} %get-tuple-element.12), channel_id=1, source_target_pairs={{0,3},{1,0},{2,1},{3,2},{4,7},{5,4},{6,5},{7,6},{8,11},{9,8},{10,9... | collective-permute-start | bytes 98312 | tf_op jit(solution)/shard_map/ppermute | solution.py:46
  126.3 1.9 %collective-permute-done.17 = f32[32,256]{1,0:T(8,128)S(1)} collective-permute-done((f32[32,256]{1,0:T(8,128)S(1)}, f32[32,256]{1,0:T(8,128)S(1)}, u32[]{:S(2)}, u32[]{:S(2)}) %collective-permute-start.17) | collective-permute-done | bytes 32800 | tf_op jit(solution)/shard_map/ppermute | solution.py:46
  128.6 1.5 collective-permute-start.20
  130.0 0.9 collective-permute-start.21
  130.9 2.8 %collective-permute-done.19 = f32[32,256]{1,0:T(8,128)S(1)} collective-permute-done((f32[32,256]{1,0:T(8,128)S(1)}, f32[32,256]{1,0:T(8,128)S(1)}, u32[]{:S(2)}, u32[]{:S(2)}) %collective-permute-start.19) | collective-permute-done | bytes 32800 | tf_op jit(solution)/shard_map/ppermute | solution.py:38
  134.3 5.4 %collective-permute-start.22 = (f32[32,256]{1,0:T(8,128)S(1)}, f32[32,256]{1,0:T(8,128)S(1)}, u32[]{:S(2)}, u32[]{:S(2)}) collective-permute-start(f32[32,256]{1,0:T(8,128)S(1)} %add_add_fusion), channel_id=1, source_target_pairs={{0,4},{1,5},{2,6},{3,7},{4,0},{5,1},{6,2},{7,3},{8,12},{9,13},{10,... | collective-permute-start | bytes 98312 | tf_op jit(solution)/shard_map/ppermute | solution.py:50
  139.6 1.9 %collective-permute-done.22 = f32[32,256]{1,0:T(8,128)S(1)} collective-permute-done((f32[32,256]{1,0:T(8,128)S(1)}, f32[32,256]{1,0:T(8,128)S(1)}, u32[]{:S(2)}, u32[]{:S(2)}) %collective-permute-start.22) | collective-permute-done | bytes 32800 | tf_op jit(solution)/shard_map/ppermute | solution.py:50
  141.6 12.2 %all_to_all.21 = f32[4,32,256]{2,1,0:T(8,128)S(1)} all-to-all(f32[4,32,256]{2,1,0:T(8,128)S(1)} %broadcast_in_dim.16), channel_id=1, replica_groups={{0,64,128,192},{8,72,136,200},{16,80,144,208},{24,88,152,216},{32,96,16..., dimensions={0} | all-to-all | bytes 262144 | tf_op jit(solution)/shard_map/all_to_all | solution.py:30
  153.9 1.2 collective-permute-done.23
  155.0 3.3 %collective-permute-start.24 = (f32[2,32,256]{2,1,0:T(8,128)S(1)}, f32[2,32,256]{2,1,0:T(8,128)S(1)}, u32[]{:S(2)}, u32[]{:S(2)}) collective-permute-start(f32[2,32,256]{2,1,0:T(8,128)S(1)} %pad_maximum_fusion.1.piece0), channel_id=1, source_target_pairs={{0,3},{1,0},{2,1},{3,2},{4,7},{5,4},{6,5},{7,6},{8,11},{9,8},{10,9... | collective-permute-start | bytes 196616 | tf_op jit(solution)/shard_map/ppermute | solution.py:46
  158.4 1.0 collective-permute-start.26
  159.3 2.1 %collective-permute-done.24.piece1 = f32[2,32,256]{2,1,0:T(8,128)S(1)} collective-permute-done((f32[2,32,256]{2,1,0:T(8,128)S(1)}, f32[2,32,256]{2,1,0:T(8,128)S(1)}, u32[]{:S(2)}, u32[]{:S(2)}) %collective-permute-start.24) | collective-permute-done | bytes 65568 | tf_op jit(solution)/shard_map/ppermute | solution.py:46
  161.4 3.0 %collective-permute-done.25.piece2 = f32[2,32,256]{2,1,0:T(8,128)S(1)} collective-permute-done((f32[2,32,256]{2,1,0:T(8,128)S(1)}, f32[2,32,256]{2,1,0:T(8,128)S(1)}, u32[]{:S(2)}, u32[]{:S(2)}) %collective-permute-start.25) | collective-permute-done | bytes 65568 | tf_op jit(solution)/shard_map/ppermute | solution.py:46
  165.4 15.0 %factor.1 = (f32[128,256]{1,0:T(8,128)}, f32[256,256]{1,0:T(8,128)}) custom-call(s32[2]{0:T(128)} %pad_add_fusion.place, f32[2,32,256]{2,1,0:T(8,128)} %copy-done.11, f32[2,32,256]{2,1,0:T(8,128)} %copy-done.15, f32[2,32,256]{2,1,0:T(8,128)} %copy-done.16, f32[2,32,256]{2,1,0:T(8,128)} %copy-done.17, f32[128,256]{1,0:T(8,128)} %get-tuple-element.6.products), custom_call_target="tpu_custom_call" | custom-call | tf_op jit(solution)/shard_map/factor/pallas_call | solution.py:212
  (70 shorter events, 4.5 us)
Async XLA Ops:
  0.6 22.2 %copy-start.10 = (bf16[128,256]{1,0:T(8,128)(2,1)S(1)}, bf16[128,256]{1,0:T(8,128)(2,1)}, u32[]{:S(2)}) copy-start(bf16[128,256]{1,0:T(8,128)(2,1)} %param.9) | copy-start | bytes 196612
  0.6 4.6 %collective-permute-start.7 = (bf16[128,256]{1,0:T(8,128)(2,1)}, bf16[128,256]{1,0:T(8,128)(2,1)S(1)}, u32[]{:S(2)}, u32[]{:S(2)}) collective-permute-start(bf16[128,256]{1,0:T(8,128)(2,1)} %param.9), channel_id=1, source_target_pairs={{0,4},{1,5},{2,6},{3,7},{4,0},{5,1},{6,2},{7,3},{8,12},{9,13},{10,... | collective-permute-start | bytes 196616 | tf_op jit(solution)/shard_map/ppermute | solution.py:50
  6.1 10.1 %copy-start.2 = (bf16[2,128,256]{2,1,0:T(8,128)(2,1)}, bf16[2,128,256]{2,1,0:T(8,128)(2,1)S(1)}, u32[]{:S(2)}) copy-start(bf16[2,128,256]{2,1,0:T(8,128)(2,1)S(1)} %pad_maximum_fusion.refs_0_) | copy-start | bytes 393220
  6.1 6.9 %collective-permute-start.10 = (bf16[2,128,256]{2,1,0:T(8,128)(2,1)S(1)}, bf16[2,128,256]{2,1,0:T(8,128)(2,1)S(1)}, u32[]{:S(2)}, u32[]{:S(2)}) collective-permute-start(bf16[2,128,256]{2,1,0:T(8,128)(2,1)S(1)} %pad_maximum_fusion.refs_0_), channel_id=1, source_target_pairs={{0,1},{1,2},{2,3},{3,0},{4,5},{5,6},{6,7},{7,4},{8,9},{9,10},{10,1... | collective-permute-start | bytes 393224 | tf_op jit(solution)/shard_map/ppermute | solution.py:46
  7.7 6.0 %collective-permute-start.8 = (bf16[2,128,256]{2,1,0:T(8,128)(2,1)S(1)}, bf16[2,128,256]{2,1,0:T(8,128)(2,1)S(1)}, u32[]{:S(2)}, u32[]{:S(2)}) collective-permute-start(bf16[2,128,256]{2,1,0:T(8,128)(2,1)S(1)} %pad_maximum_fusion.refs_0_), channel_id=1, source_target_pairs={{0,3},{1,0},{2,1},{3,2},{4,7},{5,4},{6,5},{7,6},{8,11},{9,8},{10,9... | collective-permute-start | bytes 393224 | tf_op jit(solution)/shard_map/ppermute | solution.py:46
  9.4 6.8 %collective-permute-start.9 = (bf16[2,128,256]{2,1,0:T(8,128)(2,1)S(1)}, bf16[2,128,256]{2,1,0:T(8,128)(2,1)S(1)}, u32[]{:S(2)}, u32[]{:S(2)}) collective-permute-start(bf16[2,128,256]{2,1,0:T(8,128)(2,1)S(1)} %pad_maximum_fusion.refs_0_), channel_id=1, source_target_pairs={{0,2},{1,3},{2,0},{3,1},{4,6},{5,7},{6,4},{7,5},{8,10},{9,11},{10,... | collective-permute-start | bytes 393224 | tf_op jit(solution)/shard_map/ppermute | solution.py:46
  12.9 3.2 %copy-start.12 = (bf16[2,128,256]{2,1,0:T(8,128)(2,1)}, bf16[2,128,256]{2,1,0:T(8,128)(2,1)S(1)}, u32[]{:S(2)}) copy-start(bf16[2,128,256]{2,1,0:T(8,128)(2,1)S(1)} %collective-permute-done.10.refs_3_) | copy-start | bytes 393220
  13.7 2.4 %copy-start.13 = (bf16[2,128,256]{2,1,0:T(8,128)(2,1)}, bf16[2,128,256]{2,1,0:T(8,128)(2,1)S(1)}, u32[]{:S(2)}) copy-start(bf16[2,128,256]{2,1,0:T(8,128)(2,1)S(1)} %collective-permute-done.8.refs_1_) | copy-start | bytes 393220
  16.1 0.7 copy-start.14
  22.9 46.6 %collective-permute-start.11 = (f32[16,128,256]{2,1,0:T(8,128)}, f32[16,128,256]{2,1,0:T(8,128)}, u32[]{:S(2)}, u32[]{:S(2)}) collective-permute-start(f32[16,128,256]{2,1,0:T(8,128)} %get-tuple-element.5), channel_id=1, source_target_pairs={{0,8},{8,0},{16,24},{24,16},{32,40},{40,32},{48,56},{56,48},{64,72... | collective-permute-start | bytes 6291464 | tf_op jit(solution)/shard_map/ppermute | solution.py:42
  41.3 16.1 %copy-start.1 = (bf16[4,128,256]{2,1,0:T(8,128)(2,1)}, bf16[4,128,256]{2,1,0:T(8,128)(2,1)S(1)}, u32[]{:S(2)}) copy-start(bf16[4,128,256]{2,1,0:T(8,128)(2,1)S(1)} %all_to_all.20.refs_0_) | copy-start | bytes 786436
  41.3 9.9 %collective-permute-start = (bf16[4,128,256]{2,1,0:T(8,128)(2,1)S(1)}, bf16[4,128,256]{2,1,0:T(8,128)(2,1)S(1)}, u32[]{:S(2)}, u32[]{:S(2)}) collective-permute-start(bf16[4,128,256]{2,1,0:T(8,128)(2,1)S(1)} %all_to_all.20.refs_0_), channel_id=1, source_target_pairs={{0,48},{8,56},{16,0},{24,8},{32,16},{40,24},{48,32},{56,40},{64,11... | collective-permute-start | bytes 786440 | tf_op jit(solution)/shard_map/ppermute | solution.py:38
  42.9 11.4 %collective-permute-start.1 = (bf16[4,128,256]{2,1,0:T(8,128)(2,1)S(1)}, bf16[4,128,256]{2,1,0:T(8,128)(2,1)S(1)}, u32[]{:S(2)}, u32[]{:S(2)}) collective-permute-start(bf16[4,128,256]{2,1,0:T(8,128)(2,1)S(1)} %all_to_all.20.refs_0_), channel_id=1, source_target_pairs={{0,32},{8,40},{16,48},{24,56},{32,0},{40,8},{48,16},{56,24},{64,96... | collective-permute-start | bytes 786440 | tf_op jit(solution)/shard_map/ppermute | solution.py:38
  45.0 10.9 %collective-permute-start.2 = (bf16[4,128,256]{2,1,0:T(8,128)(2,1)S(1)}, bf16[4,128,256]{2,1,0:T(8,128)(2,1)S(1)}, u32[]{:S(2)}, u32[]{:S(2)}) collective-permute-start(bf16[4,128,256]{2,1,0:T(8,128)(2,1)S(1)} %all_to_all.20.refs_0_), channel_id=1, source_target_pairs={{0,16},{8,24},{16,32},{24,40},{32,48},{40,56},{48,0},{56,8},{64,80... | collective-permute-start | bytes 786440 | tf_op jit(solution)/shard_map/ppermute | solution.py:38
  45.8 10.1 %collective-permute-start.3 = (bf16[4,128,256]{2,1,0:T(8,128)(2,1)S(1)}, bf16[4,128,256]{2,1,0:T(8,128)(2,1)S(1)}, u32[]{:S(2)}, u32[]{:S(2)}) collective-permute-start(bf16[4,128,256]{2,1,0:T(8,128)(2,1)S(1)} %all_to_all.20.refs_0_), channel_id=1, source_target_pairs={{0,8},{8,0},{16,24},{24,16},{32,40},{40,32},{48,56},{56,48},{64,72... | collective-permute-start | bytes 786440 | tf_op jit(solution)/shard_map/ppermute | solution.py:42
  51.3 6.2 %copy-start.3 = (bf16[4,128,256]{2,1,0:T(8,128)(2,1)}, bf16[4,128,256]{2,1,0:T(8,128)(2,1)S(1)}, u32[]{:S(2)}) copy-start(bf16[4,128,256]{2,1,0:T(8,128)(2,1)S(1)} %collective-permute-done.refs_1_) | copy-start | bytes 786436
  51.3 4.7 %collective-permute-start.4 = (bf16[4,128,256]{2,1,0:T(8,128)(2,1)S(1)}, bf16[4,128,256]{2,1,0:T(8,128)(2,1)S(1)}, u32[]{:S(2)}, u32[]{:S(2)}) collective-permute-start(bf16[4,128,256]{2,1,0:T(8,128)(2,1)S(1)} %collective-permute-done.refs_1_), channel_id=1, source_target_pairs={{0,8},{8,0},{16,24},{24,16},{32,40},{40,32},{48,56},{56,48},{64,72... | collective-permute-start | bytes 786440 | tf_op jit(solution)/shard_map/ppermute | solution.py:42
  54.2 3.2 %copy-start.4 = (bf16[4,128,256]{2,1,0:T(8,128)(2,1)}, bf16[4,128,256]{2,1,0:T(8,128)(2,1)S(1)}, u32[]{:S(2)}) copy-start(bf16[4,128,256]{2,1,0:T(8,128)(2,1)S(1)} %collective-permute-done.1.refs_2_) | copy-start | bytes 786436
  54.2 1.7 collective-permute-start.5
  55.9 1.6 copy-start.5
  55.9 1.5 collective-permute-start.6
  55.9 1.6 copy-start.6
  55.9 1.5 copy-start.7
  55.9 1.5 copy-start.8
  57.5 0.7 copy-start.9
  63.2 6.3 %copy-start = (f32[16,128,256]{2,1,0:T(8,128)S(1)}, f32[16,128,256]{2,1,0:T(8,128)}, u32[]{:S(2)}) copy-start(f32[16,128,256]{2,1,0:T(8,128)} %get-tuple-element.4) | copy-start | bytes 6291460
  63.2 36.9 %all-to-all-start.1 = ((f32[8,128,256]{2,1,0:T(8,128)}), f32[8,128,256]{2,1,0:T(8,128)S(1)}, u32[]{:S(2)}, u32[]{:S(2)}) async-start(f32[8,128,256]{2,1,0:T(8,128)} %shard_map.68), calls=%async_computation.1 | async-start | bytes 2097152 | tf_op jit(solution)/shard_map/all_to_all | solution.py:252
  71.5 16.2 %collective-permute-start.12 = (f32[4,128,256]{2,1,0:T(8,128)S(1)}, f32[4,128,256]{2,1,0:T(8,128)S(1)}, u32[]{:S(2)}, u32[]{:S(2)}) collective-permute-start(f32[4,128,256]{2,1,0:T(8,128)S(1)} %get-tuple-element.10), channel_id=1, source_target_pairs={{0,32},{8,40},{16,48},{24,56},{32,0},{40,8},{48,16},{56,24},{64,96... | collective-permute-start | bytes 1572872 | tf_op jit(solution)/shard_map/ppermute | solution.py:38
  72.4 25.0 %collective-permute-start.13 = (f32[4,128,256]{2,1,0:T(8,128)S(1)}, f32[4,128,256]{2,1,0:T(8,128)S(1)}, u32[]{:S(2)}, u32[]{:S(2)}) collective-permute-start(f32[4,128,256]{2,1,0:T(8,128)S(1)} %get-tuple-element.9), channel_id=1, source_target_pairs={{0,16},{8,24},{16,32},{24,40},{32,48},{40,56},{48,0},{56,8},{64,80... | collective-permute-start | bytes 1572872 | tf_op jit(solution)/shard_map/ppermute | solution.py:38
  74.0 25.1 %collective-permute-start.14 = (f32[4,128,256]{2,1,0:T(8,128)S(1)}, f32[4,128,256]{2,1,0:T(8,128)S(1)}, u32[]{:S(2)}, u32[]{:S(2)}) collective-permute-start(f32[4,128,256]{2,1,0:T(8,128)S(1)} %get-tuple-element.8), channel_id=1, source_target_pairs={{0,48},{8,56},{16,0},{24,8},{32,16},{40,24},{48,32},{56,40},{64,11... | collective-permute-start | bytes 1572872 | tf_op jit(solution)/shard_map/ppermute | solution.py:38
  100.1 17.0 %all-to-all-start.2 = ((f32[4,128,256]{2,1,0:T(8,128)}), f32[4,128,256]{2,1,0:T(8,128)S(1)}, u32[]{:S(2)}, u32[]{:S(2)}) async-start(f32[4,128,256]{2,1,0:T(8,128)} %fusion), calls=%async_computation.2 | async-start | bytes 1048576 | tf_op jit(solution)/shard_map/all_to_all | solution.py:30
  118.3 1.4 collective-permute-start.15
  119.8 6.5 %collective-permute-start.16 = (f32[32,256]{1,0:T(8,128)S(1)}, f32[32,256]{1,0:T(8,128)S(1)}, u32[]{:S(2)}, u32[]{:S(2)}) collective-permute-start(f32[32,256]{1,0:T(8,128)S(1)} %get-tuple-element.11), channel_id=1, source_target_pairs={{0,2},{1,3},{2,0},{3,1},{4,6},{5,7},{6,4},{7,5},{8,10},{9,11},{10,... | collective-permute-start | bytes 98312 | tf_op jit(solution)/shard_map/ppermute | solution.py:46
  123.0 5.1 %collective-permute-start.17 = (f32[32,256]{1,0:T(8,128)S(1)}, f32[32,256]{1,0:T(8,128)S(1)}, u32[]{:S(2)}, u32[]{:S(2)}) collective-permute-start(f32[32,256]{1,0:T(8,128)S(1)} %get-tuple-element.13), channel_id=1, source_target_pairs={{0,1},{1,2},{2,3},{3,0},{4,5},{5,6},{6,7},{7,4},{8,9},{9,10},{10,1... | collective-permute-start | bytes 98312 | tf_op jit(solution)/shard_map/ppermute | solution.py:46
  123.6 4.6 %collective-permute-start.18 = (f32[32,256]{1,0:T(8,128)S(1)}, f32[32,256]{1,0:T(8,128)S(1)}, u32[]{:S(2)}, u32[]{:S(2)}) collective-permute-start(f32[32,256]{1,0:T(8,128)S(1)} %get-tuple-element.12), channel_id=1, source_target_pairs={{0,3},{1,0},{2,1},{3,2},{4,7},{5,4},{6,5},{7,6},{8,11},{9,8},{10,9... | collective-permute-start | bytes 98312 | tf_op jit(solution)/shard_map/ppermute | solution.py:46
  128.2 5.5 %collective-permute-start.19 = (f32[32,256]{1,0:T(8,128)S(1)}, f32[32,256]{1,0:T(8,128)S(1)}, u32[]{:S(2)}, u32[]{:S(2)}) collective-permute-start(f32[32,256]{1,0:T(8,128)S(1)} %add_add_fusion.1), channel_id=1, source_target_pairs={{0,32},{8,40},{16,48},{24,56},{32,0},{40,8},{48,16},{56,24},{64,96... | collective-permute-start | bytes 98312 | tf_op jit(solution)/shard_map/ppermute | solution.py:38
  128.6 5.1 %collective-permute-start.20 = (f32[32,256]{1,0:T(8,128)S(1)}, f32[32,256]{1,0:T(8,128)S(1)}, u32[]{:S(2)}, u32[]{:S(2)}) collective-permute-start(f32[32,256]{1,0:T(8,128)S(1)} %add_add_fusion.1), channel_id=1, source_target_pairs={{0,16},{8,24},{16,32},{24,40},{32,48},{40,56},{48,0},{56,8},{64,80... | collective-permute-start | bytes 98312 | tf_op jit(solution)/shard_map/ppermute | solution.py:38
  130.0 4.2 %collective-permute-start.21 = (f32[32,256]{1,0:T(8,128)S(1)}, f32[32,256]{1,0:T(8,128)S(1)}, u32[]{:S(2)}, u32[]{:S(2)}) collective-permute-start(f32[32,256]{1,0:T(8,128)S(1)} %add_add_fusion.1), channel_id=1, source_target_pairs={{0,48},{8,56},{16,0},{24,8},{32,16},{40,24},{48,32},{56,40},{64,11... | collective-permute-start | bytes 98312 | tf_op jit(solution)/shard_map/ppermute | solution.py:38
  134.3 7.3 %collective-permute-start.22 = (f32[32,256]{1,0:T(8,128)S(1)}, f32[32,256]{1,0:T(8,128)S(1)}, u32[]{:S(2)}, u32[]{:S(2)}) collective-permute-start(f32[32,256]{1,0:T(8,128)S(1)} %add_add_fusion), channel_id=1, source_target_pairs={{0,4},{1,5},{2,6},{3,7},{4,0},{5,1},{6,2},{7,3},{8,12},{9,13},{10,... | collective-permute-start | bytes 98312 | tf_op jit(solution)/shard_map/ppermute | solution.py:50
  153.7 1.3 collective-permute-start.23
  155.0 9.8 %copy-start.11 = (f32[2,32,256]{2,1,0:T(8,128)}, f32[2,32,256]{2,1,0:T(8,128)S(1)}, u32[]{:S(2)}) copy-start(f32[2,32,256]{2,1,0:T(8,128)S(1)} %pad_maximum_fusion.1.piece0) | copy-start | bytes 196612
  155.0 6.4 %collective-permute-start.24 = (f32[2,32,256]{2,1,0:T(8,128)S(1)}, f32[2,32,256]{2,1,0:T(8,128)S(1)}, u32[]{:S(2)}, u32[]{:S(2)}) collective-permute-start(f32[2,32,256]{2,1,0:T(8,128)S(1)} %pad_maximum_fusion.1.piece0), channel_id=1, source_target_pairs={{0,3},{1,0},{2,1},{3,2},{4,7},{5,4},{6,5},{7,6},{8,11},{9,8},{10,9... | collective-permute-start | bytes 196616 | tf_op jit(solution)/shard_map/ppermute | solution.py:46
  158.4 6.0 %collective-permute-start.25 = (f32[2,32,256]{2,1,0:T(8,128)S(1)}, f32[2,32,256]{2,1,0:T(8,128)S(1)}, u32[]{:S(2)}, u32[]{:S(2)}) collective-permute-start(f32[2,32,256]{2,1,0:T(8,128)S(1)} %pad_maximum_fusion.1.piece0), channel_id=1, source_target_pairs={{0,2},{1,3},{2,0},{3,1},{4,6},{5,7},{6,4},{7,5},{8,10},{9,11},{10,... | collective-permute-start | bytes 196616 | tf_op jit(solution)/shard_map/ppermute | solution.py:46
  158.4 6.4 %collective-permute-start.26 = (f32[2,32,256]{2,1,0:T(8,128)S(1)}, f32[2,32,256]{2,1,0:T(8,128)S(1)}, u32[]{:S(2)}, u32[]{:S(2)}) collective-permute-start(f32[2,32,256]{2,1,0:T(8,128)S(1)} %pad_maximum_fusion.1.piece0), channel_id=1, source_target_pairs={{0,1},{1,2},{2,3},{3,0},{4,5},{5,6},{6,7},{7,4},{8,9},{9,10},{10,1... | collective-permute-start | bytes 196616 | tf_op jit(solution)/shard_map/ppermute | solution.py:46
  161.4 3.4 %copy-start.15 = (f32[2,32,256]{2,1,0:T(8,128)}, f32[2,32,256]{2,1,0:T(8,128)S(1)}, u32[]{:S(2)}) copy-start(f32[2,32,256]{2,1,0:T(8,128)S(1)} %collective-permute-done.24.piece1) | copy-start | bytes 196612
  164.4 0.6 copy-start.16
  164.8 0.6 copy-start.17

commit v3 on v0

--- a/solution.py
+++ b/solution.py
@@ -73,7 +73,7 @@
 def col_spot(place, cp):
     r = place[0]
     zk, xk, cx = ((cp >> 3) - (r >> 3)) & 3, ((cp >> 1) - (r >> 1)) & 3, (cp ^ r) & 1
-    return (cx * N_X + xk) * N_ZH + zk
+    return cx * N_X * N_ZH, xk, zk
 
 
 def mirror_kernel(place, counts, rows, cols, blocks, *refs):
@@ -83,7 +83,8 @@
         vectors[k * N_ZL : (k + 1) * N_ZL] = piece[...]
 
     def add(tile, rp, cp):
-        acc[col_spot(place, cp)] += lax.dot_general(
+        base, xk, zk = col_spot(place, cp)
+        acc[base + xk * N_ZH + zk] += lax.dot_general(
             tile, vectors[row_spot(place, rp)], (((0,), (0,)), ((), ())), preferred_element_type=F32
         )
 
@@ -93,14 +94,15 @@
 
 
 def direct_kernel(place, counts, rows, cols, blocks, *refs):
-    n = N_CORE * N_X
+    n = N_CORE * N_ZH
     pieces, outs, vectors, acc = refs[:n], refs[n : n + N_Y], refs[-2], refs[-1]
     acc[...] = jnp.zeros_like(acc)
     for k, piece in enumerate(pieces):
-        vectors[k * N_ZH : (k + 1) * N_ZH] = piece[...]
+        vectors[k * N_X : (k + 1) * N_X] = piece[...]
 
     def add(tile, rp, cp):
-        acc[row_spot(place, rp)] += jnp.dot(tile, vectors[col_spot(place, cp)], preferred_element_type=F32)
+        base, xk, zk = col_spot(place, cp)
+        acc[row_spot(place, rp)] += jnp.dot(tile, vectors[base + zk * N_X + xk], preferred_element_type=F32)
 
     slot_loop(counts, rows, cols, blocks, add)
     for k, out in enumerate(outs):
@@ -237,9 +239,9 @@
     place = jnp.stack([lax.axis_index("row"), lax.axis_index("col")]).astype(jnp.int32)
     scalars = (place, counts, block_rows, block_cols)
     first = jnp.stack([trials, to_zl(trials)])
-    zs = jnp.stack([trials] + [to_z(trials, -k) for k in range(1, N_ZH)])
+    xs = jnp.stack([trials] + [to_x(trials, -k) for k in range(1, N_X)])
     row_pieces = [first] + [to_y(first, -k) for k in range(1, N_Y)]
-    col_pieces = [zs] + [to_x(zs, -k) for k in range(1, N_X)]
+    col_pieces = [xs] + [to_z(xs, -k) for k in range(1, N_ZH)]
     col_keep, col_send = products_of(mirror_kernel, scalars, blocks[0], row_pieces, N_CORE, N_X * N_ZH)
     col_pieces = col_pieces + [to_core(v) for v in col_pieces]
     row_outs = products_of(direct_kernel, scalars, blocks[0], col_pieces, N_Y, N_ZL)

time: 174 us -> 181 us (1.040)
  the two profiles are of different devices: /device:TPU:1 before, /device:TPU:2 now
where the time goes in v3:
time: 181 us; the launch traced here: 178 us
  waiting for transfers between devices  82.7 us (46%)
  starting transfers between devices  61.1 us (34%)
  Pallas kernels  26.2 us (14%)
  other arithmetic  3.76 us (2%)
  local copies, waits for them, and re-layouts  2.61 us (1%)
    ppermute x9, waiting for transfers between devices, to_z(): return lax.ppermute(v, 'row', row_pairs(lambda z, x, c: (z + k, x, c)))  32.8 us
    ppermute x9, starting transfers between devices, to_z(): return lax.ppermute(v, 'row', row_pairs(lambda z, x, c: (z + k, x, c)))  26.4 us
    ppermute x12, waiting for transfers between devices, to_y(): lax.ppermute(v, 'col', [(col_at(zl, y), col_at(zl, y + k)) for zl in rang...  21.3 us
    ppermute x9, waiting for transfers between devices, to_x(): return lax.ppermute(v, 'row', row_pairs(lambda z, x, c: (z, x + k, c)))  18.4 us
    ppermute x12, starting transfers between devices, to_y(): lax.ppermute(v, 'col', [(col_at(zl, y), col_at(zl, y + k)) for zl in rang...  16 us
    pallas_call x1, Pallas kernels, factor_and_basis(): pl.pallas_call(factor_kernel, out_shape=(jax.ShapeDtypeStruct((edge, size...  15 us
    ppermute x9, starting transfers between devices, to_x(): return lax.ppermute(v, 'row', row_pairs(lambda z, x, c: (z, x + k, c)))  11.4 us
    pallas_call x2, Pallas kernels, products_of(): pl.pallas_call(kernel, out_shape=(jax.ShapeDtypeStruct((out_blocks, edge,...  11.1 us
  transfers between devices with their start and end apart: 40, of which 29 were waited for; matrix products, arithmetic and copies ran while one was open for 2% of the time, Pallas kernels for 3%

profile of v3, /device:TPU:2, one launch (start us, length us, event | category | flops | bytes accessed | tf_op | source)
XLA Modules:
  0.0 178.4 jit_solution(13595103749628865718)
XLA Ops:
  0.6 2.0 %collective-permute-start.14 = (bf16[128,256]{1,0:T(8,128)(2,1)}, bf16[128,256]{1,0:T(8,128)(2,1)S(1)}, u32[]{:S(2)}, u32[]{:S(2)}) collective-permute-start(bf16[128,256]{1,0:T(8,128)(2,1)} %param.9), channel_id=1, source_target_pairs={{0,4},{1,5},{2,6},{3,7},{4,0},{5,1},{6,2},{7,3},{8,12},{9,13},{10,... | collective-permute-start | bytes 196616 | tf_op jit(solution)/shard_map/ppermute | solution.py:45
  2.6 2.6 %collective-permute-done.14 = bf16[128,256]{1,0:T(8,128)(2,1)S(1)} collective-permute-done((bf16[128,256]{1,0:T(8,128)(2,1)}, bf16[128,256]{1,0:T(8,128)(2,1)S(1)}, u32[]{:S(2)}, u32[]{:S(2)}) %collective-permute-start.14) | collective-permute-done | bytes 65568 | tf_op jit(solution)/shard_map/ppermute | solution.py:45
  6.1 3.1 %collective-permute-start.15 = (bf16[2,128,256]{2,1,0:T(8,128)(2,1)S(1)}, bf16[2,128,256]{2,1,0:T(8,128)(2,1)S(1)}, u32[]{:S(2)}, u32[]{:S(2)}) collective-permute-start(bf16[2,128,256]{2,1,0:T(8,128)(2,1)S(1)} %pad_maximum_fusion.1.refs_0_), channel_id=1, source_target_pairs={{0,3},{1,0},{2,1},{3,2},{4,7},{5,4},{6,5},{7,6},{8,11},{9,8},{10,9... | collective-permute-start | bytes 393224 | tf_op jit(solution)/shard_map/ppermute | solution.py:41
  12.1 1.7 collective-permute-done.15.refs_1_
  13.8 2.2 %collective-permute-done.16.refs_2_ = bf16[2,128,256]{2,1,0:T(8,128)(2,1)S(1)} collective-permute-done((bf16[2,128,256]{2,1,0:T(8,128)(2,1)S(1)}, bf16[2,128,256]{2,1,0:T(8,128)(2,1)S(1)}, u32[]{:S(2)}, u32[]{:S(2)}) %collective-permute-start.16) | collective-permute-done | bytes 131104 | tf_op jit(solution)/shard_map/ppermute | solution.py:41
  16.1 1.4 collective-permute-done.17.refs_3_
  18.1 6.1 %shard_map.69 = (f32[16,128,256]{2,1,0:T(8,128)}, f32[16,128,256]{2,1,0:T(8,128)}) custom-call(s32[2]{0:T(128)} %pad_add_fusion.place, s32[1,1]{1,0:T(1,128)S(6)} %copy.7.counts, s32[1,64]{1,0:T(1,128)} %rows.3, s32[1,64]{1,0:T(1,128)} %cols.3, bf16[64,128,128]{2,1,0:T(8,128)(2,1)} %bitcast.34, bf16[2,128,256]{2,1,0:T(8,128)(2,1)} %copy-done.3, ...), custom_call_target="tpu_custom_call" | custom-call | flops 536870912 | bytes 6815744 | tf_op jit(solution)/shard_map/pallas_call | solution.py:117
  24.2 1.6 collective-permute-start.2
  25.8 1.4 collective-permute-start.1
  27.2 1.9 %collective-permute-start = (bf16[128,256]{1,0:T(8,128)(2,1)S(1)}, bf16[128,256]{1,0:T(8,128)(2,1)S(1)}, u32[]{:S(2)}, u32[]{:S(2)}) collective-permute-start(bf16[128,256]{1,0:T(8,128)(2,1)S(1)} %copy-done.6), channel_id=1, source_target_pairs={{0,48},{8,56},{16,0},{24,8},{32,16},{40,24},{48,32},{56,40},{64,11... | collective-permute-start | bytes 196616 | tf_op jit(solution)/shard_map/ppermute | solution.py:33
  29.1 3.1 %collective-permute-done.1 = bf16[128,256]{1,0:T(8,128)(2,1)S(1)} collective-permute-done((bf16[128,256]{1,0:T(8,128)(2,1)S(1)}, bf16[128,256]{1,0:T(8,128)(2,1)S(1)}, u32[]{:S(2)}, u32[]{:S(2)}) %collective-permute-start.1) | collective-permute-done | bytes 65568 | tf_op jit(solution)/shard_map/ppermute | solution.py:33
  32.5 4.6 %collective-permute-start.3 = (bf16[4,128,256]{2,1,0:T(8,128)(2,1)S(1)}, bf16[4,128,256]{2,1,0:T(8,128)(2,1)S(1)}, u32[]{:S(2)}, u32[]{:S(2)}) collective-permute-start(bf16[4,128,256]{2,1,0:T(8,128)(2,1)S(1)} %pad_maximum_fusion.refs_0_), channel_id=1, source_target_pairs={{0,192},{8,200},{16,208},{24,216},{32,224},{40,232},{48,240},{56,2... | collective-permute-start | bytes 786440 | tf_op jit(solution)/shard_map/ppermute | solution.py:29
  37.1 1.5 collective-permute-start.4
  38.6 2.8 %collective-permute-start.5 = (bf16[4,128,256]{2,1,0:T(8,128)(2,1)S(1)}, bf16[4,128,256]{2,1,0:T(8,128)(2,1)S(1)}, u32[]{:S(2)}, u32[]{:S(2)}) collective-permute-start(bf16[4,128,256]{2,1,0:T(8,128)(2,1)S(1)} %pad_maximum_fusion.refs_0_), channel_id=1, source_target_pairs={{0,64},{8,72},{16,80},{24,88},{32,96},{40,104},{48,112},{56,120},{... | collective-permute-start | bytes 786440 | tf_op jit(solution)/shard_map/ppermute | solution.py:29
  41.4 17.5 %collective-permute-done.3.refs_1_ = bf16[4,128,256]{2,1,0:T(8,128)(2,1)S(1)} collective-permute-done((bf16[4,128,256]{2,1,0:T(8,128)(2,1)S(1)}, bf16[4,128,256]{2,1,0:T(8,128)(2,1)S(1)}, u32[]{:S(2)}, u32[]{:S(2)}) %collective-permute-start.3) | collective-permute-done | bytes 262176 | tf_op jit(solution)/shard_map/ppermute | solution.py:29
  61.9 5.0 %shard_map.68 = (f32[2,128,256]{2,1,0:T(8,128)}, f32[2,128,256]{2,1,0:T(8,128)}, f32[2,128,256]{2,1,0:T(8,128)}, f32[2,128,256]{2,1,0:T(8,128)}) custom-call(s32[2]{0:T(128)} %pad_add_fusion.place, s32[1,1]{1,0:T(1,128)S(6)} %copy.7.counts, s32[1,64]{1,0:T(1,128)} %rows.3, s32[1,64]{1,0:T(1,128)} %cols.3, bf16[64,128,128]{2,1,0:T(8,128)(2,1)} %bitcast.35, ...), custom_call_target="tpu_custom_call" | custom-call | flops 536870912 | bytes 5242880 | tf_op jit(solution)/shard_map/pallas_call | solution.py:117
  67.0 3.2 %collective-permute-start.12 = (f32[2,128,256]{2,1,0:T(8,128)}, f32[2,128,256]{2,1,0:T(8,128)S(1)}, u32[]{:S(2)}, u32[]{:S(2)}) collective-permute-start(f32[2,128,256]{2,1,0:T(8,128)} %get-tuple-element.11), channel_id=1, source_target_pairs={{0,3},{1,0},{2,1},{3,2},{4,7},{5,4},{6,5},{7,6},{8,11},{9,8},{10,9... | collective-permute-start | bytes 786440 | tf_op jit(solution)/shard_map/ppermute | solution.py:41
  70.2 1.4 collective-permute-start.10
  71.6 1.9 %add.100 = f32[16,128,256]{2,1,0:T(8,128)S(1)} add(f32[16,128,256]{2,1,0:T(8,128)S(1)} %copy-done, f32[16,128,256]{2,1,0:T(8,128)} %collective-permute-done.18) | non-fusion elementwise | flops 524288 | bytes 6291456 | tf_op jit(solution)/shard_map/add | solution.py:248
  73.7 1.7 collective-permute-start.19
  76.0 6.6 %collective-permute-done.11 = f32[2,128,256]{2,1,0:T(8,128)S(1)} collective-permute-done((f32[2,128,256]{2,1,0:T(8,128)}, f32[2,128,256]{2,1,0:T(8,128)S(1)}, u32[]{:S(2)}, u32[]{:S(2)}) %collective-permute-start.11) | collective-permute-done | bytes 262176 | tf_op jit(solution)/shard_map/ppermute | solution.py:41
  83.0 4.4 %collective-permute-start.13 = (f32[128,256]{1,0:T(8,128)S(1)}, f32[128,256]{1,0:T(8,128)S(1)}, u32[]{:S(2)}, u32[]{:S(2)}) collective-permute-start(f32[128,256]{1,0:T(8,128)S(1)} %slice_bitcast_fusion.4), channel_id=1, source_target_pairs={{0,4},{1,5},{2,6},{3,7},{4,0},{5,1},{6,2},{7,3},{8,12},{9,13},{10,... | collective-permute-start | bytes 393224 | tf_op jit(solution)/shard_map/ppermute | solution.py:45
  87.4 2.7 %collective-permute-done.19 = f32[4,128,256]{2,1,0:T(8,128)S(1)} collective-permute-done((f32[4,128,256]{2,1,0:T(8,128)S(1)}, f32[4,128,256]{2,1,0:T(8,128)S(1)}, u32[]{:S(2)}, u32[]{:S(2)}) %collective-permute-start.19) | collective-permute-done | bytes 524320 | tf_op jit(solution)/shard_map/ppermute | solution.py:33
  90.1 7.7 %collective-permute-done.20 = f32[4,128,256]{2,1,0:T(8,128)S(1)} collective-permute-done((f32[4,128,256]{2,1,0:T(8,128)S(1)}, f32[4,128,256]{2,1,0:T(8,128)S(1)}, u32[]{:S(2)}, u32[]{:S(2)}) %collective-permute-start.20) | collective-permute-done | bytes 524320 | tf_op jit(solution)/shard_map/ppermute | solution.py:33
  97.8 1.0 collective-permute-done.21
  99.0 6.7 %collective-permute-start.22 = (f32[128,256]{1,0:T(8,128)S(1)}, f32[128,256]{1,0:T(8,128)S(1)}, u32[]{:S(2)}, u32[]{:S(2)}) collective-permute-start(f32[128,256]{1,0:T(8,128)S(1)} %get-tuple-element.19), channel_id=1, source_target_pairs={{0,128},{8,136},{16,144},{24,152},{32,160},{40,168},{48,176},{56,1... | collective-permute-start | bytes 393224 | tf_op jit(solution)/shard_map/ppermute | solution.py:29
  105.7 1.9 %collective-permute-start.23 = (f32[128,256]{1,0:T(8,128)S(1)}, f32[128,256]{1,0:T(8,128)S(1)}, u32[]{:S(2)}, u32[]{:S(2)}) collective-permute-start(f32[128,256]{1,0:T(8,128)S(1)} %get-tuple-element.18), channel_id=1, source_target_pairs={{0,64},{8,72},{16,80},{24,88},{32,96},{40,104},{48,112},{56,120},{... | collective-permute-start | bytes 393224 | tf_op jit(solution)/shard_map/ppermute | solution.py:29
  107.5 2.3 %collective-permute-start.24 = (f32[128,256]{1,0:T(8,128)S(1)}, f32[128,256]{1,0:T(8,128)S(1)}, u32[]{:S(2)}, u32[]{:S(2)}) collective-permute-start(f32[128,256]{1,0:T(8,128)S(1)} %get-tuple-element.17), channel_id=1, source_target_pairs={{0,192},{8,200},{16,208},{24,216},{32,224},{40,232},{48,240},{56,2... | collective-permute-start | bytes 393224 | tf_op jit(solution)/shard_map/ppermute | solution.py:29
  109.8 2.3 %collective-permute-done.22 = f32[128,256]{1,0:T(8,128)S(1)} collective-permute-done((f32[128,256]{1,0:T(8,128)S(1)}, f32[128,256]{1,0:T(8,128)S(1)}, u32[]{:S(2)}, u32[]{:S(2)}) %collective-permute-start.22) | collective-permute-done | bytes 131104 | tf_op jit(solution)/shard_map/ppermute | solution.py:29
  112.1 4.4 %collective-permute-done.23 = f32[128,256]{1,0:T(8,128)S(1)} collective-permute-done((f32[128,256]{1,0:T(8,128)S(1)}, f32[128,256]{1,0:T(8,128)S(1)}, u32[]{:S(2)}, u32[]{:S(2)}) %collective-permute-start.23) | collective-permute-done | bytes 131104 | tf_op jit(solution)/shard_map/ppermute | solution.py:29
  116.5 3.4 %collective-permute-done.24 = f32[128,256]{1,0:T(8,128)S(1)} collective-permute-done((f32[128,256]{1,0:T(8,128)S(1)}, f32[128,256]{1,0:T(8,128)S(1)}, u32[]{:S(2)}, u32[]{:S(2)}) %collective-permute-start.24) | collective-permute-done | bytes 131104 | tf_op jit(solution)/shard_map/ppermute | solution.py:29
  120.5 1.3 collective-permute-done.25
  121.9 3.2 %collective-permute-start.28 = (f32[32,256]{1,0:T(8,128)S(1)}, f32[32,256]{1,0:T(8,128)S(1)}, u32[]{:S(2)}, u32[]{:S(2)}) collective-permute-start(f32[32,256]{1,0:T(8,128)S(1)} %get-tuple-element.21), channel_id=1, source_target_pairs={{0,3},{1,0},{2,1},{3,2},{4,7},{5,4},{6,5},{7,6},{8,11},{9,8},{10,9... | collective-permute-start | bytes 98312 | tf_op jit(solution)/shard_map/ppermute | solution.py:41
  127.0 3.5 %collective-permute-done.26 = f32[32,256]{1,0:T(8,128)S(1)} collective-permute-done((f32[32,256]{1,0:T(8,128)S(1)}, f32[32,256]{1,0:T(8,128)S(1)}, u32[]{:S(2)}, u32[]{:S(2)}) %collective-permute-start.26) | collective-permute-done | bytes 32800 | tf_op jit(solution)/shard_map/ppermute | solution.py:41
  130.7 2.0 %collective-permute-start.31 = (f32[32,256]{1,0:T(8,128)S(1)}, f32[32,256]{1,0:T(8,128)S(1)}, u32[]{:S(2)}, u32[]{:S(2)}) collective-permute-start(f32[32,256]{1,0:T(8,128)S(1)} %add_add_fusion.3), channel_id=1, source_target_pairs={{0,48},{8,56},{16,0},{24,8},{32,16},{40,24},{48,32},{56,40},{64,11... | collective-permute-start | bytes 98312 | tf_op jit(solution)/shard_map/ppermute | solution.py:33
  132.7 1.8 %collective-permute-start.29 = (f32[32,256]{1,0:T(8,128)S(1)}, f32[32,256]{1,0:T(8,128)S(1)}, u32[]{:S(2)}, u32[]{:S(2)}) collective-permute-start(f32[32,256]{1,0:T(8,128)S(1)} %add_add_fusion.3), channel_id=1, source_target_pairs={{0,32},{8,40},{16,48},{24,56},{32,0},{40,8},{48,16},{56,24},{64,96... | collective-permute-start | bytes 98312 | tf_op jit(solution)/shard_map/ppermute | solution.py:33
  135.3 2.8 %collective-permute-done.29 = f32[32,256]{1,0:T(8,128)S(1)} collective-permute-done((f32[32,256]{1,0:T(8,128)S(1)}, f32[32,256]{1,0:T(8,128)S(1)}, u32[]{:S(2)}, u32[]{:S(2)}) %collective-permute-start.29) | collective-permute-done | bytes 32800 | tf_op jit(solution)/shard_map/ppermute | solution.py:33
  138.2 3.9 %collective-permute-done.32 = f32[32,256]{1,0:T(8,128)S(1)} collective-permute-done((f32[32,256]{1,0:T(8,128)S(1)}, f32[32,256]{1,0:T(8,128)S(1)}, u32[]{:S(2)}, u32[]{:S(2)}) %collective-permute-start.32) | collective-permute-done | bytes 32800 | tf_op jit(solution)/shard_map/ppermute | solution.py:45
  142.1 1.2 collective-permute-start.34
  143.3 3.0 %collective-permute-start.35 = (f32[32,256]{1,0:T(8,128)S(1)}, f32[32,256]{1,0:T(8,128)S(1)}, u32[]{:S(2)}, u32[]{:S(2)}) collective-permute-start(f32[32,256]{1,0:T(8,128)S(1)} %add.124), channel_id=1, source_target_pairs={{0,192},{8,200},{16,208},{24,216},{32,224},{40,232},{48,240},{56,2... | collective-permute-start | bytes 98312 | tf_op jit(solution)/shard_map/ppermute | solution.py:29
  146.3 2.5 %collective-permute-start.33 = (f32[32,256]{1,0:T(8,128)S(1)}, f32[32,256]{1,0:T(8,128)S(1)}, u32[]{:S(2)}, u32[]{:S(2)}) collective-permute-start(f32[32,256]{1,0:T(8,128)S(1)} %add.124), channel_id=1, source_target_pairs={{0,128},{8,136},{16,144},{24,152},{32,160},{40,168},{48,176},{56,1... | collective-permute-start | bytes 98312 | tf_op jit(solution)/shard_map/ppermute | solution.py:29
  148.9 5.2 %collective-permute-done.33 = f32[32,256]{1,0:T(8,128)S(1)} collective-permute-done((f32[32,256]{1,0:T(8,128)S(1)}, f32[32,256]{1,0:T(8,128)S(1)}, u32[]{:S(2)}, u32[]{:S(2)}) %collective-permute-start.33) | collective-permute-done | bytes 32800 | tf_op jit(solution)/shard_map/ppermute | solution.py:29
  154.2 1.2 collective-permute-done.36
  156.5 1.3 collective-permute-start.39
  157.8 2.5 %collective-permute-done.37.piece1 = f32[2,32,256]{2,1,0:T(8,128)S(1)} collective-permute-done((f32[2,32,256]{2,1,0:T(8,128)S(1)}, f32[2,32,256]{2,1,0:T(8,128)S(1)}, u32[]{:S(2)}, u32[]{:S(2)}) %collective-permute-start.37) | collective-permute-done | bytes 65568 | tf_op jit(solution)/shard_map/ppermute | solution.py:41
  160.3 1.2 collective-permute-done.38.piece2
  161.5 1.2 collective-permute-done.39.piece3
  163.3 15.0 %factor.1 = (f32[128,256]{1,0:T(8,128)}, f32[256,256]{1,0:T(8,128)}) custom-call(s32[2]{0:T(128)} %pad_add_fusion.place, f32[2,32,256]{2,1,0:T(8,128)} %copy-done.5, f32[2,32,256]{2,1,0:T(8,128)} %copy-done.16, f32[2,32,256]{2,1,0:T(8,128)} %copy-done.17, f32[2,32,256]{2,1,0:T(8,128)} %copy-done.18, f32[128,256]{1,0:T(8,128)} %copy-done.1), custom_call_target="tpu_custom_call" | custom-call | tf_op jit(solution)/shard_map/factor/pallas_call | solution.py:211
  (92 shorter events, 14.0 us)
Async XLA Ops:
  0.6 23.6 %copy-start.6 = (bf16[128,256]{1,0:T(8,128)(2,1)S(1)}, bf16[128,256]{1,0:T(8,128)(2,1)}, u32[]{:S(2)}) copy-start(bf16[128,256]{1,0:T(8,128)(2,1)} %param.9) | copy-start | bytes 196612
  0.6 4.6 %collective-permute-start.14 = (bf16[128,256]{1,0:T(8,128)(2,1)}, bf16[128,256]{1,0:T(8,128)(2,1)S(1)}, u32[]{:S(2)}, u32[]{:S(2)}) collective-permute-start(bf16[128,256]{1,0:T(8,128)(2,1)} %param.9), channel_id=1, source_target_pairs={{0,4},{1,5},{2,6},{3,7},{4,0},{5,1},{6,2},{7,3},{8,12},{9,13},{10,... | collective-permute-start | bytes 196616 | tf_op jit(solution)/shard_map/ppermute | solution.py:45
  6.1 11.4 %copy-start.3 = (bf16[2,128,256]{2,1,0:T(8,128)(2,1)}, bf16[2,128,256]{2,1,0:T(8,128)(2,1)S(1)}, u32[]{:S(2)}) copy-start(bf16[2,128,256]{2,1,0:T(8,128)(2,1)S(1)} %pad_maximum_fusion.1.refs_0_) | copy-start | bytes 393220
  6.1 7.7 %collective-permute-start.15 = (bf16[2,128,256]{2,1,0:T(8,128)(2,1)S(1)}, bf16[2,128,256]{2,1,0:T(8,128)(2,1)S(1)}, u32[]{:S(2)}, u32[]{:S(2)}) collective-permute-start(bf16[2,128,256]{2,1,0:T(8,128)(2,1)S(1)} %pad_maximum_fusion.1.refs_0_), channel_id=1, source_target_pairs={{0,3},{1,0},{2,1},{3,2},{4,7},{5,4},{6,5},{7,6},{8,11},{9,8},{10,9... | collective-permute-start | bytes 393224 | tf_op jit(solution)/shard_map/ppermute | solution.py:41
  9.2 6.9 %collective-permute-start.16 = (bf16[2,128,256]{2,1,0:T(8,128)(2,1)S(1)}, bf16[2,128,256]{2,1,0:T(8,128)(2,1)S(1)}, u32[]{:S(2)}, u32[]{:S(2)}) collective-permute-start(bf16[2,128,256]{2,1,0:T(8,128)(2,1)S(1)} %pad_maximum_fusion.1.refs_0_), channel_id=1, source_target_pairs={{0,2},{1,3},{2,0},{3,1},{4,6},{5,7},{6,4},{7,5},{8,10},{9,11},{10,... | collective-permute-start | bytes 393224 | tf_op jit(solution)/shard_map/ppermute | solution.py:41
  9.8 7.7 %collective-permute-start.17 = (bf16[2,128,256]{2,1,0:T(8,128)(2,1)S(1)}, bf16[2,128,256]{2,1,0:T(8,128)(2,1)S(1)}, u32[]{:S(2)}, u32[]{:S(2)}) collective-permute-start(bf16[2,128,256]{2,1,0:T(8,128)(2,1)S(1)} %pad_maximum_fusion.1.refs_0_), channel_id=1, source_target_pairs={{0,1},{1,2},{2,3},{3,0},{4,5},{5,6},{6,7},{7,4},{8,9},{9,10},{10,1... | collective-permute-start | bytes 393224 | tf_op jit(solution)/shard_map/ppermute | solution.py:41
  13.8 3.7 %copy-start.13 = (bf16[2,128,256]{2,1,0:T(8,128)(2,1)}, bf16[2,128,256]{2,1,0:T(8,128)(2,1)S(1)}, u32[]{:S(2)}) copy-start(bf16[2,128,256]{2,1,0:T(8,128)(2,1)S(1)} %collective-permute-done.15.refs_1_) | copy-start | bytes 393220
  24.2 47.4 %collective-permute-start.18 = (f32[16,128,256]{2,1,0:T(8,128)}, f32[16,128,256]{2,1,0:T(8,128)}, u32[]{:S(2)}, u32[]{:S(2)}) collective-permute-start(f32[16,128,256]{2,1,0:T(8,128)} %get-tuple-element.13), channel_id=1, source_target_pairs={{0,8},{8,0},{16,24},{24,16},{32,40},{40,32},{48,56},{56,48},{64,72... | collective-permute-start | bytes 6291464 | tf_op jit(solution)/shard_map/ppermute | solution.py:37
  24.2 4.8 %collective-permute-start.2 = (bf16[128,256]{1,0:T(8,128)(2,1)S(1)}, bf16[128,256]{1,0:T(8,128)(2,1)S(1)}, u32[]{:S(2)}, u32[]{:S(2)}) collective-permute-start(bf16[128,256]{1,0:T(8,128)(2,1)S(1)} %copy-done.6), channel_id=1, source_target_pairs={{0,16},{8,24},{16,32},{24,40},{32,48},{40,56},{48,0},{56,8},{64,80... | collective-permute-start | bytes 196616 | tf_op jit(solution)/shard_map/ppermute | solution.py:33
  25.8 6.4 %collective-permute-start.1 = (bf16[128,256]{1,0:T(8,128)(2,1)S(1)}, bf16[128,256]{1,0:T(8,128)(2,1)S(1)}, u32[]{:S(2)}, u32[]{:S(2)}) collective-permute-start(bf16[128,256]{1,0:T(8,128)(2,1)S(1)} %copy-done.6), channel_id=1, source_target_pairs={{0,32},{8,40},{16,48},{24,56},{32,0},{40,8},{48,16},{56,24},{64,96... | collective-permute-start | bytes 196616 | tf_op jit(solution)/shard_map/ppermute | solution.py:33
  27.2 5.3 %collective-permute-start = (bf16[128,256]{1,0:T(8,128)(2,1)S(1)}, bf16[128,256]{1,0:T(8,128)(2,1)S(1)}, u32[]{:S(2)}, u32[]{:S(2)}) collective-permute-start(bf16[128,256]{1,0:T(8,128)(2,1)S(1)} %copy-done.6), channel_id=1, source_target_pairs={{0,48},{8,56},{16,0},{24,8},{32,16},{40,24},{48,32},{56,40},{64,11... | collective-permute-start | bytes 196616 | tf_op jit(solution)/shard_map/ppermute | solution.py:33
  32.5 29.4 %copy-start.2 = (bf16[4,128,256]{2,1,0:T(8,128)(2,1)}, bf16[4,128,256]{2,1,0:T(8,128)(2,1)S(1)}, u32[]{:S(2)}) copy-start(bf16[4,128,256]{2,1,0:T(8,128)(2,1)S(1)} %pad_maximum_fusion.refs_0_) | copy-start | bytes 786436
  32.5 39.1 %copy-start = (f32[16,128,256]{2,1,0:T(8,128)S(1)}, f32[16,128,256]{2,1,0:T(8,128)}, u32[]{:S(2)}) copy-start(f32[16,128,256]{2,1,0:T(8,128)} %get-tuple-element.12) | copy-start | bytes 6291460
  32.5 26.4 %collective-permute-start.3 = (bf16[4,128,256]{2,1,0:T(8,128)(2,1)S(1)}, bf16[4,128,256]{2,1,0:T(8,128)(2,1)S(1)}, u32[]{:S(2)}, u32[]{:S(2)}) collective-permute-start(bf16[4,128,256]{2,1,0:T(8,128)(2,1)S(1)} %pad_maximum_fusion.refs_0_), channel_id=1, source_target_pairs={{0,192},{8,200},{16,208},{24,216},{32,224},{40,232},{48,240},{56,2... | collective-permute-start | bytes 786440 | tf_op jit(solution)/shard_map/ppermute | solution.py:29
  37.1 21.9 %collective-permute-start.4 = (bf16[4,128,256]{2,1,0:T(8,128)(2,1)S(1)}, bf16[4,128,256]{2,1,0:T(8,128)(2,1)S(1)}, u32[]{:S(2)}, u32[]{:S(2)}) collective-permute-start(bf16[4,128,256]{2,1,0:T(8,128)(2,1)S(1)} %pad_maximum_fusion.refs_0_), channel_id=1, source_target_pairs={{0,128},{8,136},{16,144},{24,152},{32,160},{40,168},{48,176},{56,1... | collective-permute-start | bytes 786440 | tf_op jit(solution)/shard_map/ppermute | solution.py:29
  38.6 20.9 %collective-permute-start.5 = (bf16[4,128,256]{2,1,0:T(8,128)(2,1)S(1)}, bf16[4,128,256]{2,1,0:T(8,128)(2,1)S(1)}, u32[]{:S(2)}, u32[]{:S(2)}) collective-permute-start(bf16[4,128,256]{2,1,0:T(8,128)(2,1)S(1)} %pad_maximum_fusion.refs_0_), channel_id=1, source_target_pairs={{0,64},{8,72},{16,80},{24,88},{32,96},{40,104},{48,112},{56,120},{... | collective-permute-start | bytes 786440 | tf_op jit(solution)/shard_map/ppermute | solution.py:29
  41.4 18.1 %collective-permute-start.6 = (bf16[4,128,256]{2,1,0:T(8,128)(2,1)S(1)}, bf16[4,128,256]{2,1,0:T(8,128)(2,1)S(1)}, u32[]{:S(2)}, u32[]{:S(2)}) collective-permute-start(bf16[4,128,256]{2,1,0:T(8,128)(2,1)S(1)} %pad_maximum_fusion.refs_0_), channel_id=1, source_target_pairs={{0,8},{8,0},{16,24},{24,16},{32,40},{40,32},{48,56},{56,48},{64,72... | collective-permute-start | bytes 786440 | tf_op jit(solution)/shard_map/ppermute | solution.py:37
  58.9 1.5 collective-permute-start.7
  59.0 1.9 %collective-permute-start.8 = (bf16[4,128,256]{2,1,0:T(8,128)(2,1)S(1)}, bf16[4,128,256]{2,1,0:T(8,128)(2,1)S(1)}, u32[]{:S(2)}, u32[]{:S(2)}) collective-permute-start(bf16[4,128,256]{2,1,0:T(8,128)(2,1)S(1)} %collective-permute-done.4.refs_2_), channel_id=1, source_target_pairs={{0,8},{8,0},{16,24},{24,16},{32,40},{40,32},{48,56},{56,48},{64,72... | collective-permute-start | bytes 786440 | tf_op jit(solution)/shard_map/ppermute | solution.py:37
  59.5 2.4 %collective-permute-start.9 = (bf16[4,128,256]{2,1,0:T(8,128)(2,1)S(1)}, bf16[4,128,256]{2,1,0:T(8,128)(2,1)}, u32[]{:S(2)}, u32[]{:S(2)}) collective-permute-start(bf16[4,128,256]{2,1,0:T(8,128)(2,1)S(1)} %collective-permute-done.5.refs_3_), channel_id=1, source_target_pairs={{0,8},{8,0},{16,24},{24,16},{32,40},{40,32},{48,56},{56,48},{64,72... | collective-permute-start | bytes 786440 | tf_op jit(solution)/shard_map/ppermute | solution.py:37
  67.0 15.6 %collective-permute-start.11 = (f32[2,128,256]{2,1,0:T(8,128)}, f32[2,128,256]{2,1,0:T(8,128)S(1)}, u32[]{:S(2)}, u32[]{:S(2)}) collective-permute-start(f32[2,128,256]{2,1,0:T(8,128)} %get-tuple-element.10), channel_id=1, source_target_pairs={{0,1},{1,2},{2,3},{3,0},{4,5},{5,6},{6,7},{7,4},{8,9},{9,10},{10,1... | collective-permute-start | bytes 786440 | tf_op jit(solution)/shard_map/ppermute | solution.py:41
  67.0 15.9 %collective-permute-start.12 = (f32[2,128,256]{2,1,0:T(8,128)}, f32[2,128,256]{2,1,0:T(8,128)S(1)}, u32[]{:S(2)}, u32[]{:S(2)}) collective-permute-start(f32[2,128,256]{2,1,0:T(8,128)} %get-tuple-element.11), channel_id=1, source_target_pairs={{0,3},{1,0},{2,1},{3,2},{4,7},{5,4},{6,5},{7,6},{8,11},{9,8},{10,9... | collective-permute-start | bytes 786440 | tf_op jit(solution)/shard_map/ppermute | solution.py:41
  70.2 12.7 %collective-permute-start.10 = (f32[2,128,256]{2,1,0:T(8,128)}, f32[2,128,256]{2,1,0:T(8,128)S(1)}, u32[]{:S(2)}, u32[]{:S(2)}) collective-permute-start(f32[2,128,256]{2,1,0:T(8,128)} %get-tuple-element.9), channel_id=1, source_target_pairs={{0,2},{1,3},{2,0},{3,1},{4,6},{5,7},{6,4},{7,5},{8,10},{9,11},{10,... | collective-permute-start | bytes 786440 | tf_op jit(solution)/shard_map/ppermute | solution.py:41
  73.5 9.4 %copy-start.4 = (f32[2,128,256]{2,1,0:T(8,128)S(1)}, f32[2,128,256]{2,1,0:T(8,128)}, u32[]{:S(2)}) copy-start(f32[2,128,256]{2,1,0:T(8,128)} %get-tuple-element.8) | copy-start | bytes 786436
  73.7 16.4 %collective-permute-start.19 = (f32[4,128,256]{2,1,0:T(8,128)S(1)}, f32[4,128,256]{2,1,0:T(8,128)S(1)}, u32[]{:S(2)}, u32[]{:S(2)}) collective-permute-start(f32[4,128,256]{2,1,0:T(8,128)S(1)} %get-tuple-element.16), channel_id=1, source_target_pairs={{0,32},{8,40},{16,48},{24,56},{32,0},{40,8},{48,16},{56,24},{64,96... | collective-permute-start | bytes 1572872 | tf_op jit(solution)/shard_map/ppermute | solution.py:33
  75.4 22.3 %collective-permute-start.20 = (f32[4,128,256]{2,1,0:T(8,128)S(1)}, f32[4,128,256]{2,1,0:T(8,128)S(1)}, u32[]{:S(2)}, u32[]{:S(2)}) collective-permute-start(f32[4,128,256]{2,1,0:T(8,128)S(1)} %get-tuple-element.15), channel_id=1, source_target_pairs={{0,16},{8,24},{16,32},{24,40},{32,48},{40,56},{48,0},{56,8},{64,80... | collective-permute-start | bytes 1572872 | tf_op jit(solution)/shard_map/ppermute | solution.py:33
  82.6 16.2 %collective-permute-start.21 = (f32[4,128,256]{2,1,0:T(8,128)S(1)}, f32[4,128,256]{2,1,0:T(8,128)S(1)}, u32[]{:S(2)}, u32[]{:S(2)}) collective-permute-start(f32[4,128,256]{2,1,0:T(8,128)S(1)} %get-tuple-element.14), channel_id=1, source_target_pairs={{0,48},{8,56},{16,0},{24,8},{32,16},{40,24},{48,32},{56,40},{64,11... | collective-permute-start | bytes 1572872 | tf_op jit(solution)/shard_map/ppermute | solution.py:33
  83.0 26.8 %collective-permute-start.13 = (f32[128,256]{1,0:T(8,128)S(1)}, f32[128,256]{1,0:T(8,128)S(1)}, u32[]{:S(2)}, u32[]{:S(2)}) collective-permute-start(f32[128,256]{1,0:T(8,128)S(1)} %slice_bitcast_fusion.4), channel_id=1, source_target_pairs={{0,4},{1,5},{2,6},{3,7},{4,0},{5,1},{6,2},{7,3},{8,12},{9,13},{10,... | collective-permute-start | bytes 393224 | tf_op jit(solution)/shard_map/ppermute | solution.py:45
  99.0 13.1 %collective-permute-start.22 = (f32[128,256]{1,0:T(8,128)S(1)}, f32[128,256]{1,0:T(8,128)S(1)}, u32[]{:S(2)}, u32[]{:S(2)}) collective-permute-start(f32[128,256]{1,0:T(8,128)S(1)} %get-tuple-element.19), channel_id=1, source_target_pairs={{0,128},{8,136},{16,144},{24,152},{32,160},{40,168},{48,176},{56,1... | collective-permute-start | bytes 393224 | tf_op jit(solution)/shard_map/ppermute | solution.py:29
  105.7 10.8 %collective-permute-start.23 = (f32[128,256]{1,0:T(8,128)S(1)}, f32[128,256]{1,0:T(8,128)S(1)}, u32[]{:S(2)}, u32[]{:S(2)}) collective-permute-start(f32[128,256]{1,0:T(8,128)S(1)} %get-tuple-element.18), channel_id=1, source_target_pairs={{0,64},{8,72},{16,80},{24,88},{32,96},{40,104},{48,112},{56,120},{... | collective-permute-start | bytes 393224 | tf_op jit(solution)/shard_map/ppermute | solution.py:29
  107.5 12.3 %collective-permute-start.24 = (f32[128,256]{1,0:T(8,128)S(1)}, f32[128,256]{1,0:T(8,128)S(1)}, u32[]{:S(2)}, u32[]{:S(2)}) collective-permute-start(f32[128,256]{1,0:T(8,128)S(1)} %get-tuple-element.17), channel_id=1, source_target_pairs={{0,192},{8,200},{16,208},{24,216},{32,224},{40,232},{48,240},{56,2... | collective-permute-start | bytes 393224 | tf_op jit(solution)/shard_map/ppermute | solution.py:29
  119.9 42.8 %copy-start.1 = (f32[128,256]{1,0:T(8,128)}, f32[128,256]{1,0:T(8,128)S(1)}, u32[]{:S(2)}) copy-start(f32[128,256]{1,0:T(8,128)S(1)} %fusion.3.products) | copy-start | bytes 393220
  120.4 1.4 collective-permute-start.25
  121.8 5.2 %collective-permute-start.27 = (f32[32,256]{1,0:T(8,128)S(1)}, f32[32,256]{1,0:T(8,128)S(1)}, u32[]{:S(2)}, u32[]{:S(2)}) collective-permute-start(f32[32,256]{1,0:T(8,128)S(1)} %get-tuple-element.22), channel_id=1, source_target_pairs={{0,1},{1,2},{2,3},{3,0},{4,5},{5,6},{6,7},{7,4},{8,9},{9,10},{10,1... | collective-permute-start | bytes 98312 | tf_op jit(solution)/shard_map/ppermute | solution.py:41
  121.9 5.1 %collective-permute-start.28 = (f32[32,256]{1,0:T(8,128)S(1)}, f32[32,256]{1,0:T(8,128)S(1)}, u32[]{:S(2)}, u32[]{:S(2)}) collective-permute-start(f32[32,256]{1,0:T(8,128)S(1)} %get-tuple-element.21), channel_id=1, source_target_pairs={{0,3},{1,0},{2,1},{3,2},{4,7},{5,4},{6,5},{7,6},{8,11},{9,8},{10,9... | collective-permute-start | bytes 98312 | tf_op jit(solution)/shard_map/ppermute | solution.py:41
  125.2 5.4 %collective-permute-start.26 = (f32[32,256]{1,0:T(8,128)S(1)}, f32[32,256]{1,0:T(8,128)S(1)}, u32[]{:S(2)}, u32[]{:S(2)}) collective-permute-start(f32[32,256]{1,0:T(8,128)S(1)} %get-tuple-element.20), channel_id=1, source_target_pairs={{0,2},{1,3},{2,0},{3,1},{4,6},{5,7},{6,4},{7,5},{8,10},{9,11},{10,... | collective-permute-start | bytes 98312 | tf_op jit(solution)/shard_map/ppermute | solution.py:41
  130.6 4.0 %collective-permute-start.30 = (f32[32,256]{1,0:T(8,128)S(1)}, f32[32,256]{1,0:T(8,128)S(1)}, u32[]{:S(2)}, u32[]{:S(2)}) collective-permute-start(f32[32,256]{1,0:T(8,128)S(1)} %add_add_fusion.3), channel_id=1, source_target_pairs={{0,16},{8,24},{16,32},{24,40},{32,48},{40,56},{48,0},{56,8},{64,80... | collective-permute-start | bytes 98312 | tf_op jit(solution)/shard_map/ppermute | solution.py:33
  130.7 4.6 %collective-permute-start.31 = (f32[32,256]{1,0:T(8,128)S(1)}, f32[32,256]{1,0:T(8,128)S(1)}, u32[]{:S(2)}, u32[]{:S(2)}) collective-permute-start(f32[32,256]{1,0:T(8,128)S(1)} %add_add_fusion.3), channel_id=1, source_target_pairs={{0,48},{8,56},{16,0},{24,8},{32,16},{40,24},{48,32},{56,40},{64,11... | collective-permute-start | bytes 98312 | tf_op jit(solution)/shard_map/ppermute | solution.py:33
  132.7 5.4 %collective-permute-start.29 = (f32[32,256]{1,0:T(8,128)S(1)}, f32[32,256]{1,0:T(8,128)S(1)}, u32[]{:S(2)}, u32[]{:S(2)}) collective-permute-start(f32[32,256]{1,0:T(8,128)S(1)} %add_add_fusion.3), channel_id=1, source_target_pairs={{0,32},{8,40},{16,48},{24,56},{32,0},{40,8},{48,16},{56,24},{64,96... | collective-permute-start | bytes 98312 | tf_op jit(solution)/shard_map/ppermute | solution.py:33
  138.1 4.0 %collective-permute-start.32 = (f32[32,256]{1,0:T(8,128)S(1)}, f32[32,256]{1,0:T(8,128)S(1)}, u32[]{:S(2)}, u32[]{:S(2)}) collective-permute-start(f32[32,256]{1,0:T(8,128)S(1)} %add_add_fusion.2), channel_id=1, source_target_pairs={{0,4},{1,5},{2,6},{3,7},{4,0},{5,1},{6,2},{7,3},{8,12},{9,13},{10,... | collective-permute-start | bytes 98312 | tf_op jit(solution)/shard_map/ppermute | solution.py:45
  142.1 6.7 %collective-permute-start.34 = (f32[32,256]{1,0:T(8,128)S(1)}, f32[32,256]{1,0:T(8,128)S(1)}, u32[]{:S(2)}, u32[]{:S(2)}) collective-permute-start(f32[32,256]{1,0:T(8,128)S(1)} %add.124), channel_id=1, source_target_pairs={{0,64},{8,72},{16,80},{24,88},{32,96},{40,104},{48,112},{56,120},{... | collective-permute-start | bytes 98312 | tf_op jit(solution)/shard_map/ppermute | solution.py:29
  143.3 5.6 %collective-permute-start.35 = (f32[32,256]{1,0:T(8,128)S(1)}, f32[32,256]{1,0:T(8,128)S(1)}, u32[]{:S(2)}, u32[]{:S(2)}) collective-permute-start(f32[32,256]{1,0:T(8,128)S(1)} %add.124), channel_id=1, source_target_pairs={{0,192},{8,200},{16,208},{24,216},{32,224},{40,232},{48,240},{56,2... | collective-permute-start | bytes 98312 | tf_op jit(solution)/shard_map/ppermute | solution.py:29
  146.3 7.8 %collective-permute-start.33 = (f32[32,256]{1,0:T(8,128)S(1)}, f32[32,256]{1,0:T(8,128)S(1)}, u32[]{:S(2)}, u32[]{:S(2)}) collective-permute-start(f32[32,256]{1,0:T(8,128)S(1)} %add.124), channel_id=1, source_target_pairs={{0,128},{8,136},{16,144},{24,152},{32,160},{40,168},{48,176},{56,1... | collective-permute-start | bytes 98312 | tf_op jit(solution)/shard_map/ppermute | solution.py:29
  154.1 1.3 collective-permute-start.36
  155.4 7.3 %copy-start.5 = (f32[2,32,256]{2,1,0:T(8,128)}, f32[2,32,256]{2,1,0:T(8,128)S(1)}, u32[]{:S(2)}) copy-start(f32[2,32,256]{2,1,0:T(8,128)S(1)} %pad_maximum_fusion.2.piece0) | copy-start | bytes 196612
  155.4 4.9 %collective-permute-start.37 = (f32[2,32,256]{2,1,0:T(8,128)S(1)}, f32[2,32,256]{2,1,0:T(8,128)S(1)}, u32[]{:S(2)}, u32[]{:S(2)}) collective-permute-start(f32[2,32,256]{2,1,0:T(8,128)S(1)} %pad_maximum_fusion.2.piece0), channel_id=1, source_target_pairs={{0,3},{1,0},{2,1},{3,2},{4,7},{5,4},{6,5},{7,6},{8,11},{9,8},{10,9... | collective-permute-start | bytes 196616 | tf_op jit(solution)/shard_map/ppermute | solution.py:41
  155.5 5.9 %collective-permute-start.38 = (f32[2,32,256]{2,1,0:T(8,128)S(1)}, f32[2,32,256]{2,1,0:T(8,128)S(1)}, u32[]{:S(2)}, u32[]{:S(2)}) collective-permute-start(f32[2,32,256]{2,1,0:T(8,128)S(1)} %pad_maximum_fusion.2.piece0), channel_id=1, source_target_pairs={{0,2},{1,3},{2,0},{3,1},{4,6},{5,7},{6,4},{7,5},{8,10},{9,11},{10,... | collective-permute-start | bytes 196616 | tf_op jit(solution)/shard_map/ppermute | solution.py:41
  156.5 6.2 %collective-permute-start.39 = (f32[2,32,256]{2,1,0:T(8,128)S(1)}, f32[2,32,256]{2,1,0:T(8,128)S(1)}, u32[]{:S(2)}, u32[]{:S(2)}) collective-permute-start(f32[2,32,256]{2,1,0:T(8,128)S(1)} %pad_maximum_fusion.2.piece0), channel_id=1, source_target_pairs={{0,1},{1,2},{2,3},{3,0},{4,5},{5,6},{6,7},{7,4},{8,9},{9,10},{10,1... | collective-permute-start | bytes 196616 | tf_op jit(solution)/shard_map/ppermute | solution.py:41
  (11 other events, 18.5 us)
